TPU v7x, 32 devices: a whole 2x2x4 slice. The times are simulated.
32 devices in a mesh: dp: 4 (over y, x), ctx: 8 (over z, core).
Axes of the slice: x: 2, y: 2, z: 4, core: 2. Of those that a mesh axis runs over, the one named last changes fastest.
Arguments:
- tokens: bfloat16 [4, 1024, 2048], P('dp', 'ctx'), may hold values from -6 to 6
- positions: int32 [4, 1024], P('dp', 'ctx'), may hold values from 0 to 1023, as said below
- norm_gain: float32 [2048], replicated, may hold values from 0.5 to 1.5
- norm_bias: float32 [2048], replicated, may hold values from -1.8 to 1.8
- qkv_weight: bfloat16 [2048, 6144], P('ctx'), may hold values from -0.125 to 0.125
- qkv_bias: float32 [6144], replicated, may hold values from -1.8 to 1.8
- dense_weight: bfloat16 [2048, 2048], P('ctx'), may hold values from -2 to 2
- dense_bias: float32 [2048], replicated, may hold values from -1.8 to 1.8
- up_weight: bfloat16 [2048, 8192], P('ctx'), may hold values from -0.125 to 0.125
- up_bias: float32 [8192], replicated, may hold values from -1.8 to 1.8
- down_weight: bfloat16 [8192, 2048], P('ctx'), may hold values from -0.0625 to 0.0625
- down_bias: float32 [2048], replicated, may hold values from -1.8 to 1.8
- clip_limit: int32 [32], replicated, may hold values from 3 to 11
- cotangent: bfloat16 [4, 1024, 2048], P('dp', 'ctx'), may hold values from -6 to 6
Outputs:
- layer_out: bfloat16 [4, 1024, 2048], P('dp', 'ctx')
- tokens_grad: float32 [4, 1024, 2048], P('dp', 'ctx')
- norm_gain_grad: float32 [2048], replicated
- norm_bias_grad: float32 [2048], replicated
- qkv_weight_grad: float32 [2048, 6144], P('ctx')
- qkv_bias_grad: float32 [6144], replicated
- dense_weight_grad: float32 [2048, 2048], P('ctx')
- dense_bias_grad: float32 [2048], replicated
- up_weight_grad: float32 [2048, 8192], P('ctx')
- up_bias_grad: float32 [8192], replicated
- down_weight_grad: float32 [8192, 2048], P('ctx')
- down_bias_grad: float32 [2048], replicated
- head_maxima: float32 [32], replicated
- clipped_weight: float32 [2048, 4096], P('ctx')
- clipped_bias: float32 [4096], replicated
Inputs may be any that keep to these rules, and one draw needn't show every extreme that they name: `positions`: within each sequence the ids rise by one from 0 at its first token and return to 0 at the first token of each packed document; the first sequence holds a single document.
All inputs are finite; a program needn't handle non-finite values.
Results may differ from a plain program's by a relative error of at most 0.017.
Values may be sent and summed in bfloat16 or wider, within the bound.
No kernel may reach another device: no remote copies, remote signals or barrier semaphores. Data moves between devices by JAX's collectives and lax.ppermute only.
A program may use at most 512 MiB of HBM per device.

v0:
```python
from functools import partial

import jax
import jax.numpy as jnp
from jax import lax
from jax.sharding import PartitionSpec as P

ROT = 32


epsilon = 1e-05
masked_score = -1e30
rope_base = 10000.0
no_batch = ((), ())


def from_behind(value, axis, steps):
    count = lax.axis_size(axis)
    leading, last = (max(0, -steps), min(count, count - steps))
    return lax.ppermute(value, axis, [(source, source + steps) for source in range(leading, last)])


def from_behind_2(value, axis, steps):
    count = lax.axis_size(axis)
    pairs = [(source, (source + steps) % count) for source in range(count)]
    return lax.ppermute(value, axis, pairs)


def rotary_tables(positions):
    half_rot = ROT // 2
    frequency = rope_base ** (-(jnp.arange(half_rot, dtype=jnp.float32) * 2.0 / ROT))
    angles = positions.astype(jnp.float32)[..., None] * frequency
    cosine = jnp.cos(angles)
    sine_part = jnp.sin(angles)
    return (
        jnp.concatenate([cosine, cosine], -1)[..., None, :],
        jnp.concatenate([sine_part, sine_part], -1)[..., None, :],
    )


def rotate(values, cosine, sine_part):
    half_rot = ROT // 2
    turned = values[..., :ROT]
    swapped = jnp.concatenate([-turned[..., half_rot:], turned[..., :half_rot]], -1)
    return jnp.concatenate([turned * cosine + swapped * sine_part, values[..., ROT:]], -1)


def rotate_back(gradient, cosine, sine_part):
    half_rot = ROT // 2
    turned = gradient[..., :ROT]
    scaled = turned * sine_part
    swapped = jnp.concatenate([scaled[..., half_rot:], -scaled[..., :half_rot]], -1)
    return jnp.concatenate([turned * cosine + swapped, gradient[..., ROT:]], -1)


def contract_last(left, right):
    return lax.dot_general(
        left, right, (((1,), (1,)), no_batch), preferred_element_type=jnp.float32
    )


def contract_first(left, right):
    return lax.dot_general(
        left, right, (((0,), (0,)), no_batch), preferred_element_type=jnp.float32
    )


def attend_block(cycle_state, queries, piece_keys, piece_values, allowed, score_scale):
    accumulated, run_max, run_sum = cycle_state
    scores = (
        jnp.einsum("sqhd,skhd->shqk", queries, piece_keys, preferred_element_type=jnp.float32)
        * score_scale
    )
    scores = jnp.where(allowed, scores, masked_score)
    new_max = jnp.maximum(run_max, jnp.max(scores, axis=-1))
    prob_block = jnp.where(allowed, jnp.exp(scores - new_max[..., None]), 0.0)
    shrink = jnp.exp(run_max - new_max)
    run_sum = run_sum * shrink + jnp.sum(prob_block, axis=-1)
    accumulated = accumulated * shrink[..., None] + jnp.einsum(
        "shqk,skhd->shqd",
        prob_block.astype(jnp.bfloat16),
        piece_values,
        preferred_element_type=jnp.float32,
    )
    return (accumulated, new_max, run_sum)


def per_device(
    tokens,
    positions,
    norm_gain,
    norm_bias,
    qkv_weight,
    qkv_bias,
    dense_weight,
    dense_bias,
    up_weight,
    up_bias,
    down_weight,
    down_bias,
    clip_limit,
    cotangent,
):
    seq_count, stretch_len, model_width = tokens.shape
    head_count = clip_limit.shape[0]
    head_dim = model_width // head_count
    row_count = seq_count * stretch_len
    ctx_size = lax.axis_size("ctx")
    ctx_index = lax.axis_index("ctx")
    score_scale = head_dim ** (-0.5)
    own_rows = qkv_weight.shape[0]
    ff_rows = down_weight.shape[0]
    ff_width = up_weight.shape[1]
    qkv_width = 3 * model_width
    inputs = tokens.reshape(row_count, model_width).astype(jnp.float32)
    centre = inputs - jnp.mean(inputs, axis=-1, keepdims=True)
    inv_std = lax.rsqrt(jnp.mean(centre * centre, axis=-1, keepdims=True) + epsilon)
    normed = centre * inv_std
    hidden = (normed * norm_gain + norm_bias).astype(jnp.bfloat16)
    in_local = jnp.concatenate([qkv_weight, up_weight], axis=1)
    out_local = jnp.concatenate([dense_weight, down_weight], axis=0)
    columns = hidden
    projected = jnp.dot(
        columns,
        lax.all_gather(in_local, "ctx", axis=0, tiled=True),
        preferred_element_type=jnp.float32,
    )
    joined = projected[:, :qkv_width] + qkv_bias
    upward = projected[:, qkv_width:] + up_bias
    cosine, sine_part = rotary_tables(positions)
    shaped = joined.reshape(seq_count, stretch_len, 3, head_count, head_dim)
    queries = rotate(shaped[:, :, 0], cosine, sine_part).astype(jnp.bfloat16)
    keys = rotate(shaped[:, :, 1], cosine, sine_part).astype(jnp.bfloat16)
    values = shaped[:, :, 2].astype(jnp.bfloat16)
    key_pack = keys.reshape(seq_count, stretch_len, model_width)
    value_pack = values.reshape(seq_count, stretch_len, model_width)
    query_time = ctx_index * stretch_len + jnp.arange(stretch_len, dtype=jnp.int32)
    start_state = (
        jnp.zeros((seq_count, head_count, stretch_len, head_dim), jnp.float32),
        jnp.full((seq_count, head_count, stretch_len), masked_score, jnp.float32),
        jnp.zeros((seq_count, head_count, stretch_len), jnp.float32),
    )
    cycle_state = start_state
    pieces = (
        lax.all_gather(key_pack, "ctx", axis=1, tiled=True),
        lax.all_gather(value_pack, "ctx", axis=1, tiled=True),
    )
    block_count = pieces[0].shape[1] // stretch_len
    key_blocks = pieces[0].reshape(seq_count, block_count, stretch_len, head_count, head_dim)
    value_blocks = pieces[1].reshape(seq_count, block_count, stretch_len, head_count, head_dim)

    def inner_step(carried, block_index):
        piece_keys = lax.dynamic_index_in_dim(key_blocks, block_index, 1, keepdims=False)
        piece_values = lax.dynamic_index_in_dim(value_blocks, block_index, 1, keepdims=False)
        key_time = block_index * stretch_len + jnp.arange(stretch_len, dtype=jnp.int32)
        allowed = query_time[:, None] >= key_time[None, :]
        return (
            attend_block(carried, queries, piece_keys, piece_values, allowed, score_scale),
            None,
        )

    cycle_state, unused_out = lax.scan(
        inner_step, cycle_state, jnp.arange(block_count, dtype=jnp.int32)
    )
    accumulated, row_max, row_sum = cycle_state
    head_maxima = lax.pmax(jnp.max(row_max, axis=(0, 2)), ("dp", "ctx"))
    mixed_rows = jnp.transpose(accumulated / row_sum[..., None], (0, 2, 1, 3))
    log_sum = row_max + jnp.log(row_sum)
    attended = mixed_rows.reshape(row_count, model_width).astype(jnp.bfloat16)
    activated = jax.nn.gelu(upward, approximate=True).astype(jnp.bfloat16)
    left_stack = jnp.concatenate(
        [
            attended.reshape(row_count, ctx_size, own_rows),
            activated.reshape(row_count, ctx_size, ff_rows),
        ],
        axis=2,
    ).reshape(row_count, -1)
    columns = left_stack
    branch_sum = jnp.dot(
        columns,
        lax.all_gather(out_local, "ctx", axis=0, tiled=True),
        preferred_element_type=jnp.float32,
    )
    layer_out = (inputs + branch_sum + dense_bias + down_bias).astype(jnp.bfloat16)
    grad_out = cotangent.reshape(row_count, model_width)
    left_grad = contract_last(grad_out, lax.all_gather(out_local, "ctx", axis=0, tiled=True))
    split_grad = left_grad.reshape(row_count, ctx_size, own_rows + ff_rows)
    mixed_grad = split_grad[:, :, :own_rows].reshape(row_count, model_width)
    act_grad = split_grad[:, :, own_rows:].reshape(row_count, ff_width)
    stack_owned, hidden_owned = (
        lax.all_to_all(left_stack, "ctx", split_axis=1, concat_axis=0, tiled=True),
        lax.all_to_all(hidden, "ctx", split_axis=1, concat_axis=0, tiled=True),
    )
    columns = stack_owned
    out_grad_local = contract_first(columns, lax.all_gather(grad_out, "ctx", axis=0, tiled=True))
    out_bias_grad = jnp.sum(grad_out.astype(jnp.float32), axis=0)
    unused_value, gelu_back = jax.vjp(partial(jax.nn.gelu, approximate=True), upward)
    up_grad_rows = gelu_back(act_grad)[0].astype(jnp.bfloat16)
    mixed_grad_low = mixed_grad.astype(jnp.bfloat16).reshape(
        seq_count, stretch_len, head_count, head_dim
    )
    row_delta = jnp.transpose(
        jnp.sum(mixed_grad_low.astype(jnp.float32) * mixed_rows, axis=-1), (0, 2, 1)
    )

    def back_block(cycle_state, offset):
        kv_stack, kv_grad, query_grad = cycle_state
        source = (ctx_index - offset) % ctx_size
        key_time = source * stretch_len + jnp.arange(stretch_len, dtype=jnp.int32)
        allowed = query_time[:, None] >= key_time[None, :]
        piece_keys = kv_stack[0].reshape(seq_count, stretch_len, head_count, head_dim)
        piece_values = kv_stack[1].reshape(seq_count, stretch_len, head_count, head_dim)
        scores = (
            jnp.einsum("sqhd,skhd->shqk", queries, piece_keys, preferred_element_type=jnp.float32)
            * score_scale
        )
        scores = jnp.where(allowed, scores, masked_score)
        prob_block = jnp.where(allowed, jnp.exp(scores - log_sum[..., None]), 0.0)
        value_step = jnp.einsum(
            "shqk,sqhd->skhd",
            prob_block.astype(jnp.bfloat16),
            mixed_grad_low,
            preferred_element_type=jnp.float32,
        )
        prob_grad = jnp.einsum(
            "sqhd,skhd->shqk", mixed_grad_low, piece_values, preferred_element_type=jnp.float32
        )
        score_grad = (prob_block * (prob_grad - row_delta[..., None])).astype(jnp.bfloat16)
        query_grad = (
            query_grad
            + jnp.einsum(
                "shqk,skhd->sqhd", score_grad, piece_keys, preferred_element_type=jnp.float32
            )
            * score_scale
        )
        key_step = (
            jnp.einsum("shqk,sqhd->skhd", score_grad, queries, preferred_element_type=jnp.float32)
            * score_scale
        )
        kv_grad = kv_grad + jnp.stack(
            [
                key_step.reshape(seq_count, stretch_len, model_width),
                value_step.reshape(seq_count, stretch_len, model_width),
            ]
        )
        return (kv_stack, kv_grad, query_grad)

    def move_keys(cycle_state):
        shifted = from_behind(cycle_state[0], "ctx", 1)
        return (shifted, cycle_state[1], cycle_state[2])

    def move_grads(cycle_state):
        shifted = from_behind_2(cycle_state[1].astype(jnp.bfloat16), "ctx", 1).astype(jnp.float32)
        return (cycle_state[0], shifted, cycle_state[2])

    def cycle_turn(offset, cycle_state):
        return move_grads(move_keys(back_block(cycle_state, offset)))

    cycle_state = (
        jnp.stack([key_pack, value_pack]),
        jnp.zeros((2, seq_count, stretch_len, model_width), jnp.float32),
        jnp.zeros((seq_count, stretch_len, head_count, head_dim), jnp.float32),
    )
    cycle_state = lax.fori_loop(0, ctx_size - 1, cycle_turn, cycle_state)
    cycle_state = move_grads(back_block(cycle_state, ctx_size - 1))
    kv_grad = cycle_state[1]
    query_pre = rotate_back(cycle_state[2], cosine, sine_part)
    key_pre = rotate_back(
        kv_grad[0].reshape(seq_count, stretch_len, head_count, head_dim), cosine, sine_part
    )
    value_pre = kv_grad[1].reshape(seq_count, stretch_len, head_count, head_dim)
    joined_low = (
        jnp.stack([query_pre, key_pre, value_pre], axis=2)
        .reshape(row_count, qkv_width)
        .astype(jnp.bfloat16)
    )
    qkv_bias_local = jnp.sum(joined_low.astype(jnp.float32), axis=0)
    up_bias_local = jnp.sum(up_grad_rows.astype(jnp.float32), axis=0)
    both_grads = jnp.concatenate([joined_low, up_grad_rows], axis=1)
    hidden_grad = contract_last(both_grads, lax.all_gather(in_local, "ctx", axis=0, tiled=True))
    columns = hidden_owned
    in_grad_local = contract_first(columns, lax.all_gather(both_grads, "ctx", axis=0, tiled=True))
    gain_local = jnp.sum(hidden_grad * normed, axis=0)
    normbias_local = jnp.sum(hidden_grad, axis=0)
    scaled_grad = hidden_grad * norm_gain
    tokens_grad = grad_out.astype(jnp.float32) + inv_std * (
        scaled_grad
        - jnp.mean(scaled_grad, axis=-1, keepdims=True)
        - normed * jnp.mean(scaled_grad * normed, axis=-1, keepdims=True)
    )
    out_grad_sum, in_grad_sum = (
        lax.psum(out_grad_local.astype(jnp.bfloat16), "dp").astype(jnp.float32),
        lax.psum(in_grad_local.astype(jnp.bfloat16), "dp").astype(jnp.float32),
    )
    small_sums = lax.psum(
        (gain_local, normbias_local, qkv_bias_local, out_bias_grad, up_bias_local), ("dp", "ctx")
    )
    limits = clip_limit.astype(jnp.float32)
    factor = limits / jnp.maximum(head_maxima, limits)
    column_scale = jnp.tile(jnp.repeat(jnp.sqrt(factor), head_dim), 2)
    clipped_weight = qkv_weight[:, : 2 * model_width].astype(jnp.float32) * column_scale
    clipped_bias = qkv_bias[: 2 * model_width] * column_scale
    return (
        layer_out.reshape(seq_count, stretch_len, model_width),
        tokens_grad.reshape(seq_count, stretch_len, model_width),
        small_sums[0],
        small_sums[1],
        in_grad_sum[:, :qkv_width],
        small_sums[2],
        out_grad_sum[:own_rows],
        small_sums[3],
        in_grad_sum[:, qkv_width:],
        small_sums[4],
        out_grad_sum[own_rows:],
        small_sums[3],
        head_maxima,
        clipped_weight,
        clipped_bias,
    )


def solution(mesh):
    in_specs = (
        P("dp", "ctx", None),
        P("dp", "ctx"),
        P(),
        P(),
        P("ctx", None),
        P(),
        P("ctx", None),
        P(),
        P("ctx", None),
        P(),
        P("ctx", None),
        P(),
        P(),
        P("dp", "ctx", None),
    )
    out_specs = (
        P("dp", "ctx", None),
        P("dp", "ctx", None),
        P(),
        P(),
        P("ctx", None),
        P(),
        P("ctx", None),
        P(),
        P("ctx", None),
        P(),
        P("ctx", None),
        P(),
        P(),
        P("ctx", None),
        P(),
    )
    return jax.shard_map(
        per_device, mesh=mesh, in_specs=in_specs, out_specs=out_specs, check_vma=False
    )
```

profile of v0, /device:TPU:0, one launch (start us, length us, event | category | flops | bytes accessed | tf_op | source)
XLA Modules:
  0.0 2021.1 jit_solution(2774940545295063979)
XLA Ops:
  7.2 7.0 pad_maximum_fusion
  15.4 5.4 pad_maximum_fusion.1
  22.4 490.3 %all-gather.8.cloned.1.call-done = bf16[2048,14336]{1,0:T(8,128)(2,1)} async-done(((bf16[256,14336]{1,0:T(8,128)(2,1)}), bf16[2048,14336]{1,0:T(8,128)(2,1)}) %all-gather.8.cloned.1.call-update) | async-done | bytes 58720272 | tf_op jit(solution)/shard_map/all_gather | solution.py:125
  512.6 30.2 %fusion.59 = f32[128,14336]{1,0:T(8,128)} fusion(bf16[2048,14336]{1,0:T(8,128)(2,1)} %all-gather.8.cloned.1.call-done, bf16[1,128,2048]{2,1,0:T(8,128)(2,1)S(1)} %copy-done.6, f32[2048]{0:T(1024)S(1)} %copy-done.18, f32[2048]{0:T(1024)S(1)} %copy-done.17, f32[128]{0:T(128)S(1)} %add_rsqrt_fusion, f32[128]{0:T(128)S(1)} %broadcast_multiply_fusion.2), kind=kOutput, calls=%fused_computation.116 | convolution fusion | flops 7517765632 | bytes 66601984 | tf_op jit(solution)/shard_map/dot_general | solution.py:123
  554.1 317.8 %all-gather.14.cloned.1.call-done = bf16[10240,2048]{1,0:T(8,128)(2,1)} async-done(((bf16[1280,2048]{1,0:T(8,128)(2,1)}), bf16[10240,2048]{1,0:T(8,128)(2,1)}) %all-gather.14.cloned.1.call-update) | async-done | bytes 41943056 | tf_op jit(solution)/shard_map/all_gather | solution.py:181
  872.0 19.9 fusion.63
  891.9 4.5 slice.182
  897.8 5.6 copy.56
  906.4 14.1 all-gather.10.cloned.1.call-done
  920.5 3.3 copy.57
  927.0 41.7 %all-gather.12.cloned.1.call-done = bf16[1,1024,2048]{1,2,0:T(8,128)(2,1)} async-done(((bf16[1,128,2048]{1,2,0:T(8,128)(2,1)}), bf16[1,1024,2048]{1,2,0:T(8,128)(2,1)}) %all-gather.12.cloned.1.call-update) | async-done | bytes 4194320 | tf_op jit(solution)/shard_map/all_gather | solution.py:146
  968.6 3.3 copy.58
  975.0 68.7 %while.35 = (s32[]{:T(128)}, f32[1,32,128,64]{2,3,1,0:T(8,128)}, f32[1,32,128]{2,1,0:T(8,128)S(1)}, f32[1,32,128]{2,1,0:T(8,128)S(1)}, s32[8]{0:T(128)S(1)}, /*i...) while((s32[]{:T(128)}, f32[1,32,128,64]{2,3,1,0:T(8,128)}, ...), condition=%wide.region_5.6_spmd.clone, body=%wide.region_2.5_spmd.clone.sunk | while | flops 141861120 | bytes 10291419 | solution.py:162
  1045.3 208.7 %while.36 = (s32[]{:T(128)}, bf16[2,1,128,2048]{2,3,1,0:T(8,128)(2,1)}, f32[2,1,128,2048]{2,3,1,0:T(8,128)}, f32[1,128,32,64]{1,3,2,0:T(8,128)}, s32[]{:T(128)},...) while((s32[]{:T(128)}, ...), condition=%wide.region_8.9_spmd.clone, body=%wide.region_7.8_spmd.clone.sunk | while | flops 343425280 | bytes 50923972 | solution.py:264
  1058.1 10.2 collective-permute-done.1
  1077.3 4.6 collective-permute-start.1
  1081.9 5.5 collective-permute-start
  1102.7 11.4 collective-permute-start.1
  1114.0 5.5 collective-permute-start
  1131.8 14.4 collective-permute-start.1
  1146.2 5.5 collective-permute-start
  1163.9 14.4 collective-permute-start.1
  1178.3 5.5 collective-permute-start
  1196.1 14.4 collective-permute-start.1
  1210.5 5.5 collective-permute-start
  1228.2 14.4 collective-permute-start.1
  1242.6 5.5 collective-permute-start
  1260.6 14.5 collective-permute-start.2
  1275.1 5.0 convert_reduce_fusion
  1287.5 3.5 pad_maximum_fusion.2
  1291.1 3.3 copy.54
  1296.2 12.7 all-to-all-start.1
  1311.0 30.7 %multiply_reduce_fusion = (f32[2048]{0:T(1024)}, f32[128]{0:T(128)S(1)}, f32[128]{0:T(128)S(1)}, f32[2048]{0:T(1024)}, f32[128,2048]{1,0:T(8,128)}) fusion(bf16[1,128,2048]{2,1,0:T(8,128)(2,1)S(1)} %copy-done.7, f32[128]{0:T(128)S(1)} %add_rsqrt_fusion, f32[128]{0:T(128)S(1)} %broadcast_multiply_fusion.2, f32[2048]{0:T(1024)S(1)} %copy-done.17, ...), kind=kOutput, calls=%fused_computation.107 | convolution fusion | flops 7526150144 | bytes 63989760 | tf_op jit(solution)/shard_map/dot_general | solution.py:57
  1341.7 3.5 convert_reduce_fusion.2
  1345.3 99.6 %all-to-all-done.1 = bf16[128,8,1280]{0,2,1:T(8,128)(2,1)S(1)} async-done(((bf16[128,8,1280]{0,2,1:T(8,128)(2,1)}), bf16[128,8,1280]{0,2,1:T(8,128)(2,1)S(1)}, u32[]{:S(2)}, u32[]{:S(2)}) %all-to-all-start.1) | async-done | bytes 2621472 | tf_op jit(solution)/shard_map/all_to_all | solution.py:191
  1444.9 4.1 all-to-all-start
  1451.7 10.0 convolution_convert_fusion.1
  1461.7 18.6 all-to-all-done
  1480.3 138.4 %all-gather.16.cloned.1.call-done = bf16[1024,14336]{1,0:T(8,128)(2,1)} async-done(((bf16[128,14336]{1,0:T(8,128)(2,1)}), bf16[1024,14336]{1,0:T(8,128)(2,1)}) %all-gather.16.cloned.1.call-update) | async-done | bytes 29360144 | tf_op jit(solution)/shard_map/all_gather | solution.py:282
  1618.7 15.4 convolution_convert_fusion
  1634.1 38.1 %pmax.7 = f32[32]{0:T(128)S(1)} all-reduce(f32[32]{0:T(128)S(1)} %get-tuple-element.484), channel_id=1, replica_groups=mesh['dp'=4,'ctx'=8] {'dp','ctx'}, use_global_device_ids=true, to_apply=%region_24.25 | all-reduce | flops 32 | bytes 256 | tf_op jit(solution)/shard_map/pmax | solution.py:166
  1673.0 4.1 convert_multiply_fusion
  1677.1 17.5 fusion.46
  1694.6 52.9 %all-reduce.5.cloned.1.call-done = (f32[2048]{0:T(1024)}, f32[2048]{0:T(1024)}, f32[6144]{0:T(1024)}, f32[2048]{0:T(1024)}, f32[8192]{0:T(1024)}) async-done(((f32[2048]{0:T(1024)}, f32[2048]{0:T(1024)}, f32[6144]{0:T(1024)}, f32[2048]{0:T(1024)}, f32[8192]{0:T(1024)}), (f32[2048]{0:T(1024)}, f32[2048]{0:T(1024)}, f32[6144]{0:T(1024)}, f32[2048]{0:T(1024)}, f32[8192]{0:T(1024)})) %all-reduce.5.cloned.1.call-update) | async-done | bytes 81936 | tf_op jit(solution)/shard_map/psum | solution.py:295
  1747.5 246.5 %all-reduce.7.cloned.1.call-done = (bf16[256,14336]{1,0:T(8,128)(2,1)}, bf16[1280,2048]{1,0:T(8,128)(2,1)}) async-done(((bf16[256,14336]{1,0:T(8,128)(2,1)}, bf16[1280,2048]{1,0:T(8,128)(2,1)}), (bf16[256,14336]{1,0:T(8,128)(2,1)}, bf16[1280,2048]{1,0:T(8,128)(2,1)})) %all-reduce.7.cloned.1.call-update) | async-done | bytes 12582928 | tf_op jit(solution)/shard_map/psum | solution.py:293
  1994.0 6.0 slice.183
  2000.0 4.4 slice.185
  2005.9 4.4 slice.186
  (373 shorter events, 191.4 us)
Async XLA Ops:
  7.2 505.4 %all-gather.8.cloned.1.call-start = ((), (), s32[]{:S(2)}) async-start(), calls=%async_computation.2 | async-start | bytes 66060288 | tf_op jit(solution)/shard_map/all_gather | solution.py:125
  14.2 857.7 %all-gather.14.cloned.1.call-start = ((), (), s32[]{:S(2)}) async-start(), calls=%async_computation.5 | async-start | bytes 47185920 | tf_op jit(solution)/shard_map/all_gather | solution.py:181
  20.8 491.8 %copy-start.17 = (f32[2048]{0:T(1024)S(1)}, f32[2048]{0:T(1024)}, u32[]{:S(2)}) copy-start(f32[2048]{0:T(1024)} %param.20) | copy-start | bytes 24580
  20.8 491.8 %copy-start.18 = (f32[2048]{0:T(1024)S(1)}, f32[2048]{0:T(1024)}, u32[]{:S(2)}) copy-start(f32[2048]{0:T(1024)} %param.21) | copy-start | bytes 24580
  20.9 899.7 %all-gather.10.cloned.1.call-start = ((), (), s32[]{:S(2)}) async-start(), calls=%async_computation.3 | async-start | bytes 4718592 | tf_op jit(solution)/shard_map/all_gather | solution.py:145
  22.3 520.5 %copy-start.19 = (f32[6144]{0:T(1024)S(1)}, f32[6144]{0:T(1024)}, u32[]{:S(2)}) copy-start(f32[6144]{0:T(1024)} %param.23) | copy-start | bytes 73732
  549.9 322.1 %copy-start.14 = (bf16[1,128,2048]{2,1,0:T(8,128)(2,1)S(1)}, bf16[1,128,2048]{2,1,0:T(8,128)(2,1)}, u32[]{:S(2)}) copy-start(bf16[1,128,2048]{2,1,0:T(8,128)(2,1)} %param.31) | copy-start | bytes 1572868
  550.9 417.7 %all-gather.12.cloned.1.call-start = ((), (), s32[]{:S(2)}) async-start(), calls=%async_computation.4 | async-start | bytes 4718592 | tf_op jit(solution)/shard_map/all_gather | solution.py:146
  553.1 898.6 %all-gather.18.cloned.1.call-start = ((), (), s32[]{:S(2)}) async-start(), calls=%async_computation.7 | async-start | bytes 4718592 | tf_op jit(solution)/shard_map/all_gather | solution.py:195
  553.7 1065.0 %all-gather.16.cloned.1.call-start = ((), (), s32[]{:S(2)}) async-start(), calls=%async_computation.6 | async-start | bytes 33030144 | tf_op jit(solution)/shard_map/all_gather | solution.py:282
  1051.9 16.3 collective-permute-start.1
  1052.2 18.7 collective-permute-start
  1077.3 16.3 collective-permute-start.1
  1081.9 14.4 collective-permute-start
  1102.7 20.0 collective-permute-start.1
  1114.0 11.4 collective-permute-start
  1131.8 23.1 %collective-permute-start.1 = (bf16[2,1,128,2048]{2,3,1,0:T(8,128)(2,1)}, bf16[2,1,128,2048]{2,3,1,0:T(8,128)(2,1)}, u32[]{:S(2)}, u32[]{:S(2)}) collective-permute-start(bf16[2,1,128,2048]{2,3,1,0:T(8,128)(2,1)} %fusion.137), channel_id=1, source_target_pairs={{0,1},{1,2},{2,3},{3,4},{4,5},{5,6},{6,7},{7,0},{8,9},{9,10},{10,1... | collective-permute-start | bytes 3145736 | tf_op jit(solution)/shard_map/while/body/eval_jaxpr/ppermute | solution.py:26
  1146.2 11.4 collective-permute-start
  1163.9 23.1 %collective-permute-start.1 = (bf16[2,1,128,2048]{2,3,1,0:T(8,128)(2,1)}, bf16[2,1,128,2048]{2,3,1,0:T(8,128)(2,1)}, u32[]{:S(2)}, u32[]{:S(2)}) collective-permute-start(bf16[2,1,128,2048]{2,3,1,0:T(8,128)(2,1)} %fusion.137), channel_id=1, source_target_pairs={{0,1},{1,2},{2,3},{3,4},{4,5},{5,6},{6,7},{7,0},{8,9},{9,10},{10,1... | collective-permute-start | bytes 3145736 | tf_op jit(solution)/shard_map/while/body/eval_jaxpr/ppermute | solution.py:26
  1178.3 11.4 collective-permute-start
  1196.1 23.1 %collective-permute-start.1 = (bf16[2,1,128,2048]{2,3,1,0:T(8,128)(2,1)}, bf16[2,1,128,2048]{2,3,1,0:T(8,128)(2,1)}, u32[]{:S(2)}, u32[]{:S(2)}) collective-permute-start(bf16[2,1,128,2048]{2,3,1,0:T(8,128)(2,1)} %fusion.137), channel_id=1, source_target_pairs={{0,1},{1,2},{2,3},{3,4},{4,5},{5,6},{6,7},{7,0},{8,9},{9,10},{10,1... | collective-permute-start | bytes 3145736 | tf_op jit(solution)/shard_map/while/body/eval_jaxpr/ppermute | solution.py:26
  1210.5 11.4 collective-permute-start
  1228.2 23.1 %collective-permute-start.1 = (bf16[2,1,128,2048]{2,3,1,0:T(8,128)(2,1)}, bf16[2,1,128,2048]{2,3,1,0:T(8,128)(2,1)}, u32[]{:S(2)}, u32[]{:S(2)}) collective-permute-start(bf16[2,1,128,2048]{2,3,1,0:T(8,128)(2,1)} %fusion.137), channel_id=1, source_target_pairs={{0,1},{1,2},{2,3},{3,4},{4,5},{5,6},{6,7},{7,0},{8,9},{9,10},{10,1... | collective-permute-start | bytes 3145736 | tf_op jit(solution)/shard_map/while/body/eval_jaxpr/ppermute | solution.py:26
  1242.6 11.4 collective-permute-start
  1257.3 17.8 slice-start
  1258.8 16.2 slice-start.1
  1259.3 15.8 copy-start.8
  1259.3 15.8 copy-start.21
  1260.6 19.5 copy-start.4
  1260.6 20.4 %collective-permute-start.2 = (bf16[2,1,128,2048]{2,3,1,0:T(8,128)(2,1)S(1)}, bf16[2,1,128,2048]{2,3,1,0:T(8,128)(2,1)S(1)}, u32[]{:S(2)}, u32[]{:S(2)}) collective-permute-start(bf16[2,1,128,2048]{2,3,1,0:T(8,128)(2,1)S(1)} %fusion.47), channel_id=1, source_target_pairs={{0,1},{1,2},{2,3},{3,4},{4,5},{5,6},{6,7},{7,0},{8,9},{9,10},{10,1... | collective-permute-start | bytes 3145736 | tf_op jit(solution)/shard_map/ppermute | solution.py:26
  1280.1 7.4 copy-start.9
  1296.2 12.7 copy-start.7
  1296.2 148.7 %all-to-all-start.1 = ((bf16[128,8,1280]{0,2,1:T(8,128)(2,1)}), bf16[128,8,1280]{0,2,1:T(8,128)(2,1)S(1)}, u32[]{:S(2)}, u32[]{:S(2)}) async-start(bf16[128,8,1280]{0,2,1:T(8,128)(2,1)} %pad_maximum_fusion.3), calls=%async_computation.1 | async-start | bytes 5242880 | tf_op jit(solution)/shard_map/all_to_all | solution.py:191
  1308.9 438.6 %all-reduce.5.cloned.1.call-start = ((), (), s32[]{:S(2)}) async-start(), calls=%async_computation.8 | async-start | bytes 163840 | tf_op jit(solution)/shard_map/psum | solution.py:295
  1444.9 35.4 %all-to-all-start = ((bf16[128,8,256]{2,0,1:T(8,128)(2,1)}), bf16[128,8,256]{2,0,1:T(8,128)(2,1)}, u32[]{:S(2)}, u32[]{:S(2)}) async-start(bf16[128,8,256]{2,0,1:T(8,128)(2,1)} %fusion.55), calls=%async_computation | async-start | bytes 1048576 | tf_op jit(solution)/shard_map/all_to_all | solution.py:192
  1449.1 544.9 %all-reduce.7.cloned.1.call-start = ((), (), s32[]{:S(2)}) async-start(), calls=%async_computation.9 | async-start | bytes 25165824 | tf_op jit(solution)/shard_map/psum | solution.py:293
  1634.1 38.1 %copy-start.30 = (s32[32]{0:T(128)S(1)}, s32[32]{0:T(128)}, u32[]{:S(2)}) copy-start(s32[32]{0:T(128)} %param.30) | copy-start | bytes 388
  1634.1 38.3 %copy-start.20 = (f32[6144]{0:T(1024)S(1)}, f32[6144]{0:T(1024)}, u32[]{:S(2)}) copy-start(f32[6144]{0:T(1024)} %param.23) | copy-start | bytes 73732
  1672.1 5.0 copy-start.31
  1673.0 4.2 copy-start.28
  1994.0 6.0 copy-start.5
  1994.0 10.4 slice-start.2
  2000.0 4.4 slice-start.3
  2005.9 4.5 copy-start.23
  2005.9 5.1 copy-start.26
  2005.9 5.7 copy-start.25
  2005.9 6.3 copy-start.24
  2005.9 7.5 copy-start.22
  (32 other events, 50.3 us)
Sparse Core Ops, SparseCore 0:
  14.4 498.2 all-gather.7
  514.8 357.0 all-gather.13
  874.1 46.3 all-gather.9
  922.5 46.0 all-gather.11
  970.1 45.3 all-gather.17
  1291.2 327.4 all-gather.15
  1626.3 121.1 all-reduce.4
  1752.4 241.5 all-reduce.6
where the time goes:
time: 2030 us; the launch traced here: 2020 us
  waiting for transfers between devices  1430 us (70%)
  matrix products  208 us (10%)
  starting transfers between devices  141 us (7%)
  local copies, waits for them, and re-layouts  86.2 us (4%)
  other arithmetic  76.7 us (4%)
  blocking collectives  38.1 us (2%)
  loops' own time  22 us (1%)
    all_gather x1, waiting for transfers between devices, per_device(): lax.all_gather(in_local, 'ctx', axis=0, tiled=True)  490 us
    all_gather x1, waiting for transfers between devices, per_device(): lax.all_gather(out_local, 'ctx', axis=0, tiled=True)  318 us
    psum x1, waiting for transfers between devices, per_device(): lax.psum(in_grad_local.astype(jnp.bfloat16), 'dp').astype(jnp.float32)  247 us
    all_gather x1, waiting for transfers between devices, per_device(): lax.all_gather(both_grads, 'ctx', axis=0, tiled=True)  138 us
    all_to_all x1, waiting for transfers between devices, per_device(): lax.all_to_all(left_stack, 'ctx', split_axis=1, concat_axis=0, tiled=True)  99.6 us
    ppermute x8, starting transfers between devices, from_behind_2(): return lax.ppermute(value, axis, pairs)  88.4 us
    psum x1, waiting for transfers between devices, per_device(): lax.psum((gain_local, normbias_local, qkv_bias_local, out_bias_grad, up_b...  52.9 us
    dot_general x2, matrix products, contract_last(): lax.dot_general(left, right, (((1,), (1,)), no_batch), preferred_element_...  50.6 us
  transfers between devices with their start and end apart: 25, of which 11 were waited for; matrix products, arithmetic and copies ran while one was open for 17% of the time, Pallas kernels for 0%

commit v1 on v0

v1 whole, which is shorter than its diff:
```python
from functools import partial

import jax
import jax.numpy as jnp
from jax import lax
from jax.sharding import PartitionSpec as P

ROT = 32
EPSILON = 1e-05
MASKED = -1e30
ROPE_BASE = 10000.0
BF16 = jnp.bfloat16
F32 = jnp.float32


def rotary_tables(positions):
    half_rot = ROT // 2
    frequency = ROPE_BASE ** (-(jnp.arange(half_rot, dtype=F32) * 2.0 / ROT))
    angles = positions.astype(F32)[..., None] * frequency
    cosine = jnp.cos(angles)
    sine = jnp.sin(angles)
    return (
        jnp.concatenate([cosine, cosine], -1)[..., None, :],
        jnp.concatenate([sine, sine], -1)[..., None, :],
    )


def rotate(values, cosine, sine):
    half_rot = ROT // 2
    turned = values[..., :ROT]
    swapped = jnp.concatenate([-turned[..., half_rot:], turned[..., :half_rot]], -1)
    return jnp.concatenate([turned * cosine + swapped * sine, values[..., ROT:]], -1)


def rotate_back(gradient, cosine, sine):
    half_rot = ROT // 2
    turned = gradient[..., :ROT]
    scaled = turned * sine
    swapped = jnp.concatenate([scaled[..., half_rot:], -scaled[..., :half_rot]], -1)
    return jnp.concatenate([turned * cosine + swapped, gradient[..., ROT:]], -1)


def dot(left, right, contract):
    return lax.dot_general(
        left, right, ((contract[:1], contract[1:]), ((), ())), preferred_element_type=F32
    )


def per_device(
    tokens,
    positions,
    norm_gain,
    norm_bias,
    qkv_weight,
    qkv_bias,
    dense_weight,
    dense_bias,
    up_weight,
    up_bias,
    down_weight,
    down_bias,
    clip_limit,
    cotangent,
):
    seqs, stretch, width = tokens.shape
    heads = clip_limit.shape[0]
    head_dim = width // heads
    rows = seqs * stretch
    parts = lax.axis_size("ctx")
    part = lax.axis_index("ctx")
    own_heads = heads // parts
    own = own_heads * head_dim
    own_rows = qkv_weight.shape[0]
    own_ff = down_weight.shape[0]
    length = stretch * parts
    all_rows = seqs * length
    scale = head_dim ** (-0.5)

    pieces = jnp.concatenate(
        [
            qkv_weight.reshape(own_rows, 3, parts, own)
            .transpose(2, 0, 1, 3)
            .reshape(parts, own_rows, 3 * own),
            up_weight.reshape(own_rows, parts, own_ff).transpose(1, 0, 2),
        ],
        axis=2,
    )
    in_weight = lax.all_to_all(pieces, "ctx", split_axis=0, concat_axis=0, tiled=True).reshape(
        width, 3 * own + own_ff
    )

    grad_rows = lax.all_gather(cotangent, "ctx", axis=1, tiled=True).reshape(all_rows, width)
    inputs = tokens.reshape(rows, width).astype(F32)
    centre = inputs - jnp.mean(inputs, axis=-1, keepdims=True)
    inv_std = lax.rsqrt(jnp.mean(centre * centre, axis=-1, keepdims=True) + EPSILON)
    normed = centre * inv_std
    hidden_local = (normed * norm_gain + norm_bias).astype(BF16)
    hidden = lax.all_gather(
        hidden_local.reshape(seqs, stretch, width), "ctx", axis=1, tiled=True
    ).reshape(all_rows, width)
    all_positions = lax.all_gather(positions, "ctx", axis=1, tiled=True)

    qkv_own_bias = lax.dynamic_slice_in_dim(
        qkv_bias.reshape(3, parts, own), part, 1, axis=1
    ).reshape(3 * own)
    up_own_bias = lax.dynamic_slice_in_dim(up_bias, part * own_ff, own_ff)

    projected = dot(hidden, in_weight, (1, 0))
    joined = projected[:, : 3 * own] + qkv_own_bias
    upward = projected[:, 3 * own :] + up_own_bias
    cosine, sine = rotary_tables(all_positions)
    shaped = joined.reshape(seqs, length, 3, own_heads, head_dim)
    queries = rotate(shaped[:, :, 0], cosine, sine).astype(BF16)
    keys = rotate(shaped[:, :, 1], cosine, sine).astype(BF16)
    values = shaped[:, :, 2].astype(BF16)
    place = jnp.arange(length, dtype=jnp.int32)
    allowed = place[:, None] >= place[None, :]
    scores = (
        jnp.einsum("sqhd,skhd->shqk", queries, keys, preferred_element_type=F32) * scale
    )
    scores = jnp.where(allowed, scores, MASKED)
    row_max = jnp.max(scores, axis=-1, keepdims=True)
    expo = jnp.exp(scores - row_max)
    row_sum = jnp.sum(expo, axis=-1, keepdims=True)
    probs = expo / row_sum
    probs_low = probs.astype(BF16)
    mixed = jnp.einsum("shqk,skhd->sqhd", probs_low, values, preferred_element_type=F32)
    attended = mixed.reshape(all_rows, own).astype(BF16)
    own_maxima = jnp.max(row_max, axis=(0, 2, 3))
    slots = lax.dynamic_update_slice_in_dim(
        jnp.full((heads,), MASKED, F32), own_maxima, part * own_heads, axis=0
    )
    head_maxima = lax.pmax(slots, ("dp", "ctx"))

    activated = jax.nn.gelu(upward, approximate=True).astype(BF16)
    branch = dot(attended, dense_weight, (1, 0)) + dot(activated, down_weight, (1, 0))
    branch_sum = lax.psum_scatter(
        branch.astype(BF16).reshape(seqs, length, width), "ctx", scatter_dimension=1, tiled=True
    ).reshape(rows, width)
    layer_out = (inputs + branch_sum.astype(F32) + dense_bias + down_bias).astype(BF16)

    mixed_grad = dot(grad_rows, dense_weight, (1, 1)).astype(BF16)
    act_grad = dot(grad_rows, down_weight, (1, 1))
    dense_grad = dot(attended, grad_rows, (0, 0))
    down_grad = dot(activated, grad_rows, (0, 0))
    out_bias_grad = jnp.sum(cotangent.reshape(rows, width).astype(F32), axis=0)
    unused_value, gelu_back = jax.vjp(partial(jax.nn.gelu, approximate=True), upward)
    up_low = gelu_back(act_grad)[0].astype(BF16)

    mixed_low = mixed_grad.reshape(seqs, length, own_heads, head_dim)
    value_grad = jnp.einsum("shqk,sqhd->skhd", probs_low, mixed_low, preferred_element_type=F32)
    prob_grad = jnp.einsum("sqhd,skhd->shqk", mixed_low, values, preferred_element_type=F32)
    delta = jnp.sum(probs * prob_grad, axis=-1, keepdims=True)
    score_grad = (probs * (prob_grad - delta)).astype(BF16)
    query_grad = (
        jnp.einsum("shqk,skhd->sqhd", score_grad, keys, preferred_element_type=F32) * scale
    )
    key_grad = (
        jnp.einsum("shqk,sqhd->skhd", score_grad, queries, preferred_element_type=F32) * scale
    )
    joined_low = (
        jnp.stack(
            [
                rotate_back(query_grad, cosine, sine),
                rotate_back(key_grad, cosine, sine),
                value_grad,
            ],
            axis=2,
        )
        .reshape(all_rows, 3 * own)
        .astype(BF16)
    )

    both = jnp.concatenate([joined_low, up_low], axis=1)
    hidden_part = dot(both, in_weight, (1, 1))
    hidden_grad = (
        lax.psum_scatter(
            hidden_part.astype(BF16).reshape(seqs, length, width),
            "ctx",
            scatter_dimension=1,
            tiled=True,
        )
        .reshape(rows, width)
        .astype(F32)
    )
    in_grad = dot(hidden, both, (0, 0)).astype(BF16)
    in_quarter = lax.psum_scatter(
        in_grad.reshape(parts, own_rows, 3 * own + own_ff),
        "dp",
        scatter_dimension=1,
        tiled=True,
    )
    in_quarter = lax.all_to_all(in_quarter, "ctx", split_axis=0, concat_axis=0, tiled=True)
    in_rows = lax.all_gather(in_quarter.transpose(1, 0, 2), "dp", axis=0, tiled=True)
    qkv_grad = (
        in_rows[:, :, : 3 * own]
        .reshape(own_rows, parts, 3, own)
        .transpose(0, 2, 1, 3)
        .reshape(own_rows, 3 * width)
        .astype(F32)
    )
    up_grad = in_rows[:, :, 3 * own :].reshape(own_rows, parts * own_ff).astype(F32)
    out_grad = lax.psum(jnp.concatenate([dense_grad, down_grad], axis=0).astype(BF16), "dp")

    gain_part = jnp.sum(hidden_grad * normed, axis=0)
    shift_part = jnp.sum(hidden_grad, axis=0)
    scaled = hidden_grad * norm_gain
    tokens_grad = cotangent.reshape(rows, width).astype(F32) + inv_std * (
        scaled
        - jnp.mean(scaled, axis=-1, keepdims=True)
        - normed * jnp.mean(scaled * normed, axis=-1, keepdims=True)
    )
    qkv_bias_part = lax.dynamic_update_slice(
        jnp.zeros((3, parts, own), F32),
        jnp.sum(joined_low.astype(F32), axis=0).reshape(3, 1, own),
        (0, part, 0),
    ).reshape(3 * width)
    up_bias_part = lax.dynamic_update_slice(
        jnp.zeros((parts * own_ff,), F32), jnp.sum(up_low.astype(F32), axis=0), (part * own_ff,)
    )
    gain_grad, shift_grad, qkv_bias_grad, out_bias_grad, up_bias_grad = lax.psum(
        (gain_part, shift_part, qkv_bias_part, out_bias_grad, up_bias_part), ("dp", "ctx")
    )
    limits = clip_limit.astype(F32)
    factor = limits / jnp.maximum(head_maxima, limits)
    column_scale = jnp.tile(jnp.repeat(jnp.sqrt(factor), head_dim), 2)
    clipped_weight = qkv_weight[:, : 2 * width].astype(F32) * column_scale
    clipped_bias = qkv_bias[: 2 * width] * column_scale
    return (
        layer_out.reshape(seqs, stretch, width),
        tokens_grad.reshape(seqs, stretch, width),
        gain_grad,
        shift_grad,
        qkv_grad,
        qkv_bias_grad,
        out_grad[:own].astype(F32),
        out_bias_grad,
        up_grad,
        up_bias_grad,
        out_grad[own:].astype(F32),
        out_bias_grad,
        head_maxima,
        clipped_weight,
        clipped_bias,
    )


def solution(mesh):
    rows = P("dp", "ctx", None)
    weight = P("ctx", None)
    in_specs = (rows, P("dp", "ctx"), P(), P()) + (weight, P()) * 4 + (P(), rows)
    out_specs = (
        (rows, rows, P(), P()) + (weight, P()) * 4 + (P(), weight, P())
    )
    return jax.shard_map(
        per_device, mesh=mesh, in_specs=in_specs, out_specs=out_specs, check_vma=False
    )
```

time: 2030 us -> 976 us (0.48)
  waiting for transfers between devices: 1430 us -> 472 us
  blocking collectives: 38.1 us -> 212 us
  starting transfers between devices: 141 us -> 12.1 us
  matrix products: 208 us -> 128 us
  other arithmetic: 76.7 us -> 47.3 us
  loops' own time: 22 us -> 0 us
    all_gather x6 -> x3, waiting for transfers between devices: 1000 us -> 82.7 us  [the longest x1 82.7 us: per_device(): lax.all_gather(in_quarter.transpose(1, 0, 2), 'dp', axis=0, tiled=True)]
    all_gather x0 -> x1, blocking collectives: none -> 174 us  [per_device(): all_positions = lax.all_gather(positions, 'ctx', axis=1, tiled=True)]
    reduce_scatter x0 -> x3, waiting for transfers between devices: none -> 170 us  [the longest x1 78.3 us: per_device(): lax.psum_scatter(hidden_part.astype(BF16).reshape(seqs, length, width), '...]
    ppermute x15 -> x0, starting transfers between devices: 124 us -> none  [the longest x8 88.4 us: from_behind_2(): return lax.ppermute(value, axis, pairs)]
    psum x2, waiting for transfers between devices: 299 us -> 190 us  [the longest x1 121 us: per_device(): lax.psum((gain_part, shift_part, qkv_bias_part, out_bias_grad, up_bias_pa...]
    dot_general x62 -> x15, matrix products: 208 us -> 117 us  [the longest x9 73.3 us: dot(): lax.dot_general(left, right, ((contract[:1], contract[1:]), ((), ())), pr...]
    all_to_all x2, waiting for transfers between devices: 118 us -> 29.4 us  [the longest x1 29.4 us: per_device(): lax.all_to_all(pieces, 'ctx', split_axis=0, concat_axis=0, tiled=True)]
    slice x19 -> x1, local copies, waits for them, and re-layouts: 32.3 us -> 3.75 us  [per_device(): in_rows[:, :, :3 * own].reshape(own_rows, parts, 3, own)]
  transfers between devices with their start and end apart: 25 -> 10, of which waited for: 11 -> 7; matrix products, arithmetic and copies ran while one was open for 17% -> 12% of each run, Pallas kernels for 0% -> 0%
where the time goes in v1:
time: 976 us; the launch traced here: 972 us
  waiting for transfers between devices  472 us (48%)
  blocking collectives  212 us (22%)
  matrix products  128 us (13%)
  local copies, waits for them, and re-layouts  85 us (9%)
  other arithmetic  47.3 us (5%)
  between operations  15 us (2%)
  starting transfers between devices  12.1 us (1%)
    all_gather x1, blocking collectives, per_device(): all_positions = lax.all_gather(positions, 'ctx', axis=1, tiled=True)  174 us
    psum x1, waiting for transfers between devices, per_device(): lax.psum((gain_part, shift_part, qkv_bias_part, out_bias_grad, up_bias_pa...  121 us
    all_gather x1, waiting for transfers between devices, per_device(): lax.all_gather(in_quarter.transpose(1, 0, 2), 'dp', axis=0, tiled=True)  82.7 us
    reduce_scatter x1, waiting for transfers between devices, per_device(): lax.psum_scatter(hidden_part.astype(BF16).reshape(seqs, length, width), '...  78.3 us
    dot_general x9, matrix products, dot(): lax.dot_general(left, right, ((contract[:1], contract[1:]), ((), ())), pr...  73.3 us
    psum x1, waiting for transfers between devices, per_device(): lax.psum(jnp.concatenate([dense_grad, down_grad], axis=0).astype(BF16), '...  69.2 us
    reduce_scatter x1, waiting for transfers between devices, per_device(): lax.psum_scatter(branch.astype(BF16).reshape(seqs, length, width), 'ctx',...  53.5 us
    unnamed x108, local copies, waits for them, and re-layouts  43.1 us
  transfers between devices with their start and end apart: 10, of which 7 were waited for; matrix products, arithmetic and copies ran while one was open for 12% of the time, Pallas kernels for 0%

profile of v1, /device:TPU:0, one launch (start us, length us, event | category | flops | bytes accessed | tf_op | source)
XLA Modules:
  0.0 971.5 jit_solution(4422547686251745322)
XLA Ops:
  7.9 4.6 copy.74
  12.6 3.9 copy.75
  16.4 6.4 copy.76
  22.9 6.7 pad_maximum_fusion
  29.6 6.5 all-to-all-start
  38.6 174.2 %all_gather.13 = s32[1,1024]{1,0:T(1,128)S(1)} all-gather(s32[1,128]{1,0:T(1,128)S(1)} %copy-done.37), channel_id=1, replica_groups=mesh['dp'=4,'ctx'=8] {'ctx'}, dimensions={1}, use_global_device_ids=true | all-gather | bytes 4608 | tf_op jit(solution)/shard_map/all_gather | solution.py:101
  214.9 4.6 fusion.47
  219.5 29.4 %all-to-all-done = bf16[8,256,1792]{1,2,0:T(8,128)(2,1)} async-done(((bf16[8,256,1792]{1,2,0:T(8,128)(2,1)}), bf16[8,256,1792]{1,2,0:T(8,128)(2,1)}, u32[]{:S(2)}, u32[]{:S(2)}) %all-to-all-start) | async-done | bytes 7340064 | tf_op jit(solution)/shard_map/all_to_all | solution.py:88
  248.9 9.9 %copy.77 = bf16[8,256,1792]{2,1,0:T(8,128)(2,1)} copy(bf16[8,256,1792]{1,2,0:T(8,128)(2,1)} %all-to-all-done) | data formatting | bytes 14680064 | tf_op jit(solution)/shard_map/all_to_all | solution.py:88
  258.9 11.6 %fusion.22 = f32[1024,1792]{1,0:T(8,128)S(1)} fusion(bf16[2048,1792]{1,0:T(8,128)(2,1)} %bitcast.151, bf16[1,1024,2048]{2,1,0:T(8,128)(2,1)} %all-gather.4.cloned.1.call-done), kind=kOutput, calls=%fused_computation.37 | convolution fusion | flops 7516192768 | bytes 18874368 | tf_op jit(solution)/shard_map/dot_general | solution.py:44
  270.5 3.0 copy-done.5
  275.5 3.5 copy.78
  281.1 10.1 %fusion.95 = (f32[4,1024]{1,0:T(4,128)S(1)}, f32[4,1024,1024]{1,2,0:T(8,128)}) fusion(pred[1024,1024]{0,1:T(8,128)(4,1)S(1)} %iota_compare_fusion, bf16[1024,4,32]{0,2,1:T(8,128)(2,1)S(1)} %get-tuple-element.118, bf16[1024,4,32]{0,2,1:T(8,128)(2,1)S(1)} %get-tuple-element.104, bf16[1024,4,32]{0,2,1:T(8,128)(2,1)S(1)} %get-tuple-element.117, ...), kind=kOutput, calls=%fused_computation.150 | convolution fusion | flops 555746304 | bytes 18890752 | tf_op jit(solution)/shard_map/sub | solution.py:123
  291.3 9.6 fusion.37
  300.9 15.9 %multiply_reduce_fusion = (f32[4,1024]{1,0:T(4,128)S(1)}, f32[4,1024,1024]{1,2,0:T(8,128)}) fusion(f32[4,1024,1024]{1,2,0:T(8,128)} %get-tuple-element.112, f32[4,1024]{1,0:T(4,128)S(1)} %get-tuple-element.111, bf16[1024,4,64]{0,2,1:T(8,128)(2,1)} %bitcast.164, f32[1,1024,3,4,64]{1,4,3,2,0:T(8,128)} %bitcast.148), kind=kOutput, calls=%fused_computation.2 | convolution fusion | flops 549449728 | bytes 34635776 | tf_op jit(solution)/shard_map/sqhd,skhd->shqk/dot_general | solution.py:152
  316.8 8.3 multiply_convert_fusion
  325.1 2.7 fusion.40
  332.4 12.3 %convert_reduce_fusion = (f32[1024]{0:T(1024)}, bf16[1024,1024]{1,0:T(8,128)(2,1)S(1)}) fusion(f32[1024]{0:T(1024)S(1)} %copy-done.35, f32[1024,1792]{1,0:T(8,128)} %copy-done.5, bf16[1024,2048]{1,0:T(8,128)(2,1)} %param.24, bf16[1,1024,2048]{2,1,0:T(8,128)(2,1)} %all-gather.6.cloned.1.call-done), kind=kOutput, calls=%fused_computation.40 | convolution fusion | flops 4319083520 | bytes 14688256 | tf_op jit(solution)/shard_map/dot_general | solution.py:44
  344.7 8.5 convolution_convert_fusion
  353.2 7.0 copy.84
  360.3 12.0 %convert_bitcast_fusion.1 = bf16[1,1024,2048]{2,1,0:T(8,128)(2,1)} fusion(bf16[2048,1792]{1,0:T(8,128)(2,1)} %bitcast.152, bf16[1024,1024]{1,0:T(8,128)(2,1)} %copy-done.42, bf16[1024,768]{1,0:T(8,128)(2,1)S(1)} %copy-done.4), kind=kOutput, calls=%fused_computation.41 | convolution fusion | flops 7525629952 | bytes 15204352 | tf_op jit(solution)/shard_map/dot_general | solution.py:44
  373.3 9.1 fusion.44
  382.4 8.5 fusion.92
  390.9 3.3 fusion.31
  394.7 3.6 fusion.34
  398.3 8.8 fusion.28
  407.1 2.8 pad_maximum_fusion.1
  410.0 37.8 %reduce-scatter.8.cloned.1.call-done = bf16[8,64,1792]{2,0,1:T(8,128)(2,1)} async-done(((bf16[8,256,1792]{2,0,1:T(8,128)(2,1)}), bf16[8,64,1792]{2,0,1:T(8,128)(2,1)}) %reduce-scatter.8.cloned.1.call-update) | async-done | bytes 1835024 | tf_op jit(solution)/shard_map/reduce_scatter | solution.py:187
  447.8 3.0 copy.85
  450.9 4.6 all-to-all-start.1
  456.5 78.3 %reduce-scatter.6.cloned.1.call-done = bf16[1,128,2048]{2,1,0:T(8,128)(2,1)} async-done(((bf16[1,1024,2048]{2,1,0:T(8,128)(2,1)}), bf16[1,128,2048]{2,1,0:T(8,128)(2,1)}) %reduce-scatter.6.cloned.1.call-update) | async-done | bytes 524304 | tf_op jit(solution)/shard_map/reduce_scatter | solution.py:177
  537.0 53.5 %reduce-scatter.4.cloned.1.call-done = bf16[1,128,2048]{2,1,0:T(8,128)(2,1)} async-done(((bf16[1,1024,2048]{2,1,0:T(8,128)(2,1)}), bf16[1,128,2048]{2,1,0:T(8,128)(2,1)}) %reduce-scatter.4.cloned.1.call-update) | async-done | bytes 524304 | tf_op jit(solution)/shard_map/reduce_scatter | solution.py:137
  590.5 3.9 convert_reduce_fusion.4
  594.5 2.2 copy.86
  596.8 5.3 fusion.1
  602.4 38.0 %pmax.7 = f32[32]{0:T(128)S(1)} all-reduce(f32[32]{0:T(128)S(1)} %dynamic_update_slice.11), channel_id=1, replica_groups=mesh['dp'=4,'ctx'=8] {'dp','ctx'}, use_global_device_ids=true, to_apply=%region_22.23 | all-reduce | flops 32 | bytes 256 | tf_op jit(solution)/shard_map/pmax | solution.py:133
  641.2 4.1 convert_multiply_fusion
  645.3 69.2 %all-reduce.4.cloned.1.call-done = bf16[1280,2048]{1,0:T(8,128)(2,1)} async-done(((bf16[1280,2048]{1,0:T(8,128)(2,1)}), bf16[1280,2048]{1,0:T(8,128)(2,1)}) %all-reduce.4.cloned.1.call-update) | async-done | bytes 5242896 | tf_op jit(solution)/shard_map/psum | solution.py:203
  714.5 2.8 slice_convert_fusion.2
  717.3 6.7 slice_convert_fusion
  724.0 120.5 %all-reduce.6.cloned.1.call-done = (f32[2048]{0:T(1024)}, f32[2048]{0:T(1024)}, f32[6144]{0:T(1024)}, f32[2048]{0:T(1024)}, f32[8192]{0:T(1024)}) async-done(((f32[2048]{0:T(1024)}, f32[2048]{0:T(1024)}, f32[6144]{0:T(1024)}, f32[2048]{0:T(1024)}, f32[8192]{0:T(1024)}), (f32[2048]{0:T(1024)}, f32[2048]{0:T(1024)}, f32[6144]{0:T(1024)}, f32[2048]{0:T(1024)}, f32[8192]{0:T(1024)})) %all-reduce.6.cloned.1.call-update) | async-done | bytes 81936 | tf_op jit(solution)/shard_map/psum | solution.py:221
  844.5 82.7 %all-gather.8.cloned.1.call-done = bf16[256,8,1792]{2,1,0:T(8,128)(2,1)} async-done(((bf16[64,8,1792]{2,1,0:T(8,128)(2,1)}), bf16[256,8,1792]{2,1,0:T(8,128)(2,1)}) %all-gather.8.cloned.1.call-update) | async-done | bytes 7340048 | tf_op jit(solution)/shard_map/all_gather | solution.py:194
  927.2 3.8 slice.136
  930.9 5.0 copy.94
  935.9 3.2 slice_convert_fusion.1
  939.2 11.0 %copy.96 = f32[32,8,8,1024]{3,1,2,0:T(8,128)} copy(f32[32,8,8,1024]{3,2,1,0:T(8,128)S(1)} %bitcast.139) | data formatting | bytes 16777216
  950.9 3.3 copy.88
  954.2 6.6 copy.89
  (165 shorter events, 23.9 us)
Async XLA Ops:
  7.2 207.7 %copy-start = (bf16[256,2048]{1,0:T(8,128)(2,1)S(1)}, bf16[256,2048]{1,0:T(8,128)(2,1)}, u32[]{:S(2)}) copy-start(bf16[256,2048]{1,0:T(8,128)(2,1)} %param.20) | copy-start | bytes 3145732
  7.2 207.7 %all-gather.6.cloned.1.call-start = ((), (), s32[]{:S(2)}) async-start(), calls=%async_computation.7 | async-start | bytes 4718592 | tf_op jit(solution)/shard_map/all_gather | solution.py:92
  29.6 6.6 copy-start.1
  29.6 7.8 copy-start.19
  29.6 7.8 copy-start.28
  29.6 9.1 copy-start.37
  29.6 183.3 %copy-start.21 = (f32[6144]{0:T(1024)S(1)}, f32[6144]{0:T(1024)}, u32[]{:S(2)}) copy-start(f32[6144]{0:T(1024)} %param.19) | copy-start | bytes 73732
  29.6 219.4 %all-to-all-start = ((bf16[8,256,1792]{1,2,0:T(8,128)(2,1)}), bf16[8,256,1792]{1,2,0:T(8,128)(2,1)}, u32[]{:S(2)}, u32[]{:S(2)}) async-start(bf16[8,256,1792]{1,2,0:T(8,128)(2,1)} %pad_maximum_fusion), calls=%async_computation | async-start | bytes 14680064 | tf_op jit(solution)/shard_map/all_to_all | solution.py:88
  36.1 222.8 %all-gather.4.cloned.1.call-start = ((), (), s32[]{:S(2)}) async-start(), calls=%async_computation.5 | async-start | bytes 4718592 | tf_op jit(solution)/shard_map/all_gather | solution.py:98
  38.6 409.3 %reduce-scatter.8.cloned.1.call-start = ((), (), s32[]{:S(2)}) async-start(), calls=%async_computation.9 | async-start | bytes 9175040 | tf_op jit(solution)/shard_map/reduce_scatter | solution.py:187
  214.9 76.4 %copy-start.6 = (pred[1024,1024]{0,1:T(8,128)(4,1)}, pred[1024,1024]{0,1:T(8,128)(4,1)S(1)}, u32[]{:S(2)}) copy-start(pred[1024,1024]{0,1:T(8,128)(4,1)S(1)} %iota_compare_fusion) | copy-start | bytes 3145732
  270.5 3.1 copy-start.5
  280.7 10.5 %copy-start.9 = (bf16[1024,4,32]{0,2,1:T(8,128)(2,1)}, bf16[1024,4,32]{0,2,1:T(8,128)(2,1)S(1)}, u32[]{:S(2)}) copy-start(bf16[1024,4,32]{0,2,1:T(8,128)(2,1)S(1)} %get-tuple-element.118) | copy-start | bytes 786436
  280.8 91.8 %copy-start.7 = (bf16[1024,4,32]{0,2,1:T(8,128)(2,1)}, bf16[1024,4,32]{0,2,1:T(8,128)(2,1)S(1)}, u32[]{:S(2)}) copy-start(bf16[1024,4,32]{0,2,1:T(8,128)(2,1)S(1)} %get-tuple-element.117) | copy-start | bytes 786436
  281.1 10.2 %copy-start.12 = (bf16[1024,4,32]{0,2,1:T(8,128)(2,1)}, bf16[1024,4,32]{0,2,1:T(8,128)(2,1)S(1)}, u32[]{:S(2)}) copy-start(bf16[1024,4,32]{0,2,1:T(8,128)(2,1)S(1)} %get-tuple-element.103) | copy-start | bytes 786436
  281.1 10.2 %copy-start.14 = (bf16[1024,4,32]{0,2,1:T(8,128)(2,1)}, bf16[1024,4,32]{0,2,1:T(8,128)(2,1)S(1)}, u32[]{:S(2)}) copy-start(bf16[1024,4,32]{0,2,1:T(8,128)(2,1)S(1)} %get-tuple-element.104) | copy-start | bytes 786436
  300.9 15.9 %slice-start = ((s8[16777216]{0:T(1024)(128)(4,1)}), s8[4194304]{0:T(1024)(128)(4,1)S(1)}, s32[]{:S(2)}) async-start(s8[16777216]{0:T(1024)(128)(4,1)} %bitcast.142), calls=%async_computation.13 | async-start | bytes 8388608
  300.9 15.9 %slice-start.1 = ((s8[16777216]{0:T(1024)(128)(4,1)}), s8[4194304]{0:T(1024)(128)(4,1)S(1)}, s32[]{:S(2)}) async-start(s8[16777216]{0:T(1024)(128)(4,1)} %bitcast.142), calls=%async_computation.14 | async-start | bytes 8388608
  300.9 15.9 %slice-start.2 = ((s8[16777216]{0:T(1024)(128)(4,1)}), s8[4194304]{0:T(1024)(128)(4,1)S(1)}, s32[]{:S(2)}) async-start(s8[16777216]{0:T(1024)(128)(4,1)} %bitcast.142), calls=%async_computation.15 | async-start | bytes 8388608
  300.9 15.9 %slice-start.3 = ((s8[16777216]{0:T(1024)(128)(4,1)}), s8[4194304]{0:T(1024)(128)(4,1)S(1)}, s32[]{:S(2)}) async-start(s8[16777216]{0:T(1024)(128)(4,1)} %bitcast.142), calls=%async_computation.16 | async-start | bytes 8388608
  316.8 8.3 copy-start.13
  332.4 12.3 %copy-start.4 = (bf16[1024,768]{1,0:T(8,128)(2,1)S(1)}, bf16[1024,768]{1,0:T(8,128)(2,1)}, u32[]{:S(2)}) copy-start(bf16[1024,768]{1,0:T(8,128)(2,1)} %copy.83) | copy-start | bytes 4718596
  332.4 12.3 %copy-start.39 = (bf16[1,1024,2048]{2,1,0:T(8,128)(2,1)S(1)}, bf16[1,1024,2048]{2,1,0:T(8,128)(2,1)}, u32[]{:S(2)}) copy-start(bf16[1,1024,2048]{2,1,0:T(8,128)(2,1)} %all-gather.4.cloned.1.call-done) | copy-start | bytes 12582916
  344.7 8.5 copy-start.42
  360.2 174.6 %reduce-scatter.6.cloned.1.call-start = ((), (), s32[]{:S(2)}) async-start(), calls=%async_computation.8 | async-start | bytes 4718592 | tf_op jit(solution)/shard_map/reduce_scatter | solution.py:177
  372.3 218.2 %reduce-scatter.4.cloned.1.call-start = ((), (), s32[]{:S(2)}) async-start(), calls=%async_computation.6 | async-start | bytes 4718592 | tf_op jit(solution)/shard_map/reduce_scatter | solution.py:137
  394.2 320.3 %all-reduce.4.cloned.1.call-start = ((), (), s32[]{:S(2)}) async-start(), calls=%async_computation.11 | async-start | bytes 10485760 | tf_op jit(solution)/shard_map/psum | solution.py:203
  394.7 3.6 copy-start.38
  409.9 46.4 %copy-start.36 = (f32[1024]{0:T(1024)S(1)}, f32[1024]{0:T(1024)}, u32[]{:S(2)}) copy-start(f32[1024]{0:T(1024)} %get-tuple-element.115) | copy-start | bytes 12292
  409.9 124.9 %copy-start.2 = (bf16[1,128,2048]{2,1,0:T(8,128)(2,1)S(1)}, bf16[1,128,2048]{2,1,0:T(8,128)(2,1)}, u32[]{:S(2)}) copy-start(bf16[1,128,2048]{2,1,0:T(8,128)(2,1)} %param.14) | copy-start | bytes 1572868
  410.0 124.9 %copy-start.20 = (f32[2048]{0:T(1024)S(1)}, f32[2048]{0:T(1024)}, u32[]{:S(2)}) copy-start(f32[2048]{0:T(1024)} %param.16) | copy-start | bytes 24580
  410.0 124.9 %copy-start.27 = (f32[128]{0:T(128)S(1)}, f32[128]{0:T(128)}, u32[]{:S(2)}) copy-start(f32[128]{0:T(128)} %copy-done.26) | copy-start | bytes 1540
  410.0 124.9 %copy-start.34 = (f32[128]{0:T(128)S(1)}, f32[128]{0:T(128)}, u32[]{:S(2)}) copy-start(f32[128]{0:T(128)} %copy-done.33) | copy-start | bytes 1540
  410.0 180.5 %copy-start.29 = (f32[2048]{0:T(1024)S(1)}, f32[2048]{0:T(1024)}, u32[]{:S(2)}) copy-start(f32[2048]{0:T(1024)} %param.25) | copy-start | bytes 24580
  410.0 180.5 %copy-start.30 = (f32[2048]{0:T(1024)S(1)}, f32[2048]{0:T(1024)}, u32[]{:S(2)}) copy-start(f32[2048]{0:T(1024)} %param.21) | copy-start | bytes 24580
  450.9 143.6 %all-to-all-start.1 = ((bf16[8,64,1792]{2,1,0:T(8,128)(2,1)}), bf16[8,64,1792]{2,1,0:T(8,128)(2,1)S(1)}, u32[]{:S(2)}, u32[]{:S(2)}) async-start(bf16[8,64,1792]{2,1,0:T(8,128)(2,1)} %copy.85), calls=%async_computation.4 | async-start | bytes 3670016 | tf_op jit(solution)/shard_map/all_to_all | solution.py:193
  455.5 389.0 %all-reduce.6.cloned.1.call-start = ((), (), s32[]{:S(2)}) async-start(), calls=%async_computation.12 | async-start | bytes 163840 | tf_op jit(solution)/shard_map/psum | solution.py:221
  456.5 137.9 %copy-start.18 = (f32[8192]{0:T(1024)}, f32[8192]{0:T(1024)S(1)}, u32[]{:S(2)}) copy-start(f32[8192]{0:T(1024)S(1)} %dynamic_update_slice.10) | copy-start | bytes 98308
  594.5 332.7 %all-gather.8.cloned.1.call-start = ((), (), s32[]{:S(2)}) async-start(), calls=%async_computation.10 | async-start | bytes 9175040 | tf_op jit(solution)/shard_map/all_gather | solution.py:194
  596.8 43.6 %copy-start.40 = (s32[32]{0:T(128)S(1)}, s32[32]{0:T(128)}, u32[]{:S(2)}) copy-start(s32[32]{0:T(128)} %param.26) | copy-start | bytes 388
  596.8 43.7 %copy-start.22 = (f32[6144]{0:T(1024)S(1)}, f32[6144]{0:T(1024)}, u32[]{:S(2)}) copy-start(f32[6144]{0:T(1024)} %param.19) | copy-start | bytes 73732
  640.4 76.9 %copy-start.41 = (f32[32]{0:T(128)}, f32[32]{0:T(128)S(1)}, u32[]{:S(2)}) copy-start(f32[32]{0:T(128)S(1)} %pmax.7) | copy-start | bytes 388
  939.2 11.0 %copy-start.3 = (bf16[256,8,768]{0,2,1:T(8,128)(2,1)S(1)}, bf16[256,8,768]{0,2,1:T(8,128)(2,1)}, u32[]{:S(2)}) copy-start(bf16[256,8,768]{0,2,1:T(8,128)(2,1)} %copy.94) | copy-start | bytes 9437188
  954.2 6.6 copy-start.24
  954.2 7.2 copy-start.32
  954.2 7.8 copy-start.31
  954.2 8.4 copy-start.25
  954.2 9.6 copy-start.23
  (9 other events, 15.6 us)
Sparse Core Ops, SparseCore 0:
  9.6 67.6 all-gather.5
  79.5 135.0 all-gather.3
  360.3 87.4 reduce-scatter.7
  450.6 84.2 reduce-scatter.5
  537.6 52.9 reduce-scatter.3
  594.3 120.2 all-reduce.3
  722.1 122.3 all-reduce.5
  846.9 80.2 all-gather.7

commit v2 on v1

v2 whole, which is shorter than its diff:
```python
from functools import partial

import jax
import jax.numpy as jnp
from jax import lax
from jax.experimental import pallas as pl
from jax.experimental.pallas import tpu as pltpu
from jax.sharding import PartitionSpec as P

ROT = 32
EPSILON = 1e-05
MASKED = -1e30
ROPE_BASE = 10000.0
BF16 = jnp.bfloat16
F32 = jnp.float32
LANES = 128
HEAD = 64


def dot(left, right, contract):
    return lax.dot_general(
        left, right, ((contract[:1], contract[1:]), ((), ())), preferred_element_type=F32
    )


def swap(value, axis, bit):
    return lax.ppermute(value, axis, [(i, i ^ bit) for i in range(lax.axis_size(axis))])


def bits_of(axis):
    return [1 << i for i in range(lax.axis_size(axis).bit_length() - 1)]


def all_sum(value, axes):
    for axis in axes:
        for bit in bits_of(axis):
            value = value + swap(value, axis, bit)
    return value


def all_rows(value, axis):
    index = lax.axis_index(axis)
    for bit in bits_of(axis):
        other = swap(value, axis, bit)
        upper = (index & bit) != 0
        value = jnp.where(
            upper, jnp.concatenate([other, value], 0), jnp.concatenate([value, other], 0)
        )
    return value


def take(value, start, size, axis):
    return lax.dynamic_slice_in_dim(value, start, size, axis)


def first_place(index):
    return (index & 1) * 2 + (index >> 1)


def my_part(value, axis):
    index = lax.axis_index("dp")
    size = value.shape[axis] // 8
    return jnp.concatenate(
        [
            take(value, first_place(index) * size, size, axis),
            take(value, (4 + index) * size, size, axis),
        ],
        axis,
    )


def after(value, *others):
    return lax.optimization_barrier((value, others))[0]


def along_both(pair):
    return swap(pair[0], "dp", 1), swap(pair[1], "dp", 2)


def plus(left, right):
    return (left.astype(F32) + right.astype(F32)).astype(BF16)


def outgoing(value, axis):
    index = lax.axis_index("dp")
    size = value.shape[axis] // 8
    return (
        take(value, (1 - (index & 1)) * 2 * size, 2 * size, axis),
        take(value, (4 + (1 - (index >> 1)) * 2) * size, 2 * size, axis),
    )


def first_sums(value, received, axis):
    index = lax.axis_index("dp")
    size = value.shape[axis] // 8
    return (
        plus(take(value, (index & 1) * 2 * size, 2 * size, axis), received[0]),
        plus(take(value, (4 + (index >> 1) * 2) * size, 2 * size, axis), received[1]),
    )


def outgoing_again(sums, axis):
    index = lax.axis_index("dp")
    size = sums[0].shape[axis] // 2
    return (
        take(sums[1], (1 - (index & 1)) * size, size, axis),
        take(sums[0], (1 - (index >> 1)) * size, size, axis),
    )


def second_sums(sums, received, axis):
    index = lax.axis_index("dp")
    size = sums[0].shape[axis] // 2
    return jnp.concatenate(
        [
            plus(take(sums[0], (index >> 1) * size, size, axis), received[1]),
            plus(take(sums[1], (index & 1) * size, size, axis), received[0]),
        ],
        axis,
    )


def forwarded(received, axis):
    half = received[0].shape[axis] // 2
    return (
        lax.slice_in_dim(received[1], 0, half, axis=axis),
        lax.slice_in_dim(received[0], half, 2 * half, axis=axis),
    )


def four_parts(part, near, far, axis):
    return [part, near[0], near[1], jnp.concatenate(far, axis)]


def place_rows(index_ref, *refs):
    parts, out = refs[:-1], refs[-1]
    eighth = parts[0].shape[-2] // 2
    me = index_ref[0]
    for offset, ref in enumerate(parts):
        owner = me ^ offset
        block = ref[0].astype(out.dtype)
        start = pl.multiple_of(first_place(owner) * eighth, eighth)
        out[pl.ds(start, eighth), :] = block[:eighth]
        start = pl.multiple_of((4 + owner) * eighth, eighth)
        out[pl.ds(start, eighth), :] = block[eighth:]


def place_columns(index_ref, *refs):
    parts, out = refs[:-1], refs[-1]
    eighth = parts[0].shape[-1] // 2
    me = index_ref[0]
    for offset, ref in enumerate(parts):
        owner = me ^ offset
        start = pl.multiple_of(first_place(owner) * eighth, eighth)
        out[:, pl.ds(start, eighth)] = ref[:, :eighth].astype(out.dtype)
        start = pl.multiple_of((4 + owner) * eighth, eighth)
        out[:, pl.ds(start, eighth)] = ref[:, eighth:].astype(out.dtype)


def place(body, parts, grid, in_block, in_map, out_shape, out_block, out_map):
    index = lax.axis_index("dp").astype(jnp.int32).reshape(1)
    size = sum(part.size * part.dtype.itemsize for part in parts)
    return pl.pallas_call(
        body,
        out_shape=out_shape,
        grid_spec=pltpu.PrefetchScalarGridSpec(
            num_scalar_prefetch=1,
            grid=grid,
            in_specs=[pl.BlockSpec(in_block, in_map)] * 4,
            out_specs=pl.BlockSpec(out_block, out_map),
        ),
        compiler_params=pltpu.CompilerParams(vmem_limit_bytes=32 << 20),
        cost_estimate=pl.CostEstimate(
            flops=0,
            transcendentals=0,
            bytes_accessed=size + out_shape.size * out_shape.dtype.itemsize,
        ),
    )(index, *parts)


def full_rows(parts, own_rows):
    blocks, size, columns = parts[0].shape
    return place(
        place_rows,
        parts,
        (blocks,),
        (1, size, columns),
        lambda i, index: (i, 0, 0),
        jax.ShapeDtypeStruct((blocks * own_rows, columns), parts[0].dtype),
        (own_rows, columns),
        lambda i, index: (i, 0),
    )


def full_grad(parts, own_rows, groups):
    blocks, size, columns = parts[0].shape
    width = columns // groups
    return place(
        place_rows,
        parts,
        (groups, blocks),
        (1, size, width),
        lambda g, i, index: (i, 0, g),
        jax.ShapeDtypeStruct((own_rows, groups * blocks * width), F32),
        (own_rows, width),
        lambda g, i, index: (0, g * blocks + i),
    )


def full_columns(parts, first, count, block):
    size = parts[0].shape[1]
    return place(
        place_columns,
        parts,
        (count // block,),
        (block, size),
        lambda i, index: (i + first // block, 0),
        jax.ShapeDtypeStruct((count, 4 * size), F32),
        (block, 4 * size),
        lambda i, index: (i, 0),
    )


def rotary_lanes(positions):
    half = ROT // 2
    lane = jnp.arange(LANES, dtype=jnp.int32) % HEAD
    frequency = ROPE_BASE ** (-((lane % half).astype(F32) * 2.0 / ROT))
    angles = positions.astype(F32)[:, None] * frequency
    sine = jnp.sin(angles)
    return (
        jnp.where(lane < ROT, jnp.cos(angles), 1.0),
        jnp.where(lane < half, -sine, 0.0),
        jnp.where((lane >= half) & (lane < ROT), sine, 0.0),
    )


def turn(value, cosine, above, below, sign):
    half = ROT // 2
    size = value.shape[1]
    from_above = pltpu.roll(value, size - half, 1)
    from_below = pltpu.roll(value, half, 1)
    return value * cosine + sign * (from_above * above + from_below * below)


def nt(left, right):
    return lax.dot_general(left, right, (((1,), (1,)), ((), ())), preferred_element_type=F32)


def nn(left, right):
    return lax.dot_general(left, right, (((1,), (0,)), ((), ())), preferred_element_type=F32)


def pair_of(head):
    return slice(head // 2 * LANES, head // 2 * LANES + LANES)


def only(value, head):
    lane = lax.broadcasted_iota(jnp.int32, value.shape, 1)
    return jnp.where((lane // HEAD) == head % 2, value, jnp.zeros_like(value))


def fold(value, op):
    out = value[:, :LANES]
    for start in range(LANES, value.shape[1], LANES):
        out = op(out, value[:, start : start + LANES])
    return out


def attend_kernel(
    heads, scale, joined, bias, cosine, above, below,
    q_out, k_out, v_out, mixed_out, low_out, log_out, max_out,
    k_all, v_all, scores, total,
):
    step = pl.program_id(0)
    block, own = q_out.shape
    copies = own // LANES
    tables = [jnp.concatenate([t[...]] * copies, axis=1) for t in (cosine, above, below)]
    q = turn(joined[:, :own] + bias[:, :own], *tables, 1.0).astype(BF16)
    k = turn(joined[:, own : 2 * own] + bias[:, own : 2 * own], *tables, 1.0).astype(BF16)
    v = (joined[:, 2 * own :] + bias[:, 2 * own :]).astype(BF16)
    q_out[...] = q
    k_out[...] = k
    v_out[...] = v
    here = pl.ds(pl.multiple_of(step * block, block), block)
    k_all[here, :] = k
    v_all[here, :] = v
    queries = [only(q[:, pair_of(h)], h) * jnp.asarray(scale, BF16) for h in range(heads)]
    allowed = lax.broadcasted_iota(jnp.int32, (block, block), 0) >= lax.broadcasted_iota(
        jnp.int32, (block, block), 1
    )

    def score(j, peaks, diagonal):
        spot = pl.ds(pl.multiple_of(j * block, block), block)
        out = []
        for h in range(heads):
            s = nt(queries[h], k_all[spot, pair_of(h)])
            if diagonal:
                s = jnp.where(allowed, s, MASKED)
            scores[h, :, spot] = s
            out.append(jnp.maximum(peaks[h], fold(s, jnp.maximum)))
        return out

    peaks = [jnp.full((block, LANES), MASKED, F32)] * heads
    peaks = lax.fori_loop(0, step, lambda j, c: score(j, c, False), peaks)
    peaks = score(step, peaks, True)
    peaks = [jnp.max(p, axis=1, keepdims=True) for p in peaks]
    total[...] = jnp.zeros_like(total)

    def gather(j, sums):
        spot = pl.ds(pl.multiple_of(j * block, block), block)
        out = []
        for h in range(heads):
            p = jnp.exp(scores[h, :, spot] - peaks[h])
            out.append(sums[h] + fold(p, jnp.add))
            total[h] += nn(p.astype(BF16), v_all[spot, pair_of(h)])
        return out

    sums = lax.fori_loop(0, step + 1, gather, [jnp.zeros((block, LANES), F32)] * heads)
    lane = lax.broadcasted_iota(jnp.int32, (block, LANES), 1)
    logs = jnp.zeros((block, LANES), F32)
    tops = jnp.full((1, LANES), MASKED, F32)
    for h in range(heads):
        amount = jnp.sum(sums[h], axis=1, keepdims=True)
        total[h] = total[h] / amount
        logs = jnp.where(lane == h, peaks[h] + jnp.log(amount), logs)
        tops = jnp.where(lane[:1] == h, jnp.max(peaks[h], axis=0, keepdims=True), tops)
    log_out[...] = logs
    for h in range(0, heads, 2):
        mixed = jnp.where(lane < HEAD, total[h], total[h + 1])
        mixed_out[:, pair_of(h)] = mixed
        low_out[:, pair_of(h)] = mixed.astype(BF16)

    @pl.when(step == 0)
    def _():
        max_out[...] = tops

    @pl.when(step > 0)
    def _():
        max_out[...] = jnp.maximum(max_out[...], tops)


def attend(joined, bias, tables, heads, scale, block):
    length = joined.shape[0]
    own = joined.shape[1] // 3
    row = lambda i: (i, 0)
    zero = lambda i: (0, 0)
    shapes = [
        ((length, own), BF16), ((length, own), BF16), ((length, own), BF16),
        ((length, own), F32), ((length, own), BF16), ((length, LANES), F32),
    ]
    pairs = heads * length * length // 2
    return pl.pallas_call(
        partial(attend_kernel, heads, scale),
        name="attend",
        out_shape=[jax.ShapeDtypeStruct(s, d) for s, d in shapes]
        + [jax.ShapeDtypeStruct((1, LANES), F32)],
        grid_spec=pltpu.PrefetchScalarGridSpec(
            num_scalar_prefetch=0,
            grid=(length // block,),
            in_specs=[pl.BlockSpec((block, 3 * own), row), pl.BlockSpec((1, 3 * own), zero)]
            + [pl.BlockSpec((block, LANES), row)] * 3,
            out_specs=[pl.BlockSpec((block, s[1]), row) for s, d in shapes]
            + [pl.BlockSpec((1, LANES), zero)],
            scratch_shapes=[
                pltpu.VMEM((length, own), BF16),
                pltpu.VMEM((length, own), BF16),
                pltpu.VMEM((heads, block, length), F32),
                pltpu.VMEM((heads, block, LANES), F32),
            ],
        ),
        compiler_params=pltpu.CompilerParams(vmem_limit_bytes=40 << 20),
        cost_estimate=pl.CostEstimate(
            flops=4 * pairs * 2 * LANES, transcendentals=pairs, bytes_accessed=length * own * 26
        ),
    )(joined, bias, *tables)


def attend_back_kernel(
    heads, scale, q, k, v, k_here, grad, mixed, logs, cosine, above, below,
    low_out, sum_out, k_turned, k_total, v_total, q_total,
):
    step = pl.program_id(0)
    block, own = q.shape
    length = k.shape[0]
    copies = own // LANES
    spot_here = pl.ds(pl.multiple_of(step * block, block), block)

    @pl.when(step == 0)
    def _():
        k_total[...] = jnp.zeros_like(k_total)
        v_total[...] = jnp.zeros_like(v_total)

    k_turned[:, spot_here] = k_here[...].T
    q_total[...] = jnp.zeros_like(q_total)
    log_rows = logs[...].T
    product = grad[...].astype(F32) * mixed[...]
    lane = lax.broadcasted_iota(jnp.int32, (block, LANES), 1)
    deltas = jnp.zeros((block, LANES), F32)
    for h in range(heads):
        own_sum = jnp.sum(only(product[:, pair_of(h)], h), axis=1, keepdims=True)
        deltas = jnp.where(lane == h, own_sum, deltas)
    delta_rows = deltas.T
    queries = [only(q[:, pair_of(h)], h) * jnp.asarray(scale, BF16) for h in range(heads)]
    grads = [only(grad[:, pair_of(h)], h) for h in range(heads)]
    allowed = lax.broadcasted_iota(jnp.int32, (block, block), 0) <= lax.broadcasted_iota(
        jnp.int32, (block, block), 1
    )

    def visit(j, diagonal):
        spot = pl.ds(pl.multiple_of(j * block, block), block)
        for h in range(heads):
            s = nt(k[spot, pair_of(h)], queries[h])
            if diagonal:
                s = jnp.where(allowed, s, MASKED)
            p = jnp.exp(s - log_rows[h : h + 1])
            dp = nt(v[spot, pair_of(h)], grads[h])
            ds = (p * (dp - delta_rows[h : h + 1])).astype(BF16)
            v_total[spot, pair_of(h)] += nn(p.astype(BF16), grads[h])
            k_total[spot, pair_of(h)] += nn(ds, queries[h])
            q_total[h] += nn(k_turned[pair_of(h), spot], ds)

    def body(j, carry):
        visit(j, False)
        return carry

    lax.fori_loop(0, step, body, 0)
    visit(step, True)
    row = lax.broadcasted_iota(jnp.int32, (LANES, block), 0)
    tables = (cosine[spot_here, :], above[spot_here, :], below[spot_here, :])
    sums = []
    for h in range(0, heads, 2):
        dq = jnp.where(row < HEAD, q_total[h], q_total[h + 1]).T * scale
        low = turn(dq, *tables, -1.0).astype(BF16)
        low_out[spot_here, pair_of(h)] = low
        sums.append(jnp.sum(low.astype(F32), axis=0, keepdims=True))
    sums = jnp.concatenate(sums, axis=1)

    @pl.when(step == 0)
    def _():
        sum_out[:, :own] = sums

    @pl.when(step > 0)
    def _():
        sum_out[:, :own] += sums

    @pl.when(step == length // block - 1)
    def _():
        wide = [jnp.concatenate([t[...]] * copies, axis=1) for t in (cosine, above, below)]
        low = turn(k_total[...], *wide, -1.0).astype(BF16)
        low_out[:, own : 2 * own] = low
        sum_out[:, own : 2 * own] = jnp.sum(low.astype(F32), axis=0, keepdims=True)
        low = v_total[...].astype(BF16)
        low_out[:, 2 * own :] = low
        sum_out[:, 2 * own :] = jnp.sum(low.astype(F32), axis=0, keepdims=True)


def attend_back(q, k, v, grad, mixed, logs, tables, heads, scale, block):
    length, own = q.shape
    row = lambda i: (i, 0)
    zero = lambda i: (0, 0)
    rows = pl.BlockSpec((block, own), row)
    whole = pl.BlockSpec((length, own), zero)
    pairs = heads * length * length // 2
    return pl.pallas_call(
        partial(attend_back_kernel, heads, scale),
        name="attend_back",
        out_shape=[
            jax.ShapeDtypeStruct((length, 3 * own), BF16),
            jax.ShapeDtypeStruct((1, 3 * own), F32),
        ],
        grid_spec=pltpu.PrefetchScalarGridSpec(
            num_scalar_prefetch=0,
            grid=(length // block,),
            in_specs=[rows, whole, whole, rows, rows, rows, pl.BlockSpec((block, LANES), row)]
            + [pl.BlockSpec((length, LANES), zero)] * 3,
            out_specs=[
                pl.BlockSpec((length, 3 * own), zero),
                pl.BlockSpec((1, 3 * own), zero),
            ],
            scratch_shapes=[
                pltpu.VMEM((own, length), BF16),
                pltpu.VMEM((length, own), F32),
                pltpu.VMEM((length, own), F32),
                pltpu.VMEM((heads, LANES, block), F32),
            ],
        ),
        compiler_params=pltpu.CompilerParams(vmem_limit_bytes=40 << 20),
        cost_estimate=pl.CostEstimate(
            flops=10 * pairs * 2 * LANES, transcendentals=pairs, bytes_accessed=length * own * 20
        ),
    )(q, k, v, k, grad, mixed, logs, *tables)


def to_columns(rows, groups):
    parts = lax.axis_size("ctx")
    count, columns = rows.shape
    width = columns // (groups * parts)
    return (
        rows.reshape(count, groups, parts, width)
        .transpose(2, 0, 1, 3)
        .reshape(parts, count, groups * width)
    )


def exchange(blocks):
    return lax.all_to_all(blocks, "ctx", split_axis=0, concat_axis=0, tiled=True)


def gather_weights(qkv_weight, up_weight):
    own_rows = qkv_weight.shape[0]
    if lax.axis_size("dp") != 4:
        q, u = exchange(to_columns(qkv_weight, 3)), exchange(to_columns(up_weight, 1))
        return q.reshape(-1, q.shape[2]), u.reshape(-1, u.shape[2])
    q = to_columns(my_part(qkv_weight, 0), 3)
    u = to_columns(my_part(up_weight, 0), 1)
    q = exchange(q)
    q, u = lax.optimization_barrier((q, u))
    q_near = along_both((q, q))
    u = exchange(u)
    q_near, u = lax.optimization_barrier((q_near, u))
    u_near = along_both((u, u))
    q_far = along_both(forwarded(q_near, 1))
    q_far, u_near = lax.optimization_barrier((q_far, u_near))
    u_far = along_both(forwarded(u_near, 1))
    return (
        full_rows(four_parts(q, q_near, q_far, 1), own_rows),
        full_rows(four_parts(u, u_near, u_far, 1), own_rows),
    )


def reduce_input_grad(grad, own_rows, groups):
    grad = grad.reshape(lax.axis_size("ctx"), own_rows, grad.shape[1])
    part = exchange(lax.psum_scatter(grad, "dp", scatter_dimension=1, tiled=True))
    rows = lax.all_gather(part, "dp", axis=1, tiled=True)
    return (
        rows.reshape(rows.shape[0], own_rows, groups, -1)
        .transpose(1, 2, 0, 3)
        .reshape(own_rows, -1)
        .astype(F32)
    )


def per_device(
    tokens,
    positions,
    norm_gain,
    norm_bias,
    qkv_weight,
    qkv_bias,
    dense_weight,
    dense_bias,
    up_weight,
    up_bias,
    down_weight,
    down_bias,
    clip_limit,
    cotangent,
):
    seqs, stretch, width = tokens.shape
    heads = clip_limit.shape[0]
    head_dim = width // heads
    rows = seqs * stretch
    parts = lax.axis_size("ctx")
    part = lax.axis_index("ctx")
    own_heads = heads // parts
    own = own_heads * head_dim
    own_rows = qkv_weight.shape[0]
    own_ff = down_weight.shape[0]
    length = stretch * parts
    count = seqs * length
    scale = head_dim ** (-0.5)

    inputs = tokens.reshape(rows, width).astype(F32)
    centre = inputs - jnp.mean(inputs, axis=-1, keepdims=True)
    inv_std = lax.rsqrt(jnp.mean(centre * centre, axis=-1, keepdims=True) + EPSILON)
    normed = centre * inv_std
    hidden_local = (normed * norm_gain + norm_bias).astype(BF16)
    hidden = lax.all_gather(
        hidden_local.reshape(seqs, stretch, width), "ctx", axis=1, tiled=True
    ).reshape(count, width)
    grad_rows = lax.all_gather(cotangent, "ctx", axis=1, tiled=True).reshape(count, width)
    qkv_columns, up_columns = gather_weights(qkv_weight, up_weight)
    positions_all = all_rows(positions.T, "ctx").T

    qkv_own_bias = take(qkv_bias.reshape(3, parts, own), part, 1, 1).reshape(1, 3 * own)
    up_own_bias = take(up_bias, part * own_ff, own_ff, 0)

    joined = dot(hidden, qkv_columns, (1, 0))
    block = 256 if length % 256 == 0 else length
    tables = [rotary_lanes(positions_all[s]) for s in range(seqs)]
    ahead = [
        attend(
            joined[s * length : (s + 1) * length], qkv_own_bias, tables[s], own_heads, scale, block
        )
        for s in range(seqs)
    ]
    attended = jnp.concatenate([a[4] for a in ahead])
    own_maxima = jnp.max(jnp.stack([a[6][0, :own_heads] for a in ahead]), axis=0)
    upward = dot(hidden, up_columns, (1, 0)) + up_own_bias
    activated, gelu_back = jax.vjp(partial(jax.nn.gelu, approximate=True), upward)
    activated = activated.astype(BF16)

    def feed_forward_back(grad_rows):
        act_grad = dot(grad_rows, down_weight, (1, 1))
        up_low = gelu_back(act_grad)[0].astype(BF16)
        return up_low, dot(hidden, up_low, (0, 0)).astype(BF16)

    def attention_back(grad_rows):
        mixed_low = dot(grad_rows, dense_weight, (1, 1)).astype(BF16)
        back = [
            attend_back(
                q, k, v, mixed_low[s * length : (s + 1) * length], mixed, logs, tables[s],
                own_heads, scale, block,
            )
            for s, (q, k, v, mixed, low, logs, tops) in enumerate(ahead)
        ]
        joined_low = jnp.concatenate([b[0] for b in back])
        qkv_raw = dot(hidden, joined_low, (0, 0)).astype(BF16)
        return joined_low, sum(b[1] for b in back), qkv_raw

    def sum_branch(value):
        return lax.psum_scatter(
            value.astype(BF16).reshape(seqs, length, width),
            "ctx",
            scatter_dimension=1,
            tiled=True,
        ).reshape(rows, width)

    def output_part(mixed_out):
        return sum_branch(dot(mixed_out, jnp.concatenate([dense_weight, down_weight]), (1, 0)))

    def input_part(joined_low, up_low):
        return sum_branch(
            dot(joined_low, qkv_columns, (1, 1)) + dot(up_low, up_columns, (1, 1))
        )

    grad_rows, attended, activated = lax.optimization_barrier((grad_rows, attended, activated))
    mixed_out = jnp.concatenate([attended, activated], axis=1)
    out_raw = dot(mixed_out, grad_rows, (0, 0)).astype(BF16)
    if lax.axis_size("dp") == 4:
        o_send = outgoing(out_raw, 1)
        o_got = along_both(o_send)
        up_low, up_raw = feed_forward_back(after(grad_rows, o_send))
        up_raw = up_raw.reshape(parts, own_rows, own_ff)
        u_send = outgoing(up_raw, 1)
        u_got = along_both(u_send)
        joined_low, joined_sum, qkv_raw = attention_back(after(grad_rows, u_send))
        qkv_raw = qkv_raw.reshape(parts, own_rows, 3 * own)
        q_send = outgoing(qkv_raw, 1)
        q_got = along_both(q_send)
        o_sums = first_sums(out_raw, after(o_got, q_send), 1)
        o_send = outgoing_again(o_sums, 1)
        o_got = along_both(o_send)
        branch_sum = output_part(after(mixed_out, o_send))
        u_sums = first_sums(up_raw, after(u_got, o_send), 1)
        u_send = outgoing_again(u_sums, 1)
        u_got = along_both(u_send)
        hidden_grad = input_part(after(joined_low, u_send), up_low)
        q_sums = first_sums(qkv_raw, after(q_got, u_send), 1)
        q_send = outgoing_again(q_sums, 1)
        q_got = along_both(q_send)
        o_part = second_sums(o_sums, after(o_got, q_send), 1)
        o_near = along_both((o_part, o_part))
        u_part = exchange(second_sums(u_sums, after(u_got, o_part), 1))
        q_part = exchange(second_sums(q_sums, after(q_got, u_part), 1))
        u_near = along_both((u_part, u_part))
        o_far = along_both(forwarded(after(o_near, u_part), 1))
        q_near = along_both((q_part, q_part))
        u_far = along_both(forwarded(after(u_near, q_part), 1))
        q_far = along_both(forwarded(q_near, 1))
        o_parts = four_parts(o_part, o_near, o_far, 1)
        dense_grad = full_columns(o_parts, 0, own, own)
        down_grad = full_columns(o_parts, own, own_ff, own)
        up_grad = full_grad(four_parts(u_part, u_near, u_far, 1), own_rows, 1)
        qkv_grad = full_grad(four_parts(q_part, q_near, q_far, 1), own_rows, 3)
    else:
        up_low, up_raw = feed_forward_back(grad_rows)
        joined_low, joined_sum, qkv_raw = attention_back(grad_rows)
        branch_sum = output_part(mixed_out)
        hidden_grad = input_part(joined_low, up_low)
        out_grad = lax.psum(out_raw, "dp").astype(F32)
        dense_grad, down_grad = out_grad[:own], out_grad[own:]
        up_grad = reduce_input_grad(up_raw, own_rows, 1)
        qkv_grad = reduce_input_grad(qkv_raw, own_rows, 3)
        o_part = out_grad
    layer_out = (inputs + branch_sum.astype(F32) + dense_bias + down_bias).astype(BF16)
    hidden_grad = hidden_grad.astype(F32)
    gain_part = jnp.sum(hidden_grad * normed, axis=0)
    shift_part = jnp.sum(hidden_grad, axis=0)
    scaled = hidden_grad * norm_gain
    tokens_grad = cotangent.reshape(rows, width).astype(F32) + inv_std * (
        scaled
        - jnp.mean(scaled, axis=-1, keepdims=True)
        - normed * jnp.mean(scaled * normed, axis=-1, keepdims=True)
    )
    norm_sums = all_sum(jnp.stack([gain_part, shift_part]), ("dp", "ctx"))

    sums = jnp.concatenate(
        [
            joined_sum[0],
            jnp.sum(up_low.astype(F32), axis=0),
            jnp.sum(take(grad_rows, part * own, own, 1).astype(F32), axis=0),
        ]
    )[None]
    sums, own_maxima = after((sums, own_maxima), o_part)
    maxima = own_maxima[None]
    for bit in bits_of("dp"):
        both = swap(jnp.concatenate([sums, maxima], axis=1), "dp", bit)
        sums = sums + both[:, : sums.shape[1]]
        maxima = jnp.maximum(maxima, both[:, sums.shape[1] :])
    both = all_rows(jnp.concatenate([sums, maxima], axis=1), "ctx")
    cut = 3 * own + own_ff
    qkv_bias_grad = (
        both[:, : 3 * own].reshape(parts, 3, own).transpose(1, 0, 2).reshape(3 * width)
    )
    up_bias_grad = both[:, 3 * own : cut].reshape(parts * own_ff)
    out_bias_grad = both[:, cut : cut + own].reshape(width)
    head_maxima = both[:, cut + own :].reshape(heads)

    limits = clip_limit.astype(F32)
    factor = limits / jnp.maximum(head_maxima, limits)
    column_scale = jnp.tile(jnp.repeat(jnp.sqrt(factor), head_dim), 2)
    clipped_weight = qkv_weight[:, : 2 * width].astype(F32) * column_scale
    clipped_bias = qkv_bias[: 2 * width] * column_scale
    return (
        layer_out.reshape(seqs, stretch, width),
        tokens_grad.reshape(seqs, stretch, width),
        norm_sums[0],
        norm_sums[1],
        qkv_grad,
        qkv_bias_grad,
        dense_grad,
        out_bias_grad,
        up_grad,
        up_bias_grad,
        down_grad,
        out_bias_grad,
        head_maxima,
        clipped_weight,
        clipped_bias,
    )


def solution(mesh):
    rows = P("dp", "ctx", None)
    weight = P("ctx", None)
    in_specs = (rows, P("dp", "ctx"), P(), P()) + (weight, P()) * 4 + (P(), rows)
    out_specs = (
        (rows, rows, P(), P()) + (weight, P()) * 4 + (P(), weight, P())
    )
    return jax.shard_map(
        per_device, mesh=mesh, in_specs=in_specs, out_specs=out_specs, check_vma=False
    )
```

time: 976 us -> 485 us (0.50)
  waiting for transfers between devices: 472 us -> 191 us
  blocking collectives: 212 us -> 0 us
  matrix products: 128 us -> 68.3 us
  Pallas kernels: 0 us -> 57.4 us
  starting transfers between devices: 12.1 us -> 67.6 us
  local copies, waits for them, and re-layouts: 85 us -> 41.6 us
    psum x2 -> x0, waiting for transfers between devices: 190 us -> none  [the longest x1 121 us: per_device(): lax.psum((gain_part, shift_part, qkv_bias_part, out_bias_grad, up_bias_pa...]
    all_gather x1 -> x0, blocking collectives: 174 us -> none  [per_device(): all_positions = lax.all_gather(positions, 'ctx', axis=1, tiled=True)]
    reduce_scatter x3 -> x2, waiting for transfers between devices: 170 us -> 0.01 us  [sum_branch(): lax.psum_scatter(value.astype(BF16).reshape(seqs, length, width), 'ctx',...]
    ppermute x0 -> x45, waiting for transfers between devices: none -> 92.7 us  [swap(): lax.ppermute(value, axis, [(i, i ^ bit) for i in range(lax.axis_size(axis...]
    all_gather x2 -> x1, waiting for transfers between devices: 82.7 us -> 0.01 us  [per_device(): lax.all_gather(cotangent, 'ctx', axis=1, tiled=True).reshape(count, width)]
    all_to_all x2 -> x4, waiting for transfers between devices: 29.4 us -> 97 us  [exchange(): lax.all_to_all(blocks, 'ctx', split_axis=0, concat_axis=0, tiled=True)]
    pallas_call x0 -> x8, Pallas kernels: none -> 57.4 us  [the longest x6 31.6 us: place(): pl.pallas_call(body, out_shape=out_shape, grid_spec=pltpu.PrefetchScalarG...]
    ppermute x0 -> x45, starting transfers between devices: none -> 49.2 us  [swap(): lax.ppermute(value, axis, [(i, i ^ bit) for i in range(lax.axis_size(axis...]
  transfers between devices with their start and end apart: 10 -> 53, of which waited for: 7 -> 20; matrix products, arithmetic and copies ran while one was open for 12% -> 23% of each run, Pallas kernels for 0% -> 12%
where the time goes in v2:
time: 485 us; the launch traced here: 480 us
  waiting for transfers between devices  191 us (39%)
  matrix products  68.3 us (14%)
  starting transfers between devices  67.6 us (14%)
  Pallas kernels  57.4 us (12%)
  local copies, waits for them, and re-layouts  41.6 us (9%)
  other arithmetic  39.6 us (8%)
  between operations  14.9 us (3%)
    all_to_all x4, waiting for transfers between devices, exchange(): lax.all_to_all(blocks, 'ctx', split_axis=0, concat_axis=0, tiled=True)  97 us
    ppermute x45, waiting for transfers between devices, swap(): lax.ppermute(value, axis, [(i, i ^ bit) for i in range(lax.axis_size(axis...  92.7 us
    dot_general x10, matrix products, dot(): lax.dot_general(left, right, ((contract[:1], contract[1:]), ((), ())), pr...  68.3 us
    ppermute x45, starting transfers between devices, swap(): lax.ppermute(value, axis, [(i, i ^ bit) for i in range(lax.axis_size(axis...  49.2 us
    pallas_call x6, Pallas kernels, place(): pl.pallas_call(body, out_shape=out_shape, grid_spec=pltpu.PrefetchScalarG...  31.6 us
    all_to_all x4, starting transfers between devices, exchange(): lax.all_to_all(blocks, 'ctx', split_axis=0, concat_axis=0, tiled=True)  17.7 us
    unnamed x90, local copies, waits for them, and re-layouts  16.5 us
    pallas_call x1, Pallas kernels, attend_back(): pl.pallas_call(partial(attend_back_kernel, heads, scale), name='attend_ba...  15 us
  transfers between devices with their start and end apart: 53, of which 20 were waited for; matrix products, arithmetic and copies ran while one was open for 23% of the time, Pallas kernels for 12%

profile of v2, /device:TPU:0, one launch (start us, length us, event | category | flops | bytes accessed | tf_op | source)
XLA Modules:
  0.0 480.0 jit_solution(3083388752125872103)
XLA Ops:
  10.3 2.3 fusion.42
  16.1 6.3 %all-to-all-start = ((bf16[8,64,768]{2,1,0:T(8,128)(2,1)}), bf16[8,64,768]{2,1,0:T(8,128)(2,1)S(1)}, u32[]{:S(2)}, u32[]{:S(2)}) async-start(bf16[8,64,768]{2,1,0:T(8,128)(2,1)} %reshape.493), calls=%async_computation | async-start | bytes 1572864 | tf_op jit(solution)/shard_map/all_to_all | solution.py:506
  27.0 37.7 %all-to-all-done.refs_0_ = bf16[8,64,768]{2,1,0:T(8,128)(2,1)S(1)} async-done(((bf16[8,64,768]{2,1,0:T(8,128)(2,1)}), bf16[8,64,768]{2,1,0:T(8,128)(2,1)S(1)}, u32[]{:S(2)}, u32[]{:S(2)}) %all-to-all-start) | async-done | bytes 786464 | tf_op jit(solution)/shard_map/all_to_all | solution.py:506
  64.7 3.6 all-to-all-start.1
  71.9 16.8 %collective-permute-done.1.refs_2_ = bf16[8,64,768]{2,1,0:T(8,128)(2,1)S(1)} collective-permute-done((bf16[8,64,768]{2,1,0:T(8,128)(2,1)S(1)}, bf16[8,64,768]{2,1,0:T(8,128)(2,1)S(1)}, u32[]{:S(2)}, u32[]{:S(2)}) %collective-permute-start.1) | collective-permute-done | bytes 786464 | tf_op jit(solution)/shard_map/ppermute | solution.py:27
  90.1 9.7 %all-to-all-done.1.refs_0_ = bf16[8,64,1024]{2,1,0:T(8,128)(2,1)S(1)} async-done(((bf16[8,64,1024]{2,1,0:T(8,128)(2,1)}), bf16[8,64,1024]{2,1,0:T(8,128)(2,1)S(1)}, u32[]{:S(2)}, u32[]{:S(2)}) %all-to-all-start.1) | async-done | bytes 1048608 | tf_op jit(solution)/shard_map/all_to_all | solution.py:506
  103.9 1.8 slice.69
  107.5 3.6 collective-permute-done.7
  111.2 23.6 %collective-permute-done.2 = bf16[8,32,768]{2,1,0:T(8,128)(2,1)} collective-permute-done((bf16[8,32,768]{2,1,0:T(8,128)(2,1)}, bf16[8,32,768]{2,1,0:T(8,128)(2,1)}, u32[]{:S(2)}, u32[]{:S(2)}) %collective-permute-start.2) | collective-permute-done | bytes 393248 | tf_op jit(solution)/shard_map/ppermute | solution.py:27
  137.9 3.1 fusion.50
  142.2 3.9 shard_map.253
  150.0 4.0 shard_map.254
  154.0 2.0 copy-done
  156.0 6.3 %fusion.18.joined = f32[1024,768]{1,0:T(8,128)S(1)} fusion(bf16[2048,768]{1,0:T(8,128)(2,1)} %copy-done.3, bf16[1,1024,2048]{2,1,0:T(8,128)(2,1)} %all-gather.5.cloned.1.call-done), kind=kOutput, calls=%fused_computation.22 | convolution fusion | flops 3221225472 | bytes 10485760 | tf_op jit(solution)/shard_map/dot_general | solution.py:21
  162.3 10.9 %attend.1 = (bf16[1024,256]{1,0:T(8,128)(2,1)S(1)}, bf16[1024,256]{1,0:T(8,128)(2,1)S(1)}, bf16[1024,256]{1,0:T(8,128)(2,1)S(1)}, f32[1024,256]{1,0:T(8,128)S(1)...) custom-call(f32[1024,768]{1,0:T(8,128)S(1)} %fusion.18.joined, ...), custom_call_target="tpu_custom_call" | custom-call | flops 2147483648 | bytes 6815744 | tf_op jit(solution)/shard_map/attend/pallas_call | solution.py:352
  176.4 7.2 %multiply_convert_fusion = (bf16[1024,1024]{1,0:T(8,128)(2,1)}, f32[1024,1024]{1,0:T(8,128)}) fusion(f32[1024]{0:T(1024)S(1)} %dynamic_slice.98, bf16[2048,1024]{1,0:T(8,128)(2,1)S(1)} %copy-done.1, bf16[1,1024,2048]{2,1,0:T(8,128)(2,1)S(1)} %copy-done.35), kind=kOutput, calls=%fused_computation.27 | convolution fusion | flops 4305453056 | bytes 14684160 | tf_op jit(solution)/shard_map/dot_general | solution.py:21
  183.6 1.9 constant_dynamic-update-slice_fusion
  186.4 5.8 %convolution_convert_fusion = bf16[1280,2048]{1,0:T(8,128)(2,1)S(1)} fusion(bf16[1024,1280]{1,0:T(8,128)(2,1)S(1)} %constant_dynamic-update-slice_fusion, bf16[1024,2048]{1,0:T(8,128)(2,1)S(1)} %bitcast.135), kind=kOutput, calls=%fused_computation.1 | convolution fusion | flops 5371330560 | bytes 12058624 | tf_op jit(solution)/shard_map/dot_general | solution.py:21
  193.7 10.1 %convert_reduce_fusion = (f32[1024]{0:T(1024)S(1)}, bf16[1024,1024]{1,0:T(8,128)(2,1)S(1)}) fusion(f32[1024,1024]{1,0:T(8,128)} %get-tuple-element.131, f32[1024]{0:T(1024)S(1)} %dynamic_slice.98, bf16[1024,2048]{1,0:T(8,128)(2,1)S(1)} %bitcast.136, bf16[1024,2048]{1,0:T(8,128)(2,1)} %param.24), kind=kOutput, calls=%fused_computation.25 | convolution fusion | flops 4319083520 | bytes 14688256 | tf_op jit(solution)/shard_map/dot_general | solution.py:21
  203.9 7.8 %fusion.22 = bf16[2048,1024]{1,0:T(8,128)(2,1)S(1)} fusion(bf16[1024,1024]{1,0:T(8,128)(2,1)S(1)} %get-tuple-element.105, bf16[1,1024,2048]{2,1,0:T(8,128)(2,1)} %all-gather.5.cloned.1.call-done), kind=kOutput, calls=%fused_computation.28 | convolution fusion | flops 4297064448 | bytes 10485760 | tf_op jit(solution)/shard_map/dot_general | solution.py:21
  216.4 15.0 %attend_back.1 = (bf16[1024,768]{1,0:T(8,128)(2,1)S(1)}, f32[1,768]{1,0:T(1,128)S(1)}) custom-call(bf16[1024,256]{1,0:T(8,128)(2,1)S(1)} %copy-done.10, bf16[1024,256]{1,0:T(8,128)(2,1)S(1)} %copy-done.12, bf16[1024,256]{1,0:T(8,128)(2,1)S(1)} %copy-done.14, bf16[1024,256]{1,0:T(8,128)(2,1)S(1)} %copy-done.12, ...), custom_call_target="tpu_custom_call" | custom-call | flops 5368709120 | bytes 5242880 | tf_op jit(solution)/shard_map/attend_back/pallas_call | solution.py:464
  231.4 5.9 %fusion.25 = bf16[2048,768]{1,0:T(8,128)(2,1)S(1)} fusion(bf16[1024,768]{1,0:T(8,128)(2,1)S(1)} %get-tuple-element.84, bf16[1,1024,2048]{2,1,0:T(8,128)(2,1)} %all-gather.5.cloned.1.call-done), kind=kOutput, calls=%fused_computation.29 | convolution fusion | flops 3222798336 | bytes 8912896 | tf_op jit(solution)/shard_map/dot_general | solution.py:21
  238.6 1.9 copy-done.38
  240.5 6.8 %fusion.65 = f32[1024,2048]{1,0:T(8,128)} fusion(bf16[1024,1024]{1,0:T(8,128)(2,1)S(1)} %copy-done.38, bf16[2048,1024]{1,0:T(8,128)(2,1)S(1)} %copy-done.2), kind=kOutput, calls=%fused_computation.156 | convolution fusion | flops 4294967296 | bytes 14680064 | tf_op jit(solution)/shard_map/dot_general | solution.py:21
  250.2 2.3 add_convert_fusion.3
  255.2 7.2 %fusion.11 = bf16[1,1024,2048]{2,1,0:T(8,128)(2,1)} fusion(f32[1024,2048]{1,0:T(8,128)} %fusion.65, bf16[1024,768]{1,0:T(8,128)(2,1)S(1)} %get-tuple-element.84, bf16[2048,768]{1,0:T(8,128)(2,1)S(1)} %copy-done.4), kind=kOutput, calls=%fused_computation.15 | convolution fusion | flops 3225419776 | bytes 17301504 | tf_op jit(solution)/shard_map/dot_general | solution.py:21
  267.9 9.9 %convert_bitcast_fusion = bf16[1,1024,2048]{2,1,0:T(8,128)(2,1)} fusion(bf16[1024,1280]{1,0:T(8,128)(2,1)} %copy-done.22, bf16[1024,2048]{1,0:T(8,128)(2,1)} %param.24, bf16[256,2048]{1,0:T(8,128)(2,1)} %param.20), kind=kOutput, calls=%fused_computation.26 | convolution fusion | flops 5381292032 | bytes 12058624 | tf_op jit(solution)/shard_map/dot_general | solution.py:21
  277.7 5.5 %collective-permute-done.21 = bf16[8,64,768]{2,1,0:T(8,128)(2,1)S(1)} collective-permute-done((bf16[8,64,768]{2,1,0:T(8,128)(2,1)}, bf16[8,64,768]{2,1,0:T(8,128)(2,1)S(1)}, u32[]{:S(2)}, u32[]{:S(2)}) %collective-permute-start.21) | collective-permute-done | bytes 786464 | tf_op jit(solution)/shard_map/ppermute | solution.py:27
  284.1 2.3 add_convert_fusion.6
  288.1 5.4 %collective-permute-done.26 = bf16[1280,256]{1,0:T(8,128)(2,1)} collective-permute-done((bf16[1280,256]{1,0:T(8,128)(2,1)}, bf16[1280,256]{1,0:T(8,128)(2,1)}, u32[]{:S(2)}, u32[]{:S(2)}) %collective-permute-start.26) | collective-permute-done | bytes 655392 | tf_op jit(solution)/shard_map/ppermute | solution.py:27
  303.8 9.2 %collective-permute-done.24 = bf16[8,32,1024]{2,1,0:T(8,128)(2,1)} collective-permute-done((bf16[8,32,1024]{2,1,0:T(8,128)(2,1)}, bf16[8,32,1024]{2,1,0:T(8,128)(2,1)}, u32[]{:S(2)}, u32[]{:S(2)}) %collective-permute-start.24) | collective-permute-done | bytes 524320 | tf_op jit(solution)/shard_map/ppermute | solution.py:27
  318.2 2.3 collective-permute-done.35
  321.6 4.2 all-to-all-start.2
  328.5 4.1 convert_multiply_fusion
  332.6 37.3 %all-to-all-done.2.refs_0_ = bf16[8,64,1024]{2,1,0:T(8,128)(2,1)} async-done(((bf16[8,64,1024]{2,1,0:T(8,128)(2,1)}), bf16[8,64,1024]{2,1,0:T(8,128)(2,1)}, u32[]{:S(2)}, u32[]{:S(2)}) %all-to-all-start.2) | async-done | bytes 1048608 | tf_op jit(solution)/shard_map/all_to_all | solution.py:506
  373.2 3.5 all-to-all-start.3
  378.9 1.7 fusion.33
  381.1 3.4 convert_reduce_fusion.2
  388.7 12.3 %all-to-all-done.3.refs_0_ = bf16[8,64,768]{2,1,0:T(8,128)(2,1)S(1)} async-done(((bf16[8,64,768]{2,1,0:T(8,128)(2,1)}), bf16[8,64,768]{2,1,0:T(8,128)(2,1)S(1)}, u32[]{:S(2)}, u32[]{:S(2)}) %all-to-all-start.3) | async-done | bytes 786464 | tf_op jit(solution)/shard_map/all_to_all | solution.py:506
  402.0 2.3 collective-permute-done.15
  408.7 9.7 %collective-permute-done.39 = bf16[1280,256]{1,0:T(8,128)(2,1)} collective-permute-done((bf16[1280,256]{1,0:T(8,128)(2,1)}, bf16[1280,256]{1,0:T(8,128)(2,1)}, u32[]{:S(2)}, u32[]{:S(2)}) %collective-permute-start.39) | collective-permute-done | bytes 655392 | tf_op jit(solution)/shard_map/ppermute | solution.py:27
  425.9 9.3 %collective-permute-done.28.refs_1_ = bf16[8,64,768]{2,1,0:T(8,128)(2,1)S(1)} collective-permute-done((bf16[8,64,768]{2,1,0:T(8,128)(2,1)S(1)}, bf16[8,64,768]{2,1,0:T(8,128)(2,1)S(1)}, u32[]{:S(2)}, u32[]{:S(2)}) %collective-permute-start.28) | collective-permute-done | bytes 786464 | tf_op jit(solution)/shard_map/ppermute | solution.py:27
  438.5 2.4 shard_map.256
  440.9 5.0 %shard_map.258 = f32[1024,2048]{1,0:T(8,128)} custom-call(s32[1]{0:T(128)} %bitcast.3.index_ref, bf16[1280,512]{1,0:T(8,128)(2,1)S(1)} %pad_maximum_fusion.refs_0_, bf16[1280,512]{1,0:T(8,128)(2,1)} %collective-permute-done.37.refs_1_, bf16[1280,512]{1,0:T(8,128)(2,1)S(1)} %collective-permute-done.38.refs_2_, ...), custom_call_target="tpu_custom_call" | custom-call | bytes 13631488 | tf_op jit(solution)/shard_map/pallas_call | solution.py:163
  446.0 5.9 %collective-permute-start.18 = (f32[2,2048]{1,0:T(2,128)S(1)}, f32[2,2048]{1,0:T(2,128)S(1)}, u32[]{:S(2)}, u32[]{:S(2)}) collective-permute-start(f32[2,2048]{1,0:T(2,128)S(1)} %add.283), channel_id=1, source_target_pairs={{0,2},{1,3},{2,0},{3,1},{4,6},{5,7},{6,4},{7,5},{8,10},{9,11},{10,... | collective-permute-start | bytes 49160 | tf_op jit(solution)/shard_map/ppermute | solution.py:27
  451.9 7.2 %shard_map.257 = f32[256,8192]{1,0:T(8,128)} custom-call(s32[1]{0:T(128)} %bitcast.3.index_ref, bf16[8,64,1024]{2,1,0:T(8,128)(2,1)} %all-to-all-done.2.refs_0_, bf16[8,64,1024]{2,1,0:T(8,128)(2,1)} %collective-permute-done.41.refs_1_, bf16[8,64,1024]{2,1,0:T(8,128)(2,1)} %collective-permute-done.42.refs_2_, bf16[8,64,1024]{2,1,0:T(8,128)(2,1)S(1)} %pad_maximum_fusion.4.refs_3_), custom_call_target="tpu_custom_call" | custom-call | bytes 12582912 | tf_op jit(solution)/shard_map/pallas_call | solution.py:163
  459.1 3.7 collective-permute-start.19
  462.9 9.1 %shard_map.255 = f32[256,6144]{1,0:T(8,128)} custom-call(s32[1]{0:T(128)} %bitcast.3.index_ref, bf16[8,64,768]{2,1,0:T(8,128)(2,1)S(1)} %all-to-all-done.3.refs_0_, bf16[8,64,768]{2,1,0:T(8,128)(2,1)S(1)} %collective-permute-done.28.refs_1_, bf16[8,64,768]{2,1,0:T(8,128)(2,1)S(1)} %collective-permute-done.29.refs_2_, ...), custom_call_target="tpu_custom_call" | custom-call | bytes 9437184 | tf_op jit(solution)/shard_map/pallas_call | solution.py:163
  (264 shorter events, 101.9 us)
Async XLA Ops:
  7.2 148.8 %all-gather.5.cloned.1.call-start = ((), (), s32[]{:S(2)}) async-start(), calls=%async_computation.7 | async-start | bytes 4718592 | tf_op jit(solution)/shard_map/all_gather | solution.py:578
  16.1 48.6 %all-to-all-start = ((bf16[8,64,768]{2,1,0:T(8,128)(2,1)}), bf16[8,64,768]{2,1,0:T(8,128)(2,1)S(1)}, u32[]{:S(2)}, u32[]{:S(2)}) async-start(bf16[8,64,768]{2,1,0:T(8,128)(2,1)} %reshape.493), calls=%async_computation | async-start | bytes 1572864 | tf_op jit(solution)/shard_map/all_to_all | solution.py:506
  22.4 161.2 %all-gather.3.cloned.1.call-start = ((), (), s32[]{:S(2)}) async-start(), calls=%async_computation.6 | async-start | bytes 4718592 | tf_op jit(solution)/shard_map/all_gather | solution.py:581
  64.7 35.1 %all-to-all-start.1 = ((bf16[8,64,1024]{2,1,0:T(8,128)(2,1)}), bf16[8,64,1024]{2,1,0:T(8,128)(2,1)S(1)}, u32[]{:S(2)}, u32[]{:S(2)}) async-start(bf16[8,64,1024]{2,1,0:T(8,128)(2,1)} %bitcast.110), calls=%async_computation.1 | async-start | bytes 2097152 | tf_op jit(solution)/shard_map/all_to_all | solution.py:506
  68.3 310.7 %reduce-scatter.5.cloned.1.call-start = ((), (), s32[]{:S(2)}) async-start(), calls=%async_computation.9 | async-start | bytes 4718592 | tf_op jit(solution)/shard_map/reduce_scatter | solution.py:622
  68.8 19.9 %collective-permute-start.1 = (bf16[8,64,768]{2,1,0:T(8,128)(2,1)S(1)}, bf16[8,64,768]{2,1,0:T(8,128)(2,1)S(1)}, u32[]{:S(2)}, u32[]{:S(2)}) collective-permute-start(bf16[8,64,768]{2,1,0:T(8,128)(2,1)S(1)} %all-to-all-done.refs_0_), channel_id=1, source_target_pairs={{0,16},{8,24},{16,0},{24,8},{1,17},{9,25},{17,1},{25,9},{2,18},{10... | collective-permute-start | bytes 2359304 | tf_op jit(solution)/shard_map/ppermute | solution.py:27
  70.4 19.6 %collective-permute-start = (bf16[8,64,768]{2,1,0:T(8,128)(2,1)S(1)}, bf16[8,64,768]{2,1,0:T(8,128)(2,1)}, u32[]{:S(2)}, u32[]{:S(2)}) collective-permute-start(bf16[8,64,768]{2,1,0:T(8,128)(2,1)S(1)} %all-to-all-done.refs_0_), channel_id=1, source_target_pairs={{0,8},{8,0},{16,24},{24,16},{1,9},{9,1},{17,25},{25,17},{2,10},{10... | collective-permute-start | bytes 2359304 | tf_op jit(solution)/shard_map/ppermute | solution.py:27
  99.8 35.0 %collective-permute-start.5 = (bf16[8,64,1024]{2,1,0:T(8,128)(2,1)S(1)}, bf16[8,64,1024]{2,1,0:T(8,128)(2,1)S(1)}, u32[]{:S(2)}, u32[]{:S(2)}) collective-permute-start(bf16[8,64,1024]{2,1,0:T(8,128)(2,1)S(1)} %all-to-all-done.1.refs_0_), channel_id=1, source_target_pairs={{0,16},{8,24},{16,0},{24,8},{1,17},{9,25},{17,1},{25,9},{2,18},{10... | collective-permute-start | bytes 3145736 | tf_op jit(solution)/shard_map/ppermute | solution.py:27
  101.3 33.4 %collective-permute-start.4 = (bf16[8,64,1024]{2,1,0:T(8,128)(2,1)S(1)}, bf16[8,64,1024]{2,1,0:T(8,128)(2,1)}, u32[]{:S(2)}, u32[]{:S(2)}) collective-permute-start(bf16[8,64,1024]{2,1,0:T(8,128)(2,1)S(1)} %all-to-all-done.1.refs_0_), channel_id=1, source_target_pairs={{0,8},{8,0},{16,24},{24,16},{1,9},{9,1},{17,25},{25,17},{2,10},{10... | collective-permute-start | bytes 3145736 | tf_op jit(solution)/shard_map/ppermute | solution.py:27
  105.6 29.1 %collective-permute-start.2 = (bf16[8,32,768]{2,1,0:T(8,128)(2,1)}, bf16[8,32,768]{2,1,0:T(8,128)(2,1)}, u32[]{:S(2)}, u32[]{:S(2)}) collective-permute-start(bf16[8,32,768]{2,1,0:T(8,128)(2,1)} %slice.69), channel_id=1, source_target_pairs={{0,8},{8,0},{16,24},{24,16},{1,9},{9,1},{17,25},{25,17},{2,10},{10... | collective-permute-start | bytes 1179656 | tf_op jit(solution)/shard_map/ppermute | solution.py:27
  106.2 28.5 %collective-permute-start.3 = (bf16[8,32,768]{2,1,0:T(8,128)(2,1)S(1)}, bf16[8,32,768]{2,1,0:T(8,128)(2,1)}, u32[]{:S(2)}, u32[]{:S(2)}) collective-permute-start(bf16[8,32,768]{2,1,0:T(8,128)(2,1)S(1)} %slice.70), channel_id=1, source_target_pairs={{0,16},{8,24},{16,0},{24,8},{1,17},{9,25},{17,1},{25,9},{2,18},{10... | collective-permute-start | bytes 1179656 | tf_op jit(solution)/shard_map/ppermute | solution.py:27
  111.1 26.8 %collective-permute-start.8 = (s32[512,1]{0,1:T(1,128)S(1)}, s32[512,1]{0,1:T(1,128)S(1)}, u32[]{:S(2)}, u32[]{:S(2)}) collective-permute-start(s32[512,1]{0,1:T(1,128)S(1)} %broadcast_select_fusion), channel_id=1, source_target_pairs={{0,4},{1,5},{2,6},{3,7},{4,0},{5,1},{6,2},{7,3},{8,12},{9,13},{10,... | collective-permute-start | bytes 6152 | tf_op jit(solution)/shard_map/ppermute | solution.py:27
  135.9 12.8 %collective-permute-start.9 = (bf16[8,32,1024]{2,1,0:T(8,128)(2,1)S(1)}, bf16[8,32,1024]{2,1,0:T(8,128)(2,1)S(1)}, u32[]{:S(2)}, u32[]{:S(2)}) collective-permute-start(bf16[8,32,1024]{2,1,0:T(8,128)(2,1)S(1)} %slice.71), channel_id=1, source_target_pairs={{0,8},{8,0},{16,24},{24,16},{1,9},{9,1},{17,25},{25,17},{2,10},{10... | collective-permute-start | bytes 1572872 | tf_op jit(solution)/shard_map/ppermute | solution.py:27
  137.4 12.5 %collective-permute-start.10 = (bf16[8,32,1024]{2,1,0:T(8,128)(2,1)S(1)}, bf16[8,32,1024]{2,1,0:T(8,128)(2,1)S(1)}, u32[]{:S(2)}, u32[]{:S(2)}) collective-permute-start(bf16[8,32,1024]{2,1,0:T(8,128)(2,1)S(1)} %slice.72), channel_id=1, source_target_pairs={{0,16},{8,24},{16,0},{24,8},{1,17},{9,25},{17,1},{25,9},{2,18},{10... | collective-permute-start | bytes 1572872 | tf_op jit(solution)/shard_map/ppermute | solution.py:27
  192.6 54.7 %collective-permute-start.12 = (bf16[1280,512]{1,0:T(8,128)(2,1)S(1)}, bf16[1280,512]{1,0:T(8,128)(2,1)S(1)}, u32[]{:S(2)}, u32[]{:S(2)}) collective-permute-start(bf16[1280,512]{1,0:T(8,128)(2,1)S(1)} %get-tuple-element.108), channel_id=1, source_target_pairs={{0,16},{8,24},{16,0},{24,8},{1,17},{9,25},{17,1},{25,9},{2,18},{10... | collective-permute-start | bytes 3932168 | tf_op jit(solution)/shard_map/ppermute | solution.py:27
  193.2 54.1 %collective-permute-start.11 = (bf16[1280,512]{1,0:T(8,128)(2,1)S(1)}, bf16[1280,512]{1,0:T(8,128)(2,1)S(1)}, u32[]{:S(2)}, u32[]{:S(2)}) collective-permute-start(bf16[1280,512]{1,0:T(8,128)(2,1)S(1)} %get-tuple-element.109), channel_id=1, source_target_pairs={{0,8},{8,0},{16,24},{24,16},{1,9},{9,1},{17,25},{25,17},{2,10},{10... | collective-permute-start | bytes 3932168 | tf_op jit(solution)/shard_map/ppermute | solution.py:27
  212.0 38.2 %collective-permute-start.14 = (bf16[8,64,1024]{2,1,0:T(8,128)(2,1)S(1)}, bf16[8,64,1024]{2,1,0:T(8,128)(2,1)S(1)}, u32[]{:S(2)}, u32[]{:S(2)}) collective-permute-start(bf16[8,64,1024]{2,1,0:T(8,128)(2,1)S(1)} %get-tuple-element.112), channel_id=1, source_target_pairs={{0,16},{8,24},{16,0},{24,8},{1,17},{9,25},{17,1},{25,9},{2,18},{10... | collective-permute-start | bytes 3145736 | tf_op jit(solution)/shard_map/ppermute | solution.py:27
  213.5 36.7 %collective-permute-start.13 = (bf16[8,64,1024]{2,1,0:T(8,128)(2,1)S(1)}, bf16[8,64,1024]{2,1,0:T(8,128)(2,1)}, u32[]{:S(2)}, u32[]{:S(2)}) collective-permute-start(bf16[8,64,1024]{2,1,0:T(8,128)(2,1)S(1)} %get-tuple-element.113), channel_id=1, source_target_pairs={{0,8},{8,0},{16,24},{24,16},{1,9},{9,1},{17,25},{25,17},{2,10},{10... | collective-permute-start | bytes 3145736 | tf_op jit(solution)/shard_map/ppermute | solution.py:27
  262.4 118.8 %reduce-scatter.3.cloned.1.call-start = ((), (), s32[]{:S(2)}) async-start(), calls=%async_computation.8 | async-start | bytes 4718592 | tf_op jit(solution)/shard_map/reduce_scatter | solution.py:622
  262.4 20.8 %collective-permute-start.21 = (bf16[8,64,768]{2,1,0:T(8,128)(2,1)}, bf16[8,64,768]{2,1,0:T(8,128)(2,1)S(1)}, u32[]{:S(2)}, u32[]{:S(2)}) collective-permute-start(bf16[8,64,768]{2,1,0:T(8,128)(2,1)} %get-tuple-element.118), channel_id=1, source_target_pairs={{0,16},{8,24},{16,0},{24,8},{1,17},{9,25},{17,1},{25,9},{2,18},{10... | collective-permute-start | bytes 2359304 | tf_op jit(solution)/shard_map/ppermute | solution.py:27
  263.1 20.8 %collective-permute-start.20 = (bf16[8,64,768]{2,1,0:T(8,128)(2,1)}, bf16[8,64,768]{2,1,0:T(8,128)(2,1)}, u32[]{:S(2)}, u32[]{:S(2)}) collective-permute-start(bf16[8,64,768]{2,1,0:T(8,128)(2,1)} %get-tuple-element.119), channel_id=1, source_target_pairs={{0,8},{8,0},{16,24},{24,16},{1,9},{9,1},{17,25},{25,17},{2,10},{10... | collective-permute-start | bytes 2359304 | tf_op jit(solution)/shard_map/ppermute | solution.py:27
  265.6 27.9 %collective-permute-start.26 = (bf16[1280,256]{1,0:T(8,128)(2,1)}, bf16[1280,256]{1,0:T(8,128)(2,1)}, u32[]{:S(2)}, u32[]{:S(2)}) collective-permute-start(bf16[1280,256]{1,0:T(8,128)(2,1)} %constant_dynamic-slice_fusion.5), channel_id=1, source_target_pairs={{0,8},{8,0},{16,24},{24,16},{1,9},{9,1},{17,25},{25,17},{2,10},{10... | collective-permute-start | bytes 1966088 | tf_op jit(solution)/shard_map/ppermute | solution.py:27
  266.4 27.1 %collective-permute-start.27 = (bf16[1280,256]{1,0:T(8,128)(2,1)}, bf16[1280,256]{1,0:T(8,128)(2,1)}, u32[]{:S(2)}, u32[]{:S(2)}) collective-permute-start(bf16[1280,256]{1,0:T(8,128)(2,1)} %constant_dynamic-slice_fusion.4), channel_id=1, source_target_pairs={{0,16},{8,24},{16,0},{24,8},{1,17},{9,25},{17,1},{25,9},{2,18},{10... | collective-permute-start | bytes 1966088 | tf_op jit(solution)/shard_map/ppermute | solution.py:27
  297.8 15.2 %collective-permute-start.24 = (bf16[8,32,1024]{2,1,0:T(8,128)(2,1)}, bf16[8,32,1024]{2,1,0:T(8,128)(2,1)}, u32[]{:S(2)}, u32[]{:S(2)}) collective-permute-start(bf16[8,32,1024]{2,1,0:T(8,128)(2,1)} %constant_dynamic-slice_fusion.3), channel_id=1, source_target_pairs={{0,8},{8,0},{16,24},{24,16},{1,9},{9,1},{17,25},{25,17},{2,10},{10... | collective-permute-start | bytes 1572872 | tf_op jit(solution)/shard_map/ppermute | solution.py:27
  298.3 15.3 %collective-permute-start.25 = (bf16[8,32,1024]{2,1,0:T(8,128)(2,1)}, bf16[8,32,1024]{2,1,0:T(8,128)(2,1)}, u32[]{:S(2)}, u32[]{:S(2)}) collective-permute-start(bf16[8,32,1024]{2,1,0:T(8,128)(2,1)} %constant_dynamic-slice_fusion.2), channel_id=1, source_target_pairs={{0,16},{8,24},{16,0},{24,8},{1,17},{9,25},{17,1},{25,9},{2,18},{10... | collective-permute-start | bytes 1572872 | tf_op jit(solution)/shard_map/ppermute | solution.py:27
  300.1 14.9 %collective-permute-start.33 = (f32[1,2052]{1,0:T(1,128)S(1)}, f32[1,2052]{1,0:T(1,128)S(1)}, u32[]{:S(2)}, u32[]{:S(2)}) collective-permute-start(f32[1,2052]{1,0:T(1,128)S(1)} %pad_maximum_fusion.11), channel_id=1, source_target_pairs={{0,16},{8,24},{16,0},{24,8},{1,17},{9,25},{17,1},{25,9},{2,18},{10... | collective-permute-start | bytes 24632 | tf_op jit(solution)/shard_map/ppermute | solution.py:27
  301.3 31.3 %collective-permute-start.22 = (bf16[8,32,768]{2,1,0:T(8,128)(2,1)}, bf16[8,32,768]{2,1,0:T(8,128)(2,1)}, u32[]{:S(2)}, u32[]{:S(2)}) collective-permute-start(bf16[8,32,768]{2,1,0:T(8,128)(2,1)} %constant_dynamic-slice_fusion.1), channel_id=1, source_target_pairs={{0,8},{8,0},{16,24},{24,16},{1,9},{9,1},{17,25},{25,17},{2,10},{10... | collective-permute-start | bytes 1179656 | tf_op jit(solution)/shard_map/ppermute | solution.py:27
  302.4 30.3 %collective-permute-start.23 = (bf16[8,32,768]{2,1,0:T(8,128)(2,1)}, bf16[8,32,768]{2,1,0:T(8,128)(2,1)}, u32[]{:S(2)}, u32[]{:S(2)}) collective-permute-start(bf16[8,32,768]{2,1,0:T(8,128)(2,1)} %constant_dynamic-slice_fusion), channel_id=1, source_target_pairs={{0,16},{8,24},{16,0},{24,8},{1,17},{9,25},{17,1},{25,9},{2,18},{10... | collective-permute-start | bytes 1179656 | tf_op jit(solution)/shard_map/ppermute | solution.py:27
  313.0 73.9 %collective-permute-start.38 = (bf16[1280,512]{1,0:T(8,128)(2,1)S(1)}, bf16[1280,512]{1,0:T(8,128)(2,1)S(1)}, u32[]{:S(2)}, u32[]{:S(2)}) collective-permute-start(bf16[1280,512]{1,0:T(8,128)(2,1)S(1)} %pad_maximum_fusion.refs_0_), channel_id=1, source_target_pairs={{0,16},{8,24},{16,0},{24,8},{1,17},{9,25},{17,1},{25,9},{2,18},{10... | collective-permute-start | bytes 3932168 | tf_op jit(solution)/shard_map/ppermute | solution.py:27
  313.6 73.2 %collective-permute-start.37 = (bf16[1280,512]{1,0:T(8,128)(2,1)S(1)}, bf16[1280,512]{1,0:T(8,128)(2,1)}, u32[]{:S(2)}, u32[]{:S(2)}) collective-permute-start(bf16[1280,512]{1,0:T(8,128)(2,1)S(1)} %pad_maximum_fusion.refs_0_), channel_id=1, source_target_pairs={{0,8},{8,0},{16,24},{24,16},{1,9},{9,1},{17,25},{25,17},{2,10},{10... | collective-permute-start | bytes 3932168 | tf_op jit(solution)/shard_map/ppermute | solution.py:27
  320.5 6.5 %collective-permute-start.36 = (f32[4,2052]{1,0:T(4,128)S(1)}, f32[4,2052]{1,0:T(4,128)S(1)}, u32[]{:S(2)}, u32[]{:S(2)}) collective-permute-start(f32[4,2052]{1,0:T(4,128)S(1)} %maximum_select_fusion.1), channel_id=1, source_target_pairs={{0,4},{1,5},{2,6},{3,7},{4,0},{5,1},{6,2},{7,3},{8,12},{9,13},{10,... | collective-permute-start | bytes 98504 | tf_op jit(solution)/shard_map/ppermute | solution.py:27
  321.6 48.3 %all-to-all-start.2 = ((bf16[8,64,1024]{2,1,0:T(8,128)(2,1)}), bf16[8,64,1024]{2,1,0:T(8,128)(2,1)}, u32[]{:S(2)}, u32[]{:S(2)}) async-start(bf16[8,64,1024]{2,1,0:T(8,128)(2,1)} %pad_maximum_fusion.3), calls=%async_computation.4 | async-start | bytes 2097152 | tf_op jit(solution)/shard_map/all_to_all | solution.py:506
  373.2 27.9 %all-to-all-start.3 = ((bf16[8,64,768]{2,1,0:T(8,128)(2,1)}), bf16[8,64,768]{2,1,0:T(8,128)(2,1)S(1)}, u32[]{:S(2)}, u32[]{:S(2)}) async-start(bf16[8,64,768]{2,1,0:T(8,128)(2,1)} %pad_maximum_fusion.7), calls=%async_computation.5 | async-start | bytes 1572864 | tf_op jit(solution)/shard_map/all_to_all | solution.py:506
  376.8 42.8 %collective-permute-start.42 = (bf16[8,64,1024]{2,1,0:T(8,128)(2,1)}, bf16[8,64,1024]{2,1,0:T(8,128)(2,1)}, u32[]{:S(2)}, u32[]{:S(2)}) collective-permute-start(bf16[8,64,1024]{2,1,0:T(8,128)(2,1)} %all-to-all-done.2.refs_0_), channel_id=1, source_target_pairs={{0,16},{8,24},{16,0},{24,8},{1,17},{9,25},{17,1},{25,9},{2,18},{10... | collective-permute-start | bytes 3145736 | tf_op jit(solution)/shard_map/ppermute | solution.py:27
  377.7 43.9 %collective-permute-start.41 = (bf16[8,64,1024]{2,1,0:T(8,128)(2,1)}, bf16[8,64,1024]{2,1,0:T(8,128)(2,1)}, u32[]{:S(2)}, u32[]{:S(2)}) collective-permute-start(bf16[8,64,1024]{2,1,0:T(8,128)(2,1)} %all-to-all-done.2.refs_0_), channel_id=1, source_target_pairs={{0,8},{8,0},{16,24},{24,16},{1,9},{9,1},{17,25},{25,17},{2,10},{10... | collective-permute-start | bytes 3145736 | tf_op jit(solution)/shard_map/ppermute | solution.py:27
  385.2 19.1 %collective-permute-start.15 = (f32[2,2048]{1,0:T(2,128)}, f32[2,2048]{1,0:T(2,128)}, u32[]{:S(2)}, u32[]{:S(2)}) collective-permute-start(f32[2,2048]{1,0:T(2,128)} %pad_maximum_fusion.9), channel_id=1, source_target_pairs={{0,8},{8,0},{16,24},{24,16},{1,9},{9,1},{17,25},{25,17},{2,10},{10... | collective-permute-start | bytes 49160 | tf_op jit(solution)/shard_map/ppermute | solution.py:27
  387.7 30.7 %collective-permute-start.39 = (bf16[1280,256]{1,0:T(8,128)(2,1)}, bf16[1280,256]{1,0:T(8,128)(2,1)}, u32[]{:S(2)}, u32[]{:S(2)}) collective-permute-start(bf16[1280,256]{1,0:T(8,128)(2,1)} %slice.83), channel_id=1, source_target_pairs={{0,8},{8,0},{16,24},{24,16},{1,9},{9,1},{17,25},{25,17},{2,10},{10... | collective-permute-start | bytes 1966088 | tf_op jit(solution)/shard_map/ppermute | solution.py:27
  401.1 23.9 %collective-permute-start.29 = (bf16[8,64,768]{2,1,0:T(8,128)(2,1)S(1)}, bf16[8,64,768]{2,1,0:T(8,128)(2,1)S(1)}, u32[]{:S(2)}, u32[]{:S(2)}) collective-permute-start(bf16[8,64,768]{2,1,0:T(8,128)(2,1)S(1)} %all-to-all-done.3.refs_0_), channel_id=1, source_target_pairs={{0,16},{8,24},{16,0},{24,8},{1,17},{9,25},{17,1},{25,9},{2,18},{10... | collective-permute-start | bytes 2359304 | tf_op jit(solution)/shard_map/ppermute | solution.py:27
  404.3 30.8 %collective-permute-start.28 = (bf16[8,64,768]{2,1,0:T(8,128)(2,1)S(1)}, bf16[8,64,768]{2,1,0:T(8,128)(2,1)S(1)}, u32[]{:S(2)}, u32[]{:S(2)}) collective-permute-start(bf16[8,64,768]{2,1,0:T(8,128)(2,1)S(1)} %all-to-all-done.3.refs_0_), channel_id=1, source_target_pairs={{0,8},{8,0},{16,24},{24,16},{1,9},{9,1},{17,25},{25,17},{2,10},{10... | collective-permute-start | bytes 2359304 | tf_op jit(solution)/shard_map/ppermute | solution.py:27
  418.4 20.0 %collective-permute-start.40 = (bf16[1280,256]{1,0:T(8,128)(2,1)S(1)}, bf16[1280,256]{1,0:T(8,128)(2,1)S(1)}, u32[]{:S(2)}, u32[]{:S(2)}) collective-permute-start(bf16[1280,256]{1,0:T(8,128)(2,1)S(1)} %slice.84), channel_id=1, source_target_pairs={{0,16},{8,24},{16,0},{24,8},{1,17},{9,25},{17,1},{25,9},{2,18},{10... | collective-permute-start | bytes 1966088 | tf_op jit(solution)/shard_map/ppermute | solution.py:27
  419.6 16.8 %collective-permute-start.16 = (f32[2,2048]{1,0:T(2,128)S(1)}, f32[2,2048]{1,0:T(2,128)S(1)}, u32[]{:S(2)}, u32[]{:S(2)}) collective-permute-start(f32[2,2048]{1,0:T(2,128)S(1)} %fusion.62), channel_id=1, source_target_pairs={{0,16},{8,24},{16,0},{24,8},{1,17},{9,25},{17,1},{25,9},{2,18},{10... | collective-permute-start | bytes 49160 | tf_op jit(solution)/shard_map/ppermute | solution.py:27
  423.7 28.1 %collective-permute-start.44 = (bf16[8,32,1024]{2,1,0:T(8,128)(2,1)S(1)}, bf16[8,32,1024]{2,1,0:T(8,128)(2,1)S(1)}, u32[]{:S(2)}, u32[]{:S(2)}) collective-permute-start(bf16[8,32,1024]{2,1,0:T(8,128)(2,1)S(1)} %slice.87), channel_id=1, source_target_pairs={{0,16},{8,24},{16,0},{24,8},{1,17},{9,25},{17,1},{25,9},{2,18},{10... | collective-permute-start | bytes 1572872 | tf_op jit(solution)/shard_map/ppermute | solution.py:27
  425.0 26.8 %collective-permute-start.43 = (bf16[8,32,1024]{2,1,0:T(8,128)(2,1)S(1)}, bf16[8,32,1024]{2,1,0:T(8,128)(2,1)S(1)}, u32[]{:S(2)}, u32[]{:S(2)}) collective-permute-start(bf16[8,32,1024]{2,1,0:T(8,128)(2,1)S(1)} %slice.86), channel_id=1, source_target_pairs={{0,8},{8,0},{16,24},{24,16},{1,9},{9,1},{17,25},{25,17},{2,10},{10... | collective-permute-start | bytes 1572872 | tf_op jit(solution)/shard_map/ppermute | solution.py:27
  435.1 27.6 %collective-permute-start.30 = (bf16[8,32,768]{2,1,0:T(8,128)(2,1)S(1)}, bf16[8,32,768]{2,1,0:T(8,128)(2,1)S(1)}, u32[]{:S(2)}, u32[]{:S(2)}) collective-permute-start(bf16[8,32,768]{2,1,0:T(8,128)(2,1)S(1)} %slice.94), channel_id=1, source_target_pairs={{0,8},{8,0},{16,24},{24,16},{1,9},{9,1},{17,25},{25,17},{2,10},{10... | collective-permute-start | bytes 1179656 | tf_op jit(solution)/shard_map/ppermute | solution.py:27
  436.4 26.4 %collective-permute-start.31 = (bf16[8,32,768]{2,1,0:T(8,128)(2,1)S(1)}, bf16[8,32,768]{2,1,0:T(8,128)(2,1)S(1)}, u32[]{:S(2)}, u32[]{:S(2)}) collective-permute-start(bf16[8,32,768]{2,1,0:T(8,128)(2,1)S(1)} %slice.95), channel_id=1, source_target_pairs={{0,16},{8,24},{16,0},{24,8},{1,17},{9,25},{17,1},{25,9},{2,18},{10... | collective-permute-start | bytes 1179656 | tf_op jit(solution)/shard_map/ppermute | solution.py:27
  438.4 7.6 %collective-permute-start.17 = (f32[2,2048]{1,0:T(2,128)S(1)}, f32[2,2048]{1,0:T(2,128)S(1)}, u32[]{:S(2)}, u32[]{:S(2)}) collective-permute-start(f32[2,2048]{1,0:T(2,128)S(1)} %fusion.81), channel_id=1, source_target_pairs={{0,1},{1,0},{2,3},{3,2},{4,5},{5,4},{6,7},{7,6},{8,9},{9,8},{10,11... | collective-permute-start | bytes 49160 | tf_op jit(solution)/shard_map/ppermute | solution.py:27
  446.0 13.2 %collective-permute-start.18 = (f32[2,2048]{1,0:T(2,128)S(1)}, f32[2,2048]{1,0:T(2,128)S(1)}, u32[]{:S(2)}, u32[]{:S(2)}) collective-permute-start(f32[2,2048]{1,0:T(2,128)S(1)} %add.283), channel_id=1, source_target_pairs={{0,2},{1,3},{2,0},{3,1},{4,6},{5,7},{6,4},{7,5},{8,10},{9,11},{10,... | collective-permute-start | bytes 49160 | tf_op jit(solution)/shard_map/ppermute | solution.py:27
  459.1 12.8 %collective-permute-start.19 = (f32[2,2048]{1,0:T(2,128)S(1)}, f32[2,2048]{1,0:T(2,128)S(1)}, u32[]{:S(2)}, u32[]{:S(2)}) collective-permute-start(f32[2,2048]{1,0:T(2,128)S(1)} %add.284), channel_id=1, source_target_pairs={{0,4},{1,5},{2,6},{3,7},{4,0},{5,1},{6,2},{7,3},{8,12},{9,13},{10,... | collective-permute-start | bytes 49160 | tf_op jit(solution)/shard_map/ppermute | solution.py:27
  (44 other events, 558.8 us)
Sparse Core Ops, SparseCore 0:
  12.7 81.3 all-gather.4
  95.7 45.5 all-gather.2
  262.5 47.5 reduce-scatter.4
  312.9 68.0 reduce-scatter.2

commit v3 on v2

--- a/solution.py
+++ b/solution.py
@@ -15,6 +15,8 @@
 F32 = jnp.float32
 LANES = 128
 HEAD = 64
+VMEM = 40 << 20
+LIGHT = pl.CostEstimate(flops=1, transcendentals=0, bytes_accessed=1)
 
 
 def dot(left, right, contract):
@@ -25,28 +27,6 @@
 
 def swap(value, axis, bit):
     return lax.ppermute(value, axis, [(i, i ^ bit) for i in range(lax.axis_size(axis))])
-
-
-def bits_of(axis):
-    return [1 << i for i in range(lax.axis_size(axis).bit_length() - 1)]
-
-
-def all_sum(value, axes):
-    for axis in axes:
-        for bit in bits_of(axis):
-            value = value + swap(value, axis, bit)
-    return value
-
-
-def all_rows(value, axis):
-    index = lax.axis_index(axis)
-    for bit in bits_of(axis):
-        other = swap(value, axis, bit)
-        upper = (index & bit) != 0
-        value = jnp.where(
-            upper, jnp.concatenate([other, value], 0), jnp.concatenate([value, other], 0)
-        )
-    return value
 
 
 def take(value, start, size, axis):
@@ -90,34 +70,188 @@
     )
 
 
+def dp_index():
+    return lax.axis_index("dp").astype(jnp.int32).reshape(1)
+
+
 def first_sums(value, received, axis):
     index = lax.axis_index("dp")
+    low, high = index & 1, index >> 1
     size = value.shape[axis] // 8
-    return (
-        plus(take(value, (index & 1) * 2 * size, 2 * size, axis), received[0]),
-        plus(take(value, (4 + (index >> 1) * 2) * size, 2 * size, axis), received[1]),
-    )
-
-
-def outgoing_again(sums, axis):
-    index = lax.axis_index("dp")
-    size = sums[0].shape[axis] // 2
-    return (
-        take(sums[1], (1 - (index & 1)) * size, size, axis),
-        take(sums[0], (1 - (index >> 1)) * size, size, axis),
-    )
-
-
-def second_sums(sums, received, axis):
-    index = lax.axis_index("dp")
-    size = sums[0].shape[axis] // 2
-    return jnp.concatenate(
-        [
-            plus(take(sums[0], (index >> 1) * size, size, axis), received[1]),
-            plus(take(sums[1], (index & 1) * size, size, axis), received[0]),
+    first = plus(take(value, low * 2 * size, 2 * size, axis), received[0])
+    second = plus(take(value, (4 + high * 2) * size, 2 * size, axis), received[1])
+    send = (
+        take(second, (1 - low) * size, size, axis),
+        take(first, (1 - high) * size, size, axis),
+    )
+    keep = jnp.concatenate(
+        [take(first, high * size, size, axis), take(second, low * size, size, axis)], axis
+    )
+    return send, keep
+
+
+def second_sums(keep, received, axis):
+    return plus(keep, jnp.concatenate([received[1], received[0]], axis))
+
+
+def normalize_kernel(tokens, gain, shift, hidden, stats):
+    value = tokens[...].astype(F32)
+    mean = jnp.mean(value, axis=1, keepdims=True)
+    centre = value - mean
+    inv_std = lax.rsqrt(jnp.mean(centre * centre, axis=1, keepdims=True) + EPSILON)
+    hidden[...] = (centre * inv_std * gain[...] + shift[...]).astype(BF16)
+    lane = lax.broadcasted_iota(jnp.int32, stats.shape, 1)
+    stats[...] = jnp.where(lane == 0, mean, inv_std)
+
+
+def normalize(tokens, gain, shift):
+    count, width = tokens.shape[0], gain.shape[0]
+    block = 256 if count % 256 == 0 else count
+    row = lambda i: (i, 0)
+    return pl.pallas_call(
+        normalize_kernel,
+        name="normalize",
+        out_shape=[
+            jax.ShapeDtypeStruct((count, width), BF16),
+            jax.ShapeDtypeStruct((count, LANES), F32),
         ],
-        axis,
-    )
+        grid=(count // block,),
+        in_specs=[pl.BlockSpec((block, width), row)]
+        + [pl.BlockSpec((1, width), lambda i: (0, 0))] * 2,
+        out_specs=[pl.BlockSpec((block, width), row), pl.BlockSpec((block, LANES), row)],
+        compiler_params=pltpu.CompilerParams(vmem_limit_bytes=VMEM),
+        cost_estimate=LIGHT,
+    )(tokens, gain[None], shift[None])
+
+
+def output_kernel(attended, dense, activated, down, out):
+    out[...] = (nn(attended[...], dense[...]) + nn(activated[...], down[...])).astype(BF16)
+
+
+def output_part(attended, dense, activated, down):
+    count, width = attended.shape[0], dense.shape[1]
+    block = 256
+    fixed = lambda i: (0, 0)
+    column = lambda i: (0, i)
+    return pl.pallas_call(
+        output_kernel,
+        name="output_part",
+        out_shape=jax.ShapeDtypeStruct((count, width), BF16),
+        grid=(width // block,),
+        in_specs=[
+            pl.BlockSpec(attended.shape, fixed),
+            pl.BlockSpec((dense.shape[0], block), column),
+            pl.BlockSpec(activated.shape, fixed),
+            pl.BlockSpec((down.shape[0], block), column),
+        ],
+        out_specs=pl.BlockSpec((count, block), column),
+        compiler_params=pltpu.CompilerParams(vmem_limit_bytes=VMEM),
+        cost_estimate=LIGHT,
+    )(attended, dense, activated, down)
+
+
+def input_kernel(joined, qkv, upward, up, tokens, stats, out, sums):
+    total = nt(joined[...], qkv[...]) + nt(upward[...], up[...])
+    out[...] = total.astype(BF16)
+    xhat = (tokens[...].astype(F32) - stats[:, 0:1]) * stats[:, 1:2]
+    sums[0:1, :] = jnp.sum(total * xhat, axis=0, keepdims=True)
+    sums[1:2, :] = jnp.sum(total, axis=0, keepdims=True)
+
+
+def input_part(joined, qkv, upward, up, tokens, stats):
+    count, width = tokens.shape[0], qkv.shape[0]
+    block = 256
+    fixed = lambda i: (0, 0)
+    column = lambda i: (0, i)
+    row = lambda i: (i, 0)
+    return pl.pallas_call(
+        input_kernel,
+        name="input_part",
+        out_shape=[
+            jax.ShapeDtypeStruct((count, width), BF16),
+            jax.ShapeDtypeStruct((2, width), F32),
+        ],
+        grid=(width // block,),
+        in_specs=[
+            pl.BlockSpec(joined.shape, fixed),
+            pl.BlockSpec((block, qkv.shape[1]), row),
+            pl.BlockSpec(upward.shape, fixed),
+            pl.BlockSpec((block, up.shape[1]), row),
+            pl.BlockSpec((count, block), column),
+            pl.BlockSpec(stats.shape, fixed),
+        ],
+        out_specs=[pl.BlockSpec((count, block), column), pl.BlockSpec((2, block), column)],
+        compiler_params=pltpu.CompilerParams(vmem_limit_bytes=VMEM),
+        cost_estimate=LIGHT,
+    )(joined, qkv, upward, up, tokens, stats)
+
+
+def finish_kernel(tokens, cotangent, branch, grad, gain, bias, out, tokens_grad):
+    value = tokens[...].astype(F32)
+    out[...] = (value + branch[...].astype(F32) + bias[...]).astype(BF16)
+    centre = value - jnp.mean(value, axis=1, keepdims=True)
+    inv_std = lax.rsqrt(jnp.mean(centre * centre, axis=1, keepdims=True) + EPSILON)
+    xhat = centre * inv_std
+    scaled = grad[...].astype(F32) * gain[...]
+    inner = jnp.mean(scaled * xhat, axis=1, keepdims=True)
+    scaled = scaled - jnp.mean(scaled, axis=1, keepdims=True) - xhat * inner
+    tokens_grad[...] = cotangent[...].astype(F32) + inv_std * scaled
+
+
+def finish(tokens, cotangent, branch, grad, gain, bias):
+    rows, width = tokens.shape
+    block = 64 if rows % 64 == 0 else rows
+    row = pl.BlockSpec((block, width), lambda i: (i, 0))
+    vector = pl.BlockSpec((1, width), lambda i: (0, 0))
+    return pl.pallas_call(
+        finish_kernel,
+        name="finish",
+        out_shape=[
+            jax.ShapeDtypeStruct((rows, width), BF16),
+            jax.ShapeDtypeStruct((rows, width), F32),
+        ],
+        grid=(rows // block,),
+        in_specs=[row] * 4 + [vector] * 2,
+        out_specs=[row, row],
+        compiler_params=pltpu.CompilerParams(vmem_limit_bytes=VMEM),
+        cost_estimate=LIGHT,
+    )(tokens, cotangent, branch, grad, gain[None], bias[None])
+
+
+def clip_kernel(heads, head_dim, maxima, limits, weight, bias, out, bias_out):
+    first = lax.rem(pl.program_id(0) * (out.shape[1] // head_dim), heads)
+    factor = limits[...] / jnp.maximum(maxima[...], limits[...])
+    lane = lax.broadcasted_iota(jnp.int32, (1, heads), 1)
+    head = first + lax.broadcasted_iota(jnp.int32, (1, out.shape[1]), 1) // head_dim
+    scale = jnp.zeros((1, out.shape[1]), F32)
+    for h in range(heads):
+        one = jnp.sum(jnp.where(lane == h, factor, 0.0), axis=1, keepdims=True)
+        scale = jnp.where(head == h, jnp.sqrt(one), scale)
+    out[...] = weight[...].astype(F32) * scale
+    bias_out[...] = bias[...] * scale
+
+
+def clip_columns(weight, bias, maxima, limits, head_dim):
+    rows, heads = weight.shape[0], maxima.shape[0]
+    columns = 2 * heads * head_dim
+    block = heads * head_dim // 2
+    column = lambda i: (0, i)
+    vector = pl.BlockSpec((1, heads), lambda i: (0, 0))
+    wide, thin = pl.BlockSpec((rows, block), column), pl.BlockSpec((1, block), column)
+    out, bias_out = pl.pallas_call(
+        partial(clip_kernel, heads, head_dim),
+        name="clip_columns",
+        out_shape=[
+            jax.ShapeDtypeStruct((rows, columns), F32),
+            jax.ShapeDtypeStruct((1, columns), F32),
+        ],
+        grid=(columns // block,),
+        in_specs=[vector, vector, wide, thin],
+        out_specs=[wide, thin],
+        compiler_params=pltpu.CompilerParams(vmem_limit_bytes=VMEM),
+        cost_estimate=LIGHT,
+    )(maxima[None], limits.astype(F32)[None], weight, bias[None])
+    return out, bias_out[0]
 
 
 def forwarded(received, axis):
@@ -128,54 +262,56 @@
     )
 
 
-def four_parts(part, near, far, axis):
-    return [part, near[0], near[1], jnp.concatenate(far, axis)]
+def four_parts(part, near, far):
+    return [part, near[0], near[1], far[0], far[1]]
+
+
+def pieces_of(index_ref, refs, eighth, axis):
+    me = index_ref[0]
+    first = (slice(None),) * axis + (slice(0, eighth),)
+    second = (slice(None),) * axis + (slice(eighth, 2 * eighth),)
+    for offset in range(3):
+        owner = me ^ offset
+        yield first_place(owner), refs[offset], first
+        yield 4 + owner, refs[offset], second
+    owner = me ^ 3
+    yield first_place(owner), refs[3], first
+    yield 4 + owner, refs[4], first
 
 
 def place_rows(index_ref, *refs):
-    parts, out = refs[:-1], refs[-1]
-    eighth = parts[0].shape[-2] // 2
-    me = index_ref[0]
-    for offset, ref in enumerate(parts):
-        owner = me ^ offset
-        block = ref[0].astype(out.dtype)
-        start = pl.multiple_of(first_place(owner) * eighth, eighth)
-        out[pl.ds(start, eighth), :] = block[:eighth]
-        start = pl.multiple_of((4 + owner) * eighth, eighth)
-        out[pl.ds(start, eighth), :] = block[eighth:]
+    out = refs[-1]
+    blocks, size, width = refs[0].shape
+    for spot, ref, cut in pieces_of(index_ref, refs, size // 2, 1):
+        rows = pl.ds(pl.multiple_of(spot * (size // 2), size // 2), size // 2)
+        for i in range(blocks):
+            out[rows, i * width : (i + 1) * width] = ref[(i,) + cut[1:]].astype(out.dtype)
 
 
 def place_columns(index_ref, *refs):
-    parts, out = refs[:-1], refs[-1]
-    eighth = parts[0].shape[-1] // 2
-    me = index_ref[0]
-    for offset, ref in enumerate(parts):
-        owner = me ^ offset
-        start = pl.multiple_of(first_place(owner) * eighth, eighth)
-        out[:, pl.ds(start, eighth)] = ref[:, :eighth].astype(out.dtype)
-        start = pl.multiple_of((4 + owner) * eighth, eighth)
-        out[:, pl.ds(start, eighth)] = ref[:, eighth:].astype(out.dtype)
-
-
-def place(body, parts, grid, in_block, in_map, out_shape, out_block, out_map):
-    index = lax.axis_index("dp").astype(jnp.int32).reshape(1)
-    size = sum(part.size * part.dtype.itemsize for part in parts)
+    out = refs[-1]
+    eighth = refs[0].shape[1] // 2
+    for spot, ref, cut in pieces_of(index_ref, refs, eighth, 1):
+        columns = pl.ds(pl.multiple_of(spot * eighth, eighth), eighth)
+        out[:, columns] = ref[cut].astype(out.dtype)
+
+
+def place(body, parts, axis, grid, in_block, in_map, out_shape, out_block, out_map):
+    half = list(in_block)
+    half[axis] //= 2
     return pl.pallas_call(
         body,
         out_shape=out_shape,
         grid_spec=pltpu.PrefetchScalarGridSpec(
             num_scalar_prefetch=1,
             grid=grid,
-            in_specs=[pl.BlockSpec(in_block, in_map)] * 4,
+            in_specs=[pl.BlockSpec(in_block, in_map)] * 3
+            + [pl.BlockSpec(tuple(half), in_map)] * 2,
             out_specs=pl.BlockSpec(out_block, out_map),
         ),
-        compiler_params=pltpu.CompilerParams(vmem_limit_bytes=32 << 20),
-        cost_estimate=pl.CostEstimate(
-            flops=0,
-            transcendentals=0,
-            bytes_accessed=size + out_shape.size * out_shape.dtype.itemsize,
-        ),
-    )(index, *parts)
+        compiler_params=pltpu.CompilerParams(vmem_limit_bytes=VMEM),
+        cost_estimate=LIGHT,
+    )(dp_index(), *parts)
 
 
 def full_rows(parts, own_rows):
@@ -183,6 +319,7 @@
     return place(
         place_rows,
         parts,
+        1,
         (blocks,),
         (1, size, columns),
         lambda i, index: (i, 0, 0),
@@ -195,15 +332,18 @@
 def full_grad(parts, own_rows, groups):
     blocks, size, columns = parts[0].shape
     width = columns // groups
+    several = max(1, min(blocks, 1024 // width))
+    steps = blocks // several
     return place(
         place_rows,
         parts,
-        (groups, blocks),
-        (1, size, width),
+        1,
+        (groups, steps),
+        (several, size, width),
         lambda g, i, index: (i, 0, g),
         jax.ShapeDtypeStruct((own_rows, groups * blocks * width), F32),
-        (own_rows, width),
-        lambda g, i, index: (0, g * blocks + i),
+        (own_rows, several * width),
+        lambda g, i, index: (0, g * steps + i),
     )
 
 
@@ -212,6 +352,7 @@
     return place(
         place_columns,
         parts,
+        1,
         (count // block,),
         (block, size),
         lambda i, index: (i + first // block, 0),
@@ -368,7 +509,7 @@
                 pltpu.VMEM((heads, block, LANES), F32),
             ],
         ),
-        compiler_params=pltpu.CompilerParams(vmem_limit_bytes=40 << 20),
+        compiler_params=pltpu.CompilerParams(vmem_limit_bytes=VMEM),
         cost_estimate=pl.CostEstimate(
             flops=4 * pairs * 2 * LANES, transcendentals=pairs, bytes_accessed=length * own * 26
         ),
@@ -484,7 +625,7 @@
                 pltpu.VMEM((heads, LANES, block), F32),
             ],
         ),
-        compiler_params=pltpu.CompilerParams(vmem_limit_bytes=40 << 20),
+        compiler_params=pltpu.CompilerParams(vmem_limit_bytes=VMEM),
         cost_estimate=pl.CostEstimate(
             flops=10 * pairs * 2 * LANES, transcendentals=pairs, bytes_accessed=length * own * 20
         ),
@@ -507,25 +648,15 @@
 
 
 def gather_weights(qkv_weight, up_weight):
-    own_rows = qkv_weight.shape[0]
-    if lax.axis_size("dp") != 4:
-        q, u = exchange(to_columns(qkv_weight, 3)), exchange(to_columns(up_weight, 1))
-        return q.reshape(-1, q.shape[2]), u.reshape(-1, u.shape[2])
+    u = to_columns(my_part(up_weight, 0), 1)
     q = to_columns(my_part(qkv_weight, 0), 3)
-    u = to_columns(my_part(up_weight, 0), 1)
+    u = exchange(u)
+    u, q = lax.optimization_barrier((u, q))
+    u_near = along_both((u, u))
     q = exchange(q)
-    q, u = lax.optimization_barrier((q, u))
+    u_far = along_both(forwarded(u_near, 1))
     q_near = along_both((q, q))
-    u = exchange(u)
-    q_near, u = lax.optimization_barrier((q_near, u))
-    u_near = along_both((u, u))
-    q_far = along_both(forwarded(q_near, 1))
-    q_far, u_near = lax.optimization_barrier((q_far, u_near))
-    u_far = along_both(forwarded(u_near, 1))
-    return (
-        full_rows(four_parts(q, q_near, q_far, 1), own_rows),
-        full_rows(four_parts(u, u_near, u_far, 1), own_rows),
-    )
+    return q, q_near, u, u_near, u_far
 
 
 def reduce_input_grad(grad, own_rows, groups):
@@ -570,24 +701,36 @@
     count = seqs * length
     scale = head_dim ** (-0.5)
 
-    inputs = tokens.reshape(rows, width).astype(F32)
-    centre = inputs - jnp.mean(inputs, axis=-1, keepdims=True)
-    inv_std = lax.rsqrt(jnp.mean(centre * centre, axis=-1, keepdims=True) + EPSILON)
-    normed = centre * inv_std
-    hidden_local = (normed * norm_gain + norm_bias).astype(BF16)
-    hidden = lax.all_gather(
-        hidden_local.reshape(seqs, stretch, width), "ctx", axis=1, tiled=True
+    shared = lax.axis_size("dp") == 4
+    digits = jnp.stack([positions // 32, positions % 32], axis=-1)
+    marked = jnp.concatenate(
+        [tokens, jnp.pad(digits.astype(BF16), ((0, 0), (0, 0), (0, LANES - 2)))], axis=-1
+    )
+    if shared:
+        q, q_near, u, u_near, u_far = gather_weights(qkv_weight, up_weight)
+        up_columns = full_rows(four_parts(u, u_near, u_far), own_rows)
+        q_far = along_both(forwarded(q_near, 1))
+        marked = after(marked, u)
+    else:
+        q, u = exchange(to_columns(qkv_weight, 3)), exchange(to_columns(up_weight, 1))
+        qkv_columns, up_columns = q.reshape(width, -1), u.reshape(width, -1)
+    all_tokens = lax.all_gather(marked, "ctx", axis=1, tiled=True).reshape(count, width + LANES)
+    grad_rows = lax.all_gather(
+        after(cotangent, marked), "ctx", axis=1, tiled=True
     ).reshape(count, width)
-    grad_rows = lax.all_gather(cotangent, "ctx", axis=1, tiled=True).reshape(count, width)
-    qkv_columns, up_columns = gather_weights(qkv_weight, up_weight)
-    positions_all = all_rows(positions.T, "ctx").T
+    hidden, stats = normalize(all_tokens, norm_gain, norm_bias)
+    if shared:
+        q_far = after(q_far, up_columns, hidden)
+        qkv_columns = full_rows(four_parts(q, q_near, q_far), own_rows)
+    digits = all_tokens[:, width : width + 2].astype(F32)
+    places = (digits[:, 0] * 32.0 + digits[:, 1]).reshape(seqs, length)
+    tables = [rotary_lanes(places[s]) for s in range(seqs)]
 
     qkv_own_bias = take(qkv_bias.reshape(3, parts, own), part, 1, 1).reshape(1, 3 * own)
     up_own_bias = take(up_bias, part * own_ff, own_ff, 0)
 
     joined = dot(hidden, qkv_columns, (1, 0))
     block = 256 if length % 256 == 0 else length
-    tables = [rotary_lanes(positions_all[s]) for s in range(seqs)]
     ahead = [
         attend(
             joined[s * length : (s + 1) * length], qkv_own_bias, tables[s], own_heads, scale, block
@@ -620,113 +763,141 @@
 
     def sum_branch(value):
         return lax.psum_scatter(
-            value.astype(BF16).reshape(seqs, length, width),
+            value.reshape(seqs, length, width),
             "ctx",
             scatter_dimension=1,
             tiled=True,
         ).reshape(rows, width)
 
-    def output_part(mixed_out):
-        return sum_branch(dot(mixed_out, jnp.concatenate([dense_weight, down_weight]), (1, 0)))
-
-    def input_part(joined_low, up_low):
-        return sum_branch(
-            dot(joined_low, qkv_columns, (1, 1)) + dot(up_low, up_columns, (1, 1))
+    def own_sums(joined_sum, up_low):
+        return jnp.concatenate(
+            [
+                joined_sum[0],
+                jnp.sum(up_low.astype(F32), axis=0),
+                jnp.sum(take(grad_rows, part * own, own, 1).astype(F32), axis=0),
+            ]
         )
+
+    def small_sums(shifts, mine):
+        return jnp.concatenate([shifts.reshape(2 * width), mine])[None], own_maxima[None]
+
+    def finish_rows(branch_sum, hidden_grad):
+        return finish(
+            tokens.reshape(rows, width),
+            cotangent.reshape(rows, width),
+            branch_sum,
+            hidden_grad,
+            norm_gain,
+            dense_bias + down_bias,
+        )
+
+    def dp_step(small, bit):
+        sums, tops = small
+        got = swap(jnp.concatenate([sums, tops], axis=1), "dp", bit)
+        cut = sums.shape[1]
+        return sums + got[:, :cut], jnp.maximum(tops, got[:, cut:])
+
+    def spread(small):
+        value = jnp.concatenate(small, axis=1)
+        return exchange(jnp.broadcast_to(value[None], (parts,) + value.shape))
+
+    def clip(small):
+        head_maxima = small[:, 0, small.shape[2] - own_heads :].reshape(heads)
+        return head_maxima, clip_columns(qkv_weight, qkv_bias, head_maxima, clip_limit, head_dim)
 
     grad_rows, attended, activated = lax.optimization_barrier((grad_rows, attended, activated))
     mixed_out = jnp.concatenate([attended, activated], axis=1)
     out_raw = dot(mixed_out, grad_rows, (0, 0)).astype(BF16)
-    if lax.axis_size("dp") == 4:
-        o_send = outgoing(out_raw, 1)
-        o_got = along_both(o_send)
+    if shared:
+        together = lax.optimization_barrier
+        o_got = along_both(o_send := outgoing(out_raw, 1))
         up_low, up_raw = feed_forward_back(after(grad_rows, o_send))
         up_raw = up_raw.reshape(parts, own_rows, own_ff)
-        u_send = outgoing(up_raw, 1)
-        u_got = along_both(u_send)
-        joined_low, joined_sum, qkv_raw = attention_back(after(grad_rows, u_send))
+        u_got = along_both(u_send := outgoing(up_raw, 1))
+        branch = output_part(after(attended, u_send), dense_weight, activated, down_weight)
+        branch_sum = sum_branch(branch)
+        o_send, o_keep = first_sums(out_raw, after(o_got, branch), 1)
+        o_got = along_both(o_send)
+        joined_low, joined_sum, qkv_raw = attention_back(after(grad_rows, o_send))
         qkv_raw = qkv_raw.reshape(parts, own_rows, 3 * own)
         q_send = outgoing(qkv_raw, 1)
+        q_send, u_got = together((q_send, u_got))
         q_got = along_both(q_send)
-        o_sums = first_sums(out_raw, after(o_got, q_send), 1)
-        o_send = outgoing_again(o_sums, 1)
-        o_got = along_both(o_send)
-        branch_sum = output_part(after(mixed_out, o_send))
-        u_sums = first_sums(up_raw, after(u_got, o_send), 1)
-        u_send = outgoing_again(u_sums, 1)
+        u_send, u_keep = first_sums(up_raw, u_got, 1)
+        u_send, o_got = together((u_send, o_got))
         u_got = along_both(u_send)
-        hidden_grad = input_part(after(joined_low, u_send), up_low)
-        q_sums = first_sums(qkv_raw, after(q_got, u_send), 1)
-        q_send = outgoing_again(q_sums, 1)
+        o_part = second_sums(o_keep, o_got, 1)
+        hidden_part, shifts = input_part(
+            after(joined_low, o_part), qkv_columns, up_low, up_columns, all_tokens, stats
+        )
+        mine = own_sums(joined_sum, after(up_low, qkv_raw))
+        q_got, o_part, shifts, mine = together((q_got, o_part, shifts, mine))
+        q_send, q_keep = first_sums(qkv_raw, q_got, 1)
+        small = small_sums(shifts, mine)
+        q_send, u_got, small = together((q_send, u_got, small))
+        u_part = second_sums(u_keep, u_got, 1)
+        u_part, o_part, q_send, small = together((u_part, o_part, q_send, small))
         q_got = along_both(q_send)
-        o_part = second_sums(o_sums, after(o_got, q_send), 1)
         o_near = along_both((o_part, o_part))
-        u_part = exchange(second_sums(u_sums, after(u_got, o_part), 1))
-        q_part = exchange(second_sums(q_sums, after(q_got, u_part), 1))
+        u_part = exchange(u_part)
+        small = dp_step(small, 1)
+        q_got, u_part, o_near, small = together((q_got, u_part, o_near, small))
+        hidden_grad = sum_branch(after(hidden_part, u_part))
         u_near = along_both((u_part, u_part))
-        o_far = along_both(forwarded(after(o_near, u_part), 1))
+        o_send = forwarded(o_near, 1)
+        q_part = exchange(second_sums(q_keep, q_got, 1))
+        o_far = along_both(o_send)
+        small = dp_step(small, 2)
+        u_near, q_part, o_far, small = together((u_near, q_part, o_far, small))
         q_near = along_both((q_part, q_part))
-        u_far = along_both(forwarded(after(u_near, q_part), 1))
-        q_far = along_both(forwarded(q_near, 1))
-        o_parts = four_parts(o_part, o_near, o_far, 1)
+        u_send = forwarded(u_near, 1)
+        u_far = along_both(u_send)
+        o_parts = four_parts(o_part, o_near, after(o_far, u_send))
         dense_grad = full_columns(o_parts, 0, own, own)
         down_grad = full_columns(o_parts, own, own_ff, own)
-        up_grad = full_grad(four_parts(u_part, u_near, u_far, 1), own_rows, 1)
-        qkv_grad = full_grad(four_parts(q_part, q_near, q_far, 1), own_rows, 3)
+        small = spread(after(small, down_grad))
+        q_near, u_far, small, dense_grad, down_grad = together(
+            (q_near, u_far, small, dense_grad, down_grad)
+        )
+        q_send = forwarded(q_near, 1)
+        q_far = along_both(q_send)
+        u_far, branch_sum, hidden_grad = after((u_far, branch_sum, hidden_grad), q_send)
+        up_grad = full_grad(four_parts(u_part, u_near, u_far), own_rows, 1)
+        ends = finish_rows(branch_sum, hidden_grad)
+        head_maxima, (clipped_weight, clipped_bias) = clip(after(small, q_send))
+        q_far, up_grad, ends, clipped_weight = together((q_far, up_grad, ends, clipped_weight))
+        qkv_grad = full_grad(four_parts(q_part, q_near, q_far), own_rows, 3)
     else:
         up_low, up_raw = feed_forward_back(grad_rows)
         joined_low, joined_sum, qkv_raw = attention_back(grad_rows)
-        branch_sum = output_part(mixed_out)
-        hidden_grad = input_part(joined_low, up_low)
+        branch_sum = sum_branch(output_part(attended, dense_weight, activated, down_weight))
+        hidden_part, shifts = input_part(
+            joined_low, qkv_columns, up_low, up_columns, all_tokens, stats
+        )
+        hidden_grad = sum_branch(hidden_part)
         out_grad = lax.psum(out_raw, "dp").astype(F32)
         dense_grad, down_grad = out_grad[:own], out_grad[own:]
         up_grad = reduce_input_grad(up_raw, own_rows, 1)
         qkv_grad = reduce_input_grad(qkv_raw, own_rows, 3)
-        o_part = out_grad
-    layer_out = (inputs + branch_sum.astype(F32) + dense_bias + down_bias).astype(BF16)
-    hidden_grad = hidden_grad.astype(F32)
-    gain_part = jnp.sum(hidden_grad * normed, axis=0)
-    shift_part = jnp.sum(hidden_grad, axis=0)
-    scaled = hidden_grad * norm_gain
-    tokens_grad = cotangent.reshape(rows, width).astype(F32) + inv_std * (
-        scaled
-        - jnp.mean(scaled, axis=-1, keepdims=True)
-        - normed * jnp.mean(scaled * normed, axis=-1, keepdims=True)
-    )
-    norm_sums = all_sum(jnp.stack([gain_part, shift_part]), ("dp", "ctx"))
-
-    sums = jnp.concatenate(
-        [
-            joined_sum[0],
-            jnp.sum(up_low.astype(F32), axis=0),
-            jnp.sum(take(grad_rows, part * own, own, 1).astype(F32), axis=0),
-        ]
-    )[None]
-    sums, own_maxima = after((sums, own_maxima), o_part)
-    maxima = own_maxima[None]
-    for bit in bits_of("dp"):
-        both = swap(jnp.concatenate([sums, maxima], axis=1), "dp", bit)
-        sums = sums + both[:, : sums.shape[1]]
-        maxima = jnp.maximum(maxima, both[:, sums.shape[1] :])
-    both = all_rows(jnp.concatenate([sums, maxima], axis=1), "ctx")
+        small = small_sums(shifts, own_sums(joined_sum, up_low))
+        small = spread((lax.psum(small[0], "dp"), lax.pmax(small[1], "dp")))
+        head_maxima, (clipped_weight, clipped_bias) = clip(small)
+        ends = finish_rows(branch_sum, hidden_grad)
+    layer_out, tokens_grad = ends
+    shifts = jnp.sum(small[:, 0, : 2 * width], axis=0)
+    both = small[:, 0, 2 * width :]
     cut = 3 * own + own_ff
     qkv_bias_grad = (
         both[:, : 3 * own].reshape(parts, 3, own).transpose(1, 0, 2).reshape(3 * width)
     )
     up_bias_grad = both[:, 3 * own : cut].reshape(parts * own_ff)
     out_bias_grad = both[:, cut : cut + own].reshape(width)
-    head_maxima = both[:, cut + own :].reshape(heads)
-
-    limits = clip_limit.astype(F32)
-    factor = limits / jnp.maximum(head_maxima, limits)
-    column_scale = jnp.tile(jnp.repeat(jnp.sqrt(factor), head_dim), 2)
-    clipped_weight = qkv_weight[:, : 2 * width].astype(F32) * column_scale
-    clipped_bias = qkv_bias[: 2 * width] * column_scale
+
     return (
         layer_out.reshape(seqs, stretch, width),
         tokens_grad.reshape(seqs, stretch, width),
-        norm_sums[0],
-        norm_sums[1],
+        shifts[:width],
+        shifts[width:],
         qkv_grad,
         qkv_bias_grad,
         dense_grad,

time: 485 us -> 439 us (0.905)
  waiting for transfers between devices: 191 us -> 151 us
  matrix products: 68.3 us -> 36.1 us
  Pallas kernels: 57.4 us -> 82.9 us
  local copies, waits for them, and re-layouts: 41.6 us -> 62.2 us
  other arithmetic: 39.6 us -> 25 us
  starting transfers between devices: 67.6 us -> 61.4 us
    dot_general x10 -> x7, matrix products: 68.3 us -> 36.1 us  [dot(): lax.dot_general(left, right, ((contract[:1], contract[1:]), ((), ())), pr...]
    all_to_all x4 -> x5, waiting for transfers between devices: 97 us -> 65.8 us  [exchange(): lax.all_to_all(blocks, 'ctx', split_axis=0, concat_axis=0, tiled=True)]
    pallas_call x0 -> x5, Pallas kernels: none -> 27.9 us  [the longest x1 11.5 us: input_part(): pl.pallas_call(input_kernel, name='input_part', out_shape=[jax.ShapeDtype...]
    ppermute x45 -> x34, starting transfers between devices: 49.2 us -> 35.1 us  [swap(): lax.ppermute(value, axis, [(i, i ^ bit) for i in range(lax.axis_size(axis...]
    unnamed x90 -> x150, local copies, waits for them, and re-layouts: 16.5 us -> 29.6 us
    ppermute x45 -> x34, waiting for transfers between devices: 92.7 us -> 84.4 us  [swap(): lax.ppermute(value, axis, [(i, i ^ bit) for i in range(lax.axis_size(axis...]
    all_to_all x4 -> x5, starting transfers between devices: 17.7 us -> 25.7 us  [exchange(): lax.all_to_all(blocks, 'ctx', split_axis=0, concat_axis=0, tiled=True)]
    convert_element_type x9 -> x6, other arithmetic: 13.5 us -> 16.3 us  [plus(): return (left.astype(F32) + right.astype(F32)).astype(BF16)]
  transfers between devices with their start and end apart: 53 -> 43, of which waited for: 20 -> 13; matrix products, arithmetic and copies ran while one was open for 23% -> 19% of each run, Pallas kernels for 12% -> 18%
where the time goes in v3:
time: 439 us; the launch traced here: 434 us
  waiting for transfers between devices  151 us (34%)
  Pallas kernels  82.9 us (19%)
  local copies, waits for them, and re-layouts  62.2 us (14%)
  starting transfers between devices  61.4 us (14%)
  matrix products  36.1 us (8%)
  other arithmetic  25 us (6%)
  between operations  15 us (3%)
    ppermute x34, waiting for transfers between devices, swap(): lax.ppermute(value, axis, [(i, i ^ bit) for i in range(lax.axis_size(axis...  84.4 us
    all_to_all x5, waiting for transfers between devices, exchange(): lax.all_to_all(blocks, 'ctx', split_axis=0, concat_axis=0, tiled=True)  65.8 us
    dot_general x7, matrix products, dot(): lax.dot_general(left, right, ((contract[:1], contract[1:]), ((), ())), pr...  36.1 us
    ppermute x34, starting transfers between devices, swap(): lax.ppermute(value, axis, [(i, i ^ bit) for i in range(lax.axis_size(axis...  35.1 us
    pallas_call x6, Pallas kernels, place(): pl.pallas_call(body, out_shape=out_shape, grid_spec=pltpu.PrefetchScalarG...  29.6 us
    unnamed x150, local copies, waits for them, and re-layouts  29.6 us
    all_to_all x5, starting transfers between devices, exchange(): lax.all_to_all(blocks, 'ctx', split_axis=0, concat_axis=0, tiled=True)  25.7 us
    convert_element_type x6, other arithmetic, plus(): return (left.astype(F32) + right.astype(F32)).astype(BF16)  16.3 us
  transfers between devices with their start and end apart: 43, of which 13 were waited for; matrix products, arithmetic and copies ran while one was open for 19% of the time, Pallas kernels for 18%

profile of v3, /device:TPU:0, one launch (start us, length us, event | category | flops | bytes accessed | tf_op | source)
XLA Modules:
  0.0 433.6 jit_solution(15344997969531514554)
XLA Ops:
  10.7 6.3 %all-to-all-start = ((bf16[8,64,1024]{2,1,0:T(8,128)(2,1)}), bf16[8,64,1024]{2,1,0:T(8,128)(2,1)S(1)}, u32[]{:S(2)}, u32[]{:S(2)}) async-start(bf16[8,64,1024]{2,1,0:T(8,128)(2,1)} %bitcast.70), calls=%async_computation | async-start | bytes 2097152 | tf_op jit(solution)/shard_map/all_to_all | solution.py:647
  21.6 22.0 %all-to-all-done.refs_0_ = bf16[8,64,1024]{2,1,0:T(8,128)(2,1)S(1)} async-done(((bf16[8,64,1024]{2,1,0:T(8,128)(2,1)}), bf16[8,64,1024]{2,1,0:T(8,128)(2,1)S(1)}, u32[]{:S(2)}, u32[]{:S(2)}) %all-to-all-start) | async-done | bytes 1048608 | tf_op jit(solution)/shard_map/all_to_all | solution.py:647
  44.4 3.6 all-to-all-start.1
  51.6 36.7 %all-to-all-done.1.refs_0_ = bf16[8,64,768]{2,1,0:T(8,128)(2,1)S(1)} async-done(((bf16[8,64,768]{2,1,0:T(8,128)(2,1)}), bf16[8,64,768]{2,1,0:T(8,128)(2,1)S(1)}, u32[]{:S(2)}, u32[]{:S(2)}) %all-to-all-start.1) | async-done | bytes 786464 | tf_op jit(solution)/shard_map/all_to_all | solution.py:647
  92.8 1.9 slice.107
  95.8 13.1 %collective-permute-done.1.refs_2_ = bf16[8,64,768]{2,1,0:T(8,128)(2,1)} collective-permute-done((bf16[8,64,768]{2,1,0:T(8,128)(2,1)S(1)}, bf16[8,64,768]{2,1,0:T(8,128)(2,1)}, u32[]{:S(2)}, u32[]{:S(2)}) %collective-permute-start.1) | collective-permute-done | bytes 786464 | tf_op jit(solution)/shard_map/ppermute | solution.py:29
  115.6 6.1 %collective-permute-done.6.refs_3_ = bf16[8,32,1024]{2,1,0:T(8,128)(2,1)S(1)} collective-permute-done((bf16[8,32,1024]{2,1,0:T(8,128)(2,1)}, bf16[8,32,1024]{2,1,0:T(8,128)(2,1)S(1)}, u32[]{:S(2)}, u32[]{:S(2)}) %collective-permute-start.6) | collective-permute-done | bytes 524320 | tf_op jit(solution)/shard_map/ppermute | solution.py:29
  121.6 4.0 shard_map.253.up
  125.7 2.0 copy-done.2
  127.7 2.3 copy-done
  130.1 3.4 normalize.1
  133.5 5.1 %shard_map.254.qkv = bf16[2048,768]{1,0:T(8,128)(2,1)S(1)} custom-call(s32[1]{0:T(128)} %bitcast.9.index_ref, bf16[8,64,768]{2,1,0:T(8,128)(2,1)S(1)} %copy-done.11, bf16[8,64,768]{2,1,0:T(8,128)(2,1)} %collective-permute-done.refs_1_, bf16[8,64,768]{2,1,0:T(8,128)(2,1)} %collective-permute-done.1.refs_2_, ...), custom_call_target="tpu_custom_call" | custom-call | flops 1 | bytes 1 | tf_op jit(solution)/shard_map/pallas_call | solution.py:302
  140.0 2.0 fusion.11
  142.0 3.4 fusion.27.joined
  145.5 10.7 %attend.1 = (bf16[1024,256]{1,0:T(8,128)(2,1)S(1)}, bf16[1024,256]{1,0:T(8,128)(2,1)S(1)}, bf16[1024,256]{1,0:T(8,128)(2,1)S(1)}, f32[1024,256]{1,0:T(8,128)S(1)...) custom-call(f32[1024,768]{1,0:T(8,128)S(1)} %fusion.27.joined, ...), custom_call_target="tpu_custom_call" | custom-call | flops 2147483648 | bytes 6815744 | tf_op jit(solution)/shard_map/attend/pallas_call | solution.py:493
  161.2 7.2 %multiply_convert_fusion = (bf16[1024,1024]{1,0:T(8,128)(2,1)}, f32[1024,1024]{1,0:T(8,128)}) fusion(f32[1024]{0:T(1024)S(1)} %dynamic_slice.98, bf16[1024,2048]{1,0:T(8,128)(2,1)S(1)} %get-tuple-element.112, bf16[2048,1024]{1,0:T(8,128)(2,1)S(1)} %copy-done.3), kind=kOutput, calls=%fused_computation.11 | convolution fusion | flops 4305453056 | bytes 14684160 | tf_op jit(solution)/shard_map/dot_general | solution.py:23
  168.4 8.5 %convolution_convert_fusion = bf16[1280,2048]{1,0:T(8,128)(2,1)S(1)} fusion(bf16[1024,2048]{1,0:T(8,128)(2,1)} %bitcast.108, bf16[1024,1024]{1,0:T(8,128)(2,1)} %get-tuple-element.120.activated, bf16[1024,256]{1,0:T(8,128)(2,1)} %copy-done.28), kind=kOutput, calls=%fused_computation | convolution fusion | flops 5376573440 | bytes 12058624 | tf_op jit(solution)/shard_map/dot_general | solution.py:23
  177.0 1.8 constant_dynamic-slice_fusion.16
  181.9 7.1 %fusion.6.upward = bf16[1024,1024]{1,0:T(8,128)(2,1)S(1)} fusion(f32[1024,1024]{1,0:T(8,128)S(1)} %copy-done.69, f32[1024]{0:T(1024)S(1)} %dynamic_slice.98, bf16[1024,2048]{1,0:T(8,128)(2,1)S(1)} %bitcast.110, bf16[1024,2048]{1,0:T(8,128)(2,1)S(1)} %copy-done.8), kind=kOutput, calls=%fused_computation.9 | convolution fusion | flops 4316987392 | bytes 14684160 | tf_op jit(solution)/shard_map/dot_general | solution.py:23
  189.0 4.9 %convolution_convert_fusion.1 = bf16[2048,1024]{1,0:T(8,128)(2,1)S(1)} fusion(bf16[1024,2048]{1,0:T(8,128)(2,1)S(1)} %copy-done.42, bf16[1024,1024]{1,0:T(8,128)(2,1)S(1)} %fusion.6.upward), kind=kOutput, calls=%fused_computation.12 | convolution fusion | flops 4297064448 | bytes 10485760 | tf_op jit(solution)/shard_map/dot_general | solution.py:23
  198.1 8.2 %output_part.1 = bf16[1024,2048]{1,0:T(8,128)(2,1)S(1)} custom-call(bf16[1024,256]{1,0:T(8,128)(2,1)S(1)} %copy-done.29, bf16[256,2048]{1,0:T(8,128)(2,1)S(1)} %copy-done.24, bf16[1024,1024]{1,0:T(8,128)(2,1)S(1)} %copy-done.21, bf16[1024,2048]{1,0:T(8,128)(2,1)S(1)} %copy-done.8), custom_call_target="tpu_custom_call" | custom-call | flops 1 | bytes 1 | tf_op jit(solution)/shard_map/output_part/pallas_call | solution.py:136
  206.3 2.0 copy-done.1
  211.6 3.3 add_convert_fusion.1
  221.1 14.7 %attend_back.1 = (bf16[1024,768]{1,0:T(8,128)(2,1)S(1)}, f32[1,768]{1,0:T(1,128)S(1)}) custom-call(bf16[1024,256]{1,0:T(8,128)(2,1)S(1)} %copy-done.47, bf16[1024,256]{1,0:T(8,128)(2,1)S(1)} %copy-done.49, bf16[1024,256]{1,0:T(8,128)(2,1)S(1)} %copy-done.51, bf16[1024,256]{1,0:T(8,128)(2,1)S(1)} %copy-done.49, ...), custom_call_target="tpu_custom_call" | custom-call | flops 5368709120 | bytes 5242880 | tf_op jit(solution)/shard_map/attend_back/pallas_call | solution.py:605
  235.8 3.8 convolution_convert_fusion.2
  244.3 2.0 convert_reduce_fusion
  246.3 3.2 add_convert_fusion.5
  250.9 3.1 add_convert_fusion.refs_0_
  256.3 11.5 %input_part.1 = (bf16[1024,2048]{1,0:T(8,128)(2,1)S(1)}, f32[2,2048]{1,0:T(2,128)S(1)}) custom-call(bf16[1024,768]{1,0:T(8,128)(2,1)S(1)} %copy-done.23, bf16[2048,768]{1,0:T(8,128)(2,1)S(1)} %shard_map.254.qkv, bf16[1024,1024]{1,0:T(8,128)(2,1)S(1)} %copy-done.6, bf16[2048,1024]{1,0:T(8,128)(2,1)} %copy-done.2, bf16[1024,2176]{1,0:T(8,128)(2,1)} %bitcast.75, ...), custom_call_target="tpu_custom_call" | custom-call | flops 1 | bytes 1 | tf_op jit(solution)/shard_map/input_part/pallas_call | solution.py:167
  267.9 3.0 add_convert_fusion.7
  274.0 7.0 %all-to-all-start.2 = ((bf16[8,64,1024]{2,1,0:T(8,128)(2,1)}), bf16[8,64,1024]{2,1,0:T(8,128)(2,1)}, u32[]{:S(2)}, u32[]{:S(2)}) async-start(bf16[8,64,1024]{2,1,0:T(8,128)(2,1)} %add_convert_fusion.3), calls=%async_computation.2 | async-start | bytes 2097152 | tf_op jit(solution)/shard_map/all_to_all | solution.py:647
  285.9 35.5 %collective-permute-done.18 = bf16[8,32,768]{2,1,0:T(8,128)(2,1)S(1)} collective-permute-done((bf16[8,32,768]{2,1,0:T(8,128)(2,1)}, bf16[8,32,768]{2,1,0:T(8,128)(2,1)S(1)}, u32[]{:S(2)}, u32[]{:S(2)}) %collective-permute-start.18) | collective-permute-done | bytes 393248 | tf_op jit(solution)/shard_map/ppermute | solution.py:29
  325.8 2.2 add_convert_fusion.6
  327.9 4.8 %all-to-all-start.3 = ((bf16[8,64,768]{2,1,0:T(8,128)(2,1)}), bf16[8,64,768]{2,1,0:T(8,128)(2,1)S(1)}, u32[]{:S(2)}, u32[]{:S(2)}) async-start(bf16[8,64,768]{2,1,0:T(8,128)(2,1)} %add_convert_fusion.6), calls=%async_computation.3 | async-start | bytes 1572864 | tf_op jit(solution)/shard_map/all_to_all | solution.py:647
  336.0 14.5 %collective-permute-done.27 = f32[1,6148]{1,0:T(1,128)S(1)} collective-permute-done((f32[1,6148]{1,0:T(1,128)S(1)}, f32[1,6148]{1,0:T(1,128)S(1)}, u32[]{:S(2)}, u32[]{:S(2)}) %collective-permute-start.27) | collective-permute-done | bytes 24624 | tf_op jit(solution)/shard_map/ppermute | solution.py:29
  350.5 10.9 %collective-permute-done.25.refs_3_ = bf16[1280,256]{1,0:T(8,128)(2,1)S(1)} collective-permute-done((bf16[1280,256]{1,0:T(8,128)(2,1)S(1)}, bf16[1280,256]{1,0:T(8,128)(2,1)S(1)}, u32[]{:S(2)}, u32[]{:S(2)}) %collective-permute-start.25) | collective-permute-done | bytes 655392 | tf_op jit(solution)/shard_map/ppermute | solution.py:29
  363.3 3.3 all-to-all-done.3.refs_0_
  368.5 1.9 slice.92
  370.4 1.9 slice.93
  376.6 5.0 %shard_map.255 = f32[1024,2048]{1,0:T(8,128)} custom-call(s32[1]{0:T(128)} %bitcast.9.index_ref, bf16[1280,512]{1,0:T(8,128)(2,1)S(1)} %copy-done.4, bf16[1280,512]{1,0:T(8,128)(2,1)S(1)} %collective-permute-done.20.refs_1_, bf16[1280,512]{1,0:T(8,128)(2,1)} %collective-permute-done.21.refs_2_, bf16[1280,256]{1,0:T(8,128)(2,1)S(1)} %copy-done.13, ...), custom_call_target="tpu_custom_call" | custom-call | flops 1 | bytes 1 | tf_op jit(solution)/shard_map/pallas_call | solution.py:302
  382.5 4.0 all-to-all-start.4
  388.8 2.4 shard_map.256
  391.2 3.8 all-to-all-done.4
  395.0 2.1 collective-permute-done.30.refs_3_
  403.1 1.9 copy-done.7
  405.0 2.9 clip_columns.1
  411.5 7.5 %shard_map.257 = f32[256,8192]{1,0:T(8,128)} custom-call(s32[1]{0:T(128)} %bitcast.9.index_ref, bf16[8,64,1024]{2,1,0:T(8,128)(2,1)} %all-to-all-done.2.refs_0_, bf16[8,64,1024]{2,1,0:T(8,128)(2,1)} %collective-permute-done.23.refs_1_, bf16[8,64,1024]{2,1,0:T(8,128)(2,1)} %collective-permute-done.24.refs_2_, ...), custom_call_target="tpu_custom_call" | custom-call | flops 1 | bytes 1 | tf_op jit(solution)/shard_map/pallas_call | solution.py:302
  420.7 5.5 %shard_map.258 = f32[256,6144]{1,0:T(8,128)} custom-call(s32[1]{0:T(128)} %bitcast.9.index_ref, bf16[8,64,768]{2,1,0:T(8,128)(2,1)S(1)} %all-to-all-done.3.refs_0_, bf16[8,64,768]{2,1,0:T(8,128)(2,1)} %collective-permute-done.28.refs_1_, bf16[8,64,768]{2,1,0:T(8,128)(2,1)} %collective-permute-done.29.refs_2_, ...), custom_call_target="tpu_custom_call" | custom-call | flops 1 | bytes 1 | tf_op jit(solution)/shard_map/pallas_call | solution.py:302
  (279 shorter events, 94.6 us)
Async XLA Ops:
  10.7 32.9 %all-to-all-start = ((bf16[8,64,1024]{2,1,0:T(8,128)(2,1)}), bf16[8,64,1024]{2,1,0:T(8,128)(2,1)S(1)}, u32[]{:S(2)}, u32[]{:S(2)}) async-start(bf16[8,64,1024]{2,1,0:T(8,128)(2,1)} %bitcast.70), calls=%async_computation | async-start | bytes 2097152 | tf_op jit(solution)/shard_map/all_to_all | solution.py:647
  17.0 110.7 %all-gather.3.cloned.1.call-start = ((), (), s32[]{:S(2)}) async-start(), calls=%async_computation.7 | async-start | bytes 5013504 | tf_op jit(solution)/shard_map/all_gather | solution.py:717
  20.6 74.5 %copy-start.38 = (f32[6144]{0:T(1024)S(1)}, f32[6144]{0:T(1024)}, u32[]{:S(2)}) copy-start(f32[6144]{0:T(1024)} %param.19) | copy-start | bytes 73732
  43.6 124.8 %all-gather.5.cloned.1.call-start = ((), (), s32[]{:S(2)}) async-start(), calls=%async_computation.8 | async-start | bytes 4718592 | tf_op jit(solution)/shard_map/all_gather | solution.py:718
  44.4 44.0 %all-to-all-start.1 = ((bf16[8,64,768]{2,1,0:T(8,128)(2,1)}), bf16[8,64,768]{2,1,0:T(8,128)(2,1)S(1)}, u32[]{:S(2)}, u32[]{:S(2)}) async-start(bf16[8,64,768]{2,1,0:T(8,128)(2,1)} %reshape.178), calls=%async_computation.1 | async-start | bytes 1572864 | tf_op jit(solution)/shard_map/all_to_all | solution.py:647
  48.0 363.5 %reduce-scatter.3.cloned.1.call-start = ((), (), s32[]{:S(2)}) async-start(), calls=%async_computation.9 | async-start | bytes 4718592 | tf_op jit(solution)/shard_map/reduce_scatter | solution.py:765
  48.5 42.8 %collective-permute-start.5 = (bf16[8,64,1024]{2,1,0:T(8,128)(2,1)S(1)}, bf16[8,64,1024]{2,1,0:T(8,128)(2,1)S(1)}, u32[]{:S(2)}, u32[]{:S(2)}) collective-permute-start(bf16[8,64,1024]{2,1,0:T(8,128)(2,1)S(1)} %all-to-all-done.refs_0_), channel_id=1, source_target_pairs={{0,16},{8,24},{16,0},{24,8},{1,17},{9,25},{17,1},{25,9},{2,18},{10... | collective-permute-start | bytes 3145736 | tf_op jit(solution)/shard_map/ppermute | solution.py:29
  50.1 42.6 %collective-permute-start.4 = (bf16[8,64,1024]{2,1,0:T(8,128)(2,1)S(1)}, bf16[8,64,1024]{2,1,0:T(8,128)(2,1)}, u32[]{:S(2)}, u32[]{:S(2)}) collective-permute-start(bf16[8,64,1024]{2,1,0:T(8,128)(2,1)S(1)} %all-to-all-done.refs_0_), channel_id=1, source_target_pairs={{0,8},{8,0},{16,24},{24,16},{1,9},{9,1},{17,25},{25,17},{2,10},{10... | collective-permute-start | bytes 3145736 | tf_op jit(solution)/shard_map/ppermute | solution.py:29
  88.4 37.3 %copy-start.10 = (bf16[8,64,768]{2,1,0:T(8,128)(2,1)}, bf16[8,64,768]{2,1,0:T(8,128)(2,1)S(1)}, u32[]{:S(2)}) copy-start(bf16[8,64,768]{2,1,0:T(8,128)(2,1)S(1)} %all-to-all-done.1.refs_0_) | copy-start | bytes 2359300
  88.4 20.6 %collective-permute-start.1 = (bf16[8,64,768]{2,1,0:T(8,128)(2,1)S(1)}, bf16[8,64,768]{2,1,0:T(8,128)(2,1)}, u32[]{:S(2)}, u32[]{:S(2)}) collective-permute-start(bf16[8,64,768]{2,1,0:T(8,128)(2,1)S(1)} %all-to-all-done.1.refs_0_), channel_id=1, source_target_pairs={{0,16},{8,24},{16,0},{24,8},{1,17},{9,25},{17,1},{25,9},{2,18},{10... | collective-permute-start | bytes 2359304 | tf_op jit(solution)/shard_map/ppermute | solution.py:29
  89.9 22.3 %collective-permute-start = (bf16[8,64,768]{2,1,0:T(8,128)(2,1)S(1)}, bf16[8,64,768]{2,1,0:T(8,128)(2,1)}, u32[]{:S(2)}, u32[]{:S(2)}) collective-permute-start(bf16[8,64,768]{2,1,0:T(8,128)(2,1)S(1)} %all-to-all-done.1.refs_0_), channel_id=1, source_target_pairs={{0,8},{8,0},{16,24},{24,16},{1,9},{9,1},{17,25},{25,17},{2,10},{10... | collective-permute-start | bytes 2359304 | tf_op jit(solution)/shard_map/ppermute | solution.py:29
  92.2 29.4 %collective-permute-start.6 = (bf16[8,32,1024]{2,1,0:T(8,128)(2,1)}, bf16[8,32,1024]{2,1,0:T(8,128)(2,1)S(1)}, u32[]{:S(2)}, u32[]{:S(2)}) collective-permute-start(bf16[8,32,1024]{2,1,0:T(8,128)(2,1)} %slice.106), channel_id=1, source_target_pairs={{0,8},{8,0},{16,24},{24,16},{1,9},{9,1},{17,25},{25,17},{2,10},{10... | collective-permute-start | bytes 1572872 | tf_op jit(solution)/shard_map/ppermute | solution.py:29
  94.6 27.0 %collective-permute-start.7 = (bf16[8,32,1024]{2,1,0:T(8,128)(2,1)}, bf16[8,32,1024]{2,1,0:T(8,128)(2,1)}, u32[]{:S(2)}, u32[]{:S(2)}) collective-permute-start(bf16[8,32,1024]{2,1,0:T(8,128)(2,1)} %slice.107), channel_id=1, source_target_pairs={{0,16},{8,24},{16,0},{24,8},{1,17},{9,25},{17,1},{25,9},{2,18},{10... | collective-permute-start | bytes 1572872 | tf_op jit(solution)/shard_map/ppermute | solution.py:29
  110.7 22.8 %collective-permute-start.2 = (bf16[8,32,768]{2,1,0:T(8,128)(2,1)}, bf16[8,32,768]{2,1,0:T(8,128)(2,1)}, u32[]{:S(2)}, u32[]{:S(2)}) collective-permute-start(bf16[8,32,768]{2,1,0:T(8,128)(2,1)} %slice.104), channel_id=1, source_target_pairs={{0,8},{8,0},{16,24},{24,16},{1,9},{9,1},{17,25},{25,17},{2,10},{10... | collective-permute-start | bytes 1179656 | tf_op jit(solution)/shard_map/ppermute | solution.py:29
  114.0 19.5 %collective-permute-start.3 = (bf16[8,32,768]{2,1,0:T(8,128)(2,1)}, bf16[8,32,768]{2,1,0:T(8,128)(2,1)}, u32[]{:S(2)}, u32[]{:S(2)}) collective-permute-start(bf16[8,32,768]{2,1,0:T(8,128)(2,1)} %slice.105), channel_id=1, source_target_pairs={{0,16},{8,24},{16,0},{24,8},{1,17},{9,25},{17,1},{25,9},{2,18},{10... | collective-permute-start | bytes 1179656 | tf_op jit(solution)/shard_map/ppermute | solution.py:29
  133.5 22.7 %copy-start.41 = (bf16[1024,2048]{1,0:T(8,128)(2,1)}, bf16[1024,2048]{1,0:T(8,128)(2,1)S(1)}, u32[]{:S(2)}) copy-start(bf16[1024,2048]{1,0:T(8,128)(2,1)S(1)} %get-tuple-element.112) | copy-start | bytes 12582916
  178.7 32.8 %collective-permute-start.8 = (bf16[1280,512]{1,0:T(8,128)(2,1)}, bf16[1280,512]{1,0:T(8,128)(2,1)}, u32[]{:S(2)}, u32[]{:S(2)}) collective-permute-start(bf16[1280,512]{1,0:T(8,128)(2,1)} %get-tuple-element.208), channel_id=1, source_target_pairs={{0,8},{8,0},{16,24},{24,16},{1,9},{9,1},{17,25},{25,17},{2,10},{10... | collective-permute-start | bytes 3932168 | tf_op jit(solution)/shard_map/ppermute | solution.py:29
  180.2 31.4 %collective-permute-start.9 = (bf16[1280,512]{1,0:T(8,128)(2,1)}, bf16[1280,512]{1,0:T(8,128)(2,1)}, u32[]{:S(2)}, u32[]{:S(2)}) collective-permute-start(bf16[1280,512]{1,0:T(8,128)(2,1)} %get-tuple-element.207), channel_id=1, source_target_pairs={{0,16},{8,24},{16,0},{24,8},{1,17},{9,25},{17,1},{25,9},{2,18},{10... | collective-permute-start | bytes 3932168 | tf_op jit(solution)/shard_map/ppermute | solution.py:29
  208.4 34.2 %collective-permute-start.10 = (bf16[8,64,1024]{2,1,0:T(8,128)(2,1)}, bf16[8,64,1024]{2,1,0:T(8,128)(2,1)}, u32[]{:S(2)}, u32[]{:S(2)}) collective-permute-start(bf16[8,64,1024]{2,1,0:T(8,128)(2,1)} %get-tuple-element.212), channel_id=1, source_target_pairs={{0,8},{8,0},{16,24},{24,16},{1,9},{9,1},{17,25},{25,17},{2,10},{10... | collective-permute-start | bytes 3145736 | tf_op jit(solution)/shard_map/ppermute | solution.py:29
  209.9 32.7 %collective-permute-start.11 = (bf16[8,64,1024]{2,1,0:T(8,128)(2,1)}, bf16[8,64,1024]{2,1,0:T(8,128)(2,1)}, u32[]{:S(2)}, u32[]{:S(2)}) collective-permute-start(bf16[8,64,1024]{2,1,0:T(8,128)(2,1)} %get-tuple-element.211), channel_id=1, source_target_pairs={{0,16},{8,24},{16,0},{24,8},{1,17},{9,25},{17,1},{25,9},{2,18},{10... | collective-permute-start | bytes 3145736 | tf_op jit(solution)/shard_map/ppermute | solution.py:29
  216.1 33.8 %collective-permute-start.15 = (bf16[1280,256]{1,0:T(8,128)(2,1)}, bf16[1280,256]{1,0:T(8,128)(2,1)}, u32[]{:S(2)}, u32[]{:S(2)}) collective-permute-start(bf16[1280,256]{1,0:T(8,128)(2,1)} %get-tuple-element.222), channel_id=1, source_target_pairs={{0,16},{8,24},{16,0},{24,8},{1,17},{9,25},{17,1},{25,9},{2,18},{10... | collective-permute-start | bytes 1966088 | tf_op jit(solution)/shard_map/ppermute | solution.py:29
  218.8 31.0 %collective-permute-start.14 = (bf16[1280,256]{1,0:T(8,128)(2,1)}, bf16[1280,256]{1,0:T(8,128)(2,1)}, u32[]{:S(2)}, u32[]{:S(2)}) collective-permute-start(bf16[1280,256]{1,0:T(8,128)(2,1)} %get-tuple-element.224), channel_id=1, source_target_pairs={{0,8},{8,0},{16,24},{24,16},{1,9},{9,1},{17,25},{25,17},{2,10},{10... | collective-permute-start | bytes 1966088 | tf_op jit(solution)/shard_map/ppermute | solution.py:29
  242.6 25.3 %collective-permute-start.12 = (bf16[8,64,768]{2,1,0:T(8,128)(2,1)}, bf16[8,64,768]{2,1,0:T(8,128)(2,1)}, u32[]{:S(2)}, u32[]{:S(2)}) collective-permute-start(bf16[8,64,768]{2,1,0:T(8,128)(2,1)} %get-tuple-element.134), channel_id=1, source_target_pairs={{0,8},{8,0},{16,24},{24,16},{1,9},{9,1},{17,25},{25,17},{2,10},{10... | collective-permute-start | bytes 2359304 | tf_op jit(solution)/shard_map/ppermute | solution.py:29
  243.8 24.0 %collective-permute-start.13 = (bf16[8,64,768]{2,1,0:T(8,128)(2,1)}, bf16[8,64,768]{2,1,0:T(8,128)(2,1)}, u32[]{:S(2)}, u32[]{:S(2)}) collective-permute-start(bf16[8,64,768]{2,1,0:T(8,128)(2,1)} %get-tuple-element.135), channel_id=1, source_target_pairs={{0,16},{8,24},{16,0},{24,8},{1,17},{9,25},{17,1},{25,9},{2,18},{10... | collective-permute-start | bytes 2359304 | tf_op jit(solution)/shard_map/ppermute | solution.py:29
  254.0 18.6 %collective-permute-start.16 = (bf16[8,32,1024]{2,1,0:T(8,128)(2,1)S(1)}, bf16[8,32,1024]{2,1,0:T(8,128)(2,1)S(1)}, u32[]{:S(2)}, u32[]{:S(2)}) collective-permute-start(bf16[8,32,1024]{2,1,0:T(8,128)(2,1)S(1)} %get-tuple-element.145), channel_id=1, source_target_pairs={{0,8},{8,0},{16,24},{24,16},{1,9},{9,1},{17,25},{25,17},{2,10},{10... | collective-permute-start | bytes 1572872 | tf_op jit(solution)/shard_map/ppermute | solution.py:29
  254.8 17.7 %collective-permute-start.17 = (bf16[8,32,1024]{2,1,0:T(8,128)(2,1)S(1)}, bf16[8,32,1024]{2,1,0:T(8,128)(2,1)S(1)}, u32[]{:S(2)}, u32[]{:S(2)}) collective-permute-start(bf16[8,32,1024]{2,1,0:T(8,128)(2,1)S(1)} %get-tuple-element.146), channel_id=1, source_target_pairs={{0,16},{8,24},{16,0},{24,8},{1,17},{9,25},{17,1},{25,9},{2,18},{10... | collective-permute-start | bytes 1572872 | tf_op jit(solution)/shard_map/ppermute | solution.py:29
  274.0 49.0 %all-to-all-start.2 = ((bf16[8,64,1024]{2,1,0:T(8,128)(2,1)}), bf16[8,64,1024]{2,1,0:T(8,128)(2,1)}, u32[]{:S(2)}, u32[]{:S(2)}) async-start(bf16[8,64,1024]{2,1,0:T(8,128)(2,1)} %add_convert_fusion.3), calls=%async_computation.2 | async-start | bytes 2097152 | tf_op jit(solution)/shard_map/all_to_all | solution.py:647
  281.1 130.4 %reduce-scatter.5.cloned.1.call-start = ((), (), s32[]{:S(2)}) async-start(), calls=%async_computation.10 | async-start | bytes 4718592 | tf_op jit(solution)/shard_map/reduce_scatter | solution.py:765
  281.2 4.7 %collective-permute-start.22 = (f32[1,6148]{1,0:T(1,128)S(1)}, f32[1,6148]{1,0:T(1,128)S(1)}, u32[]{:S(2)}, u32[]{:S(2)}) collective-permute-start(f32[1,6148]{1,0:T(1,128)S(1)} %pad_maximum_fusion.2), channel_id=1, source_target_pairs={{0,8},{8,0},{16,24},{24,16},{1,9},{9,1},{17,25},{25,17},{2,10},{10... | collective-permute-start | bytes 73784 | tf_op jit(solution)/shard_map/ppermute | solution.py:29
  281.8 40.5 %collective-permute-start.20 = (bf16[1280,512]{1,0:T(8,128)(2,1)S(1)}, bf16[1280,512]{1,0:T(8,128)(2,1)S(1)}, u32[]{:S(2)}, u32[]{:S(2)}) collective-permute-start(bf16[1280,512]{1,0:T(8,128)(2,1)S(1)} %copy-done.4), channel_id=1, source_target_pairs={{0,8},{8,0},{16,24},{24,16},{1,9},{9,1},{17,25},{25,17},{2,10},{10... | collective-permute-start | bytes 3932168 | tf_op jit(solution)/shard_map/ppermute | solution.py:29
  283.2 39.8 %collective-permute-start.21 = (bf16[1280,512]{1,0:T(8,128)(2,1)S(1)}, bf16[1280,512]{1,0:T(8,128)(2,1)}, u32[]{:S(2)}, u32[]{:S(2)}) collective-permute-start(bf16[1280,512]{1,0:T(8,128)(2,1)S(1)} %copy-done.4), channel_id=1, source_target_pairs={{0,16},{8,24},{16,0},{24,8},{1,17},{9,25},{17,1},{25,9},{2,18},{10... | collective-permute-start | bytes 3932168 | tf_op jit(solution)/shard_map/ppermute | solution.py:29
  283.8 37.5 %collective-permute-start.18 = (bf16[8,32,768]{2,1,0:T(8,128)(2,1)}, bf16[8,32,768]{2,1,0:T(8,128)(2,1)S(1)}, u32[]{:S(2)}, u32[]{:S(2)}) collective-permute-start(bf16[8,32,768]{2,1,0:T(8,128)(2,1)} %get-tuple-element.157), channel_id=1, source_target_pairs={{0,8},{8,0},{16,24},{24,16},{1,9},{9,1},{17,25},{25,17},{2,10},{10... | collective-permute-start | bytes 1179656 | tf_op jit(solution)/shard_map/ppermute | solution.py:29
  284.3 37.9 %collective-permute-start.19 = (bf16[8,32,768]{2,1,0:T(8,128)(2,1)}, bf16[8,32,768]{2,1,0:T(8,128)(2,1)S(1)}, u32[]{:S(2)}, u32[]{:S(2)}) collective-permute-start(bf16[8,32,768]{2,1,0:T(8,128)(2,1)} %get-tuple-element.158), channel_id=1, source_target_pairs={{0,16},{8,24},{16,0},{24,8},{1,17},{9,25},{17,1},{25,9},{2,18},{10... | collective-permute-start | bytes 1179656 | tf_op jit(solution)/shard_map/ppermute | solution.py:29
  323.0 40.2 %collective-permute-start.23 = (bf16[8,64,1024]{2,1,0:T(8,128)(2,1)}, bf16[8,64,1024]{2,1,0:T(8,128)(2,1)}, u32[]{:S(2)}, u32[]{:S(2)}) collective-permute-start(bf16[8,64,1024]{2,1,0:T(8,128)(2,1)} %all-to-all-done.2.refs_0_), channel_id=1, source_target_pairs={{0,8},{8,0},{16,24},{24,16},{1,9},{9,1},{17,25},{25,17},{2,10},{10... | collective-permute-start | bytes 3145736 | tf_op jit(solution)/shard_map/ppermute | solution.py:29
  323.7 39.6 %collective-permute-start.24 = (bf16[8,64,1024]{2,1,0:T(8,128)(2,1)}, bf16[8,64,1024]{2,1,0:T(8,128)(2,1)}, u32[]{:S(2)}, u32[]{:S(2)}) collective-permute-start(bf16[8,64,1024]{2,1,0:T(8,128)(2,1)} %all-to-all-done.2.refs_0_), channel_id=1, source_target_pairs={{0,16},{8,24},{16,0},{24,8},{1,17},{9,25},{17,1},{25,9},{2,18},{10... | collective-permute-start | bytes 3145736 | tf_op jit(solution)/shard_map/ppermute | solution.py:29
  324.2 26.3 %collective-permute-start.27 = (f32[1,6148]{1,0:T(1,128)S(1)}, f32[1,6148]{1,0:T(1,128)S(1)}, u32[]{:S(2)}, u32[]{:S(2)}) collective-permute-start(f32[1,6148]{1,0:T(1,128)S(1)} %pad_maximum_fusion.3), channel_id=1, source_target_pairs={{0,16},{8,24},{16,0},{24,8},{1,17},{9,25},{17,1},{25,9},{2,18},{10... | collective-permute-start | bytes 73784 | tf_op jit(solution)/shard_map/ppermute | solution.py:29
  327.9 38.6 %all-to-all-start.3 = ((bf16[8,64,768]{2,1,0:T(8,128)(2,1)}), bf16[8,64,768]{2,1,0:T(8,128)(2,1)S(1)}, u32[]{:S(2)}, u32[]{:S(2)}) async-start(bf16[8,64,768]{2,1,0:T(8,128)(2,1)} %add_convert_fusion.6), calls=%async_computation.3 | async-start | bytes 1572864 | tf_op jit(solution)/shard_map/all_to_all | solution.py:647
  333.8 27.6 %collective-permute-start.25 = (bf16[1280,256]{1,0:T(8,128)(2,1)S(1)}, bf16[1280,256]{1,0:T(8,128)(2,1)S(1)}, u32[]{:S(2)}, u32[]{:S(2)}) collective-permute-start(bf16[1280,256]{1,0:T(8,128)(2,1)S(1)} %slice.88), channel_id=1, source_target_pairs={{0,8},{8,0},{16,24},{24,16},{1,9},{9,1},{17,25},{25,17},{2,10},{10... | collective-permute-start | bytes 1966088 | tf_op jit(solution)/shard_map/ppermute | solution.py:29
  335.4 27.0 %collective-permute-start.26 = (bf16[1280,256]{1,0:T(8,128)(2,1)S(1)}, bf16[1280,256]{1,0:T(8,128)(2,1)S(1)}, u32[]{:S(2)}, u32[]{:S(2)}) collective-permute-start(bf16[1280,256]{1,0:T(8,128)(2,1)S(1)} %slice.89), channel_id=1, source_target_pairs={{0,16},{8,24},{16,0},{24,8},{1,17},{9,25},{17,1},{25,9},{2,18},{10... | collective-permute-start | bytes 1966088 | tf_op jit(solution)/shard_map/ppermute | solution.py:29
  366.6 31.6 %collective-permute-start.28 = (bf16[8,64,768]{2,1,0:T(8,128)(2,1)S(1)}, bf16[8,64,768]{2,1,0:T(8,128)(2,1)}, u32[]{:S(2)}, u32[]{:S(2)}) collective-permute-start(bf16[8,64,768]{2,1,0:T(8,128)(2,1)S(1)} %all-to-all-done.3.refs_0_), channel_id=1, source_target_pairs={{0,8},{8,0},{16,24},{24,16},{1,9},{9,1},{17,25},{25,17},{2,10},{10... | collective-permute-start | bytes 2359304 | tf_op jit(solution)/shard_map/ppermute | solution.py:29
  368.0 30.2 %collective-permute-start.29 = (bf16[8,64,768]{2,1,0:T(8,128)(2,1)S(1)}, bf16[8,64,768]{2,1,0:T(8,128)(2,1)}, u32[]{:S(2)}, u32[]{:S(2)}) collective-permute-start(bf16[8,64,768]{2,1,0:T(8,128)(2,1)S(1)} %all-to-all-done.3.refs_0_), channel_id=1, source_target_pairs={{0,16},{8,24},{16,0},{24,8},{1,17},{9,25},{17,1},{25,9},{2,18},{10... | collective-permute-start | bytes 2359304 | tf_op jit(solution)/shard_map/ppermute | solution.py:29
  370.4 16.2 %copy-start.68 = (s32[32]{0:T(128)S(1)}, s32[32]{0:T(128)}, u32[]{:S(2)}) copy-start(s32[32]{0:T(128)} %param.26) | copy-start | bytes 388
  372.3 24.7 %collective-permute-start.30 = (bf16[8,32,1024]{2,1,0:T(8,128)(2,1)}, bf16[8,32,1024]{2,1,0:T(8,128)(2,1)}, u32[]{:S(2)}, u32[]{:S(2)}) collective-permute-start(bf16[8,32,1024]{2,1,0:T(8,128)(2,1)} %slice.92), channel_id=1, source_target_pairs={{0,8},{8,0},{16,24},{24,16},{1,9},{9,1},{17,25},{25,17},{2,10},{10... | collective-permute-start | bytes 1572872 | tf_op jit(solution)/shard_map/ppermute | solution.py:29
  372.9 25.3 %collective-permute-start.31 = (bf16[8,32,1024]{2,1,0:T(8,128)(2,1)}, bf16[8,32,1024]{2,1,0:T(8,128)(2,1)}, u32[]{:S(2)}, u32[]{:S(2)}) collective-permute-start(bf16[8,32,1024]{2,1,0:T(8,128)(2,1)} %slice.93), channel_id=1, source_target_pairs={{0,16},{8,24},{16,0},{24,8},{1,17},{9,25},{17,1},{25,9},{2,18},{10... | collective-permute-start | bytes 1572872 | tf_op jit(solution)/shard_map/ppermute | solution.py:29
  382.5 12.4 %all-to-all-start.4 = ((f32[8,1,6148]{2,1,0:T(1,128)}), f32[8,1,6148]{2,1,0:T(1,128)}, u32[]{:S(2)}, u32[]{:S(2)}) async-start(f32[8,1,6148]{2,1,0:T(1,128)} %broadcast_in_dim.57), calls=%async_computation.4 | async-start | bytes 401408 | tf_op jit(solution)/shard_map/all_to_all | solution.py:647
  400.3 20.4 %collective-permute-start.32 = (bf16[8,32,768]{2,1,0:T(8,128)(2,1)S(1)}, bf16[8,32,768]{2,1,0:T(8,128)(2,1)S(1)}, u32[]{:S(2)}, u32[]{:S(2)}) collective-permute-start(bf16[8,32,768]{2,1,0:T(8,128)(2,1)S(1)} %slice.94), channel_id=1, source_target_pairs={{0,8},{8,0},{16,24},{24,16},{1,9},{9,1},{17,25},{25,17},{2,10},{10... | collective-permute-start | bytes 1179656 | tf_op jit(solution)/shard_map/ppermute | solution.py:29
  400.9 19.8 %collective-permute-start.33 = (bf16[8,32,768]{2,1,0:T(8,128)(2,1)S(1)}, bf16[8,32,768]{2,1,0:T(8,128)(2,1)S(1)}, u32[]{:S(2)}, u32[]{:S(2)}) collective-permute-start(bf16[8,32,768]{2,1,0:T(8,128)(2,1)S(1)} %slice.95), channel_id=1, source_target_pairs={{0,16},{8,24},{16,0},{24,8},{1,17},{9,25},{17,1},{25,9},{2,18},{10... | collective-permute-start | bytes 1179656 | tf_op jit(solution)/shard_map/ppermute | solution.py:29
  409.8 16.4 %copy-start.64 = (f32[1,2,8,128]{3,1,2,0:T(2,128)}, f32[1,2,8,128]{3,1,2,0:T(2,128)S(1)}, u32[]{:S(2)}) copy-start(f32[1,2,8,128]{3,1,2,0:T(2,128)S(1)} %copy.44) | copy-start | bytes 24580
  (65 other events, 288.4 us)
Sparse Core Ops, SparseCore 0:
  43.8 62.6 all-gather.2
  108.1 45.9 all-gather.4
  208.5 50.3 reduce-scatter.2
  323.2 61.8 reduce-scatter.4

commit v4 on v3

--- a/solution.py
+++ b/solution.py
@@ -150,12 +150,16 @@
     )(attended, dense, activated, down)
 
 
-def input_kernel(joined, qkv, upward, up, tokens, stats, out, sums):
+def input_kernel(joined, qkv, upward, up, tokens, stats, out, sums, up_sum):
     total = nt(joined[...], qkv[...]) + nt(upward[...], up[...])
     out[...] = total.astype(BF16)
     xhat = (tokens[...].astype(F32) - stats[:, 0:1]) * stats[:, 1:2]
     sums[0:1, :] = jnp.sum(total * xhat, axis=0, keepdims=True)
     sums[1:2, :] = jnp.sum(total, axis=0, keepdims=True)
+
+    @pl.when(pl.program_id(0) == 0)
+    def _():
+        up_sum[...] = jnp.sum(upward[...].astype(F32), axis=0, keepdims=True)
 
 
 def input_part(joined, qkv, upward, up, tokens, stats):
@@ -170,6 +174,7 @@
         out_shape=[
             jax.ShapeDtypeStruct((count, width), BF16),
             jax.ShapeDtypeStruct((2, width), F32),
+            jax.ShapeDtypeStruct((1, upward.shape[1]), F32),
         ],
         grid=(width // block,),
         in_specs=[
@@ -180,7 +185,11 @@
             pl.BlockSpec((count, block), column),
             pl.BlockSpec(stats.shape, fixed),
         ],
-        out_specs=[pl.BlockSpec((count, block), column), pl.BlockSpec((2, block), column)],
+        out_specs=[
+            pl.BlockSpec((count, block), column),
+            pl.BlockSpec((2, block), column),
+            pl.BlockSpec((1, upward.shape[1]), fixed),
+        ],
         compiler_params=pltpu.CompilerParams(vmem_limit_bytes=VMEM),
         cost_estimate=LIGHT,
     )(joined, qkv, upward, up, tokens, stats)
@@ -218,40 +227,90 @@
     )(tokens, cotangent, branch, grad, gain[None], bias[None])
 
 
-def clip_kernel(heads, head_dim, maxima, limits, weight, bias, out, bias_out):
+def clip_kernel(own_heads, head_dim, tops, limits, weight, bias, out, bias_out):
+    parts = tops.shape[0]
+    heads = parts * own_heads
     first = lax.rem(pl.program_id(0) * (out.shape[1] // head_dim), heads)
-    factor = limits[...] / jnp.maximum(maxima[...], limits[...])
-    lane = lax.broadcasted_iota(jnp.int32, (1, heads), 1)
+    lane = lax.broadcasted_iota(jnp.int32, (1, LANES), 1)
     head = first + lax.broadcasted_iota(jnp.int32, (1, out.shape[1]), 1) // head_dim
     scale = jnp.zeros((1, out.shape[1]), F32)
-    for h in range(heads):
-        one = jnp.sum(jnp.where(lane == h, factor, 0.0), axis=1, keepdims=True)
-        scale = jnp.where(head == h, jnp.sqrt(one), scale)
+    for part in range(parts):
+        limit = limits[part : part + 1, :]
+        factor = jnp.sqrt(limit / jnp.maximum(tops[part], limit))
+        for h in range(own_heads):
+            one = jnp.sum(jnp.where(lane == h, factor, 0.0), axis=1, keepdims=True)
+            scale = jnp.where(head == part * own_heads + h, one, scale)
     out[...] = weight[...].astype(F32) * scale
     bias_out[...] = bias[...] * scale
 
 
-def clip_columns(weight, bias, maxima, limits, head_dim):
-    rows, heads = weight.shape[0], maxima.shape[0]
-    columns = 2 * heads * head_dim
-    block = heads * head_dim // 2
+def clip_columns(weight, bias, small, limits, own_heads, head_dim):
+    rows, parts = weight.shape[0], small.shape[0]
+    columns = 2 * parts * own_heads * head_dim
+    block = columns // 4
     column = lambda i: (0, i)
-    vector = pl.BlockSpec((1, heads), lambda i: (0, 0))
     wide, thin = pl.BlockSpec((rows, block), column), pl.BlockSpec((1, block), column)
-    out, bias_out = pl.pallas_call(
-        partial(clip_kernel, heads, head_dim),
+    limits = jnp.pad(
+        limits.astype(F32).reshape(parts, own_heads),
+        ((0, 0), (0, LANES - own_heads)),
+        constant_values=1.0,
+    )
+    return pl.pallas_call(
+        partial(clip_kernel, own_heads, head_dim),
         name="clip_columns",
         out_shape=[
             jax.ShapeDtypeStruct((rows, columns), F32),
             jax.ShapeDtypeStruct((1, columns), F32),
         ],
         grid=(columns // block,),
-        in_specs=[vector, vector, wide, thin],
+        in_specs=[
+            pl.BlockSpec((parts, 1, LANES), lambda i: (0, 0, small.shape[2] // LANES - 1)),
+            pl.BlockSpec((parts, LANES), lambda i: (0, 0)),
+            wide,
+            thin,
+        ],
         out_specs=[wide, thin],
         compiler_params=pltpu.CompilerParams(vmem_limit_bytes=VMEM),
         cost_estimate=LIGHT,
-    )(maxima[None], limits.astype(F32)[None], weight, bias[None])
-    return out, bias_out[0]
+    )(small, limits, weight, bias[None])
+
+
+def unpack_kernel(common, own, own_ff, own_heads, small, *outs):
+    *shifts, qkv_bias, up_bias, maxima = outs
+    parts = small.shape[0]
+    width = common // len(shifts)
+    for i, out in enumerate(shifts):
+        total = small[0, :, i * width : (i + 1) * width]
+        for part in range(1, parts):
+            total = total + small[part, :, i * width : (i + 1) * width]
+        out[...] = total
+    lane = lax.broadcasted_iota(jnp.int32, maxima.shape, 1)
+    tops = jnp.zeros(maxima.shape, F32)
+    for part in range(parts):
+        for group in range(3):
+            spot = (group * parts + part) * own
+            qkv_bias[:, spot : spot + own] = small[
+                part, :, common + group * own : common + (group + 1) * own
+            ]
+        start = common + 3 * own
+        up_bias[:, part * own_ff : (part + 1) * own_ff] = small[part, :, start : start + own_ff]
+        for h in range(own_heads):
+            one = small[part, :, start + own_ff + h : start + own_ff + h + 1]
+            tops = jnp.where(lane == part * own_heads + h, one, tops)
+    maxima[...] = tops
+
+
+def unpack(small, common, own, own_ff, own_heads):
+    parts = small.shape[0]
+    shapes = [common // 3] * 3 + [3 * parts * own, parts * own_ff, parts * own_heads]
+    *shifts, qkv_bias, up_bias, maxima = pl.pallas_call(
+        partial(unpack_kernel, common, own, own_ff, own_heads),
+        name="unpack",
+        out_shape=[jax.ShapeDtypeStruct((1, n), F32) for n in shapes],
+        compiler_params=pltpu.CompilerParams(vmem_limit_bytes=VMEM),
+        cost_estimate=LIGHT,
+    )(small)
+    return shifts, qkv_bias, up_bias, maxima
 
 
 def forwarded(received, axis):
@@ -274,15 +333,16 @@
         owner = me ^ offset
         yield first_place(owner), refs[offset], first
         yield 4 + owner, refs[offset], second
-    owner = me ^ 3
-    yield first_place(owner), refs[3], first
-    yield 4 + owner, refs[4], first
+    if len(refs) > 3:
+        owner = me ^ 3
+        yield first_place(owner), refs[3], first
+        yield 4 + owner, refs[4], first
 
 
 def place_rows(index_ref, *refs):
     out = refs[-1]
     blocks, size, width = refs[0].shape
-    for spot, ref, cut in pieces_of(index_ref, refs, size // 2, 1):
+    for spot, ref, cut in pieces_of(index_ref, refs[:-1], size // 2, 1):
         rows = pl.ds(pl.multiple_of(spot * (size // 2), size // 2), size // 2)
         for i in range(blocks):
             out[rows, i * width : (i + 1) * width] = ref[(i,) + cut[1:]].astype(out.dtype)
@@ -291,7 +351,7 @@
 def place_columns(index_ref, *refs):
     out = refs[-1]
     eighth = refs[0].shape[1] // 2
-    for spot, ref, cut in pieces_of(index_ref, refs, eighth, 1):
+    for spot, ref, cut in pieces_of(index_ref, refs[:-1], eighth, 1):
         columns = pl.ds(pl.multiple_of(spot * eighth, eighth), eighth)
         out[:, columns] = ref[cut].astype(out.dtype)
 
@@ -306,7 +366,7 @@
             num_scalar_prefetch=1,
             grid=grid,
             in_specs=[pl.BlockSpec(in_block, in_map)] * 3
-            + [pl.BlockSpec(tuple(half), in_map)] * 2,
+            + [pl.BlockSpec(tuple(half), in_map)] * (len(parts) - 3),
             out_specs=pl.BlockSpec(out_block, out_map),
         ),
         compiler_params=pltpu.CompilerParams(vmem_limit_bytes=VMEM),
@@ -655,6 +715,7 @@
     u_near = along_both((u, u))
     q = exchange(q)
     u_far = along_both(forwarded(u_near, 1))
+    q, u_far = lax.optimization_barrier((q, u_far))
     q_near = along_both((q, q))
     return q, q_near, u, u_near, u_far
 
@@ -702,6 +763,7 @@
     scale = head_dim ** (-0.5)
 
     shared = lax.axis_size("dp") == 4
+    cotangent_sum = jnp.sum(cotangent.astype(F32), axis=(0, 1))[None]
     digits = jnp.stack([positions // 32, positions % 32], axis=-1)
     marked = jnp.concatenate(
         [tokens, jnp.pad(digits.astype(BF16), ((0, 0), (0, 0), (0, LANES - 2)))], axis=-1
@@ -709,7 +771,8 @@
     if shared:
         q, q_near, u, u_near, u_far = gather_weights(qkv_weight, up_weight)
         up_columns = full_rows(four_parts(u, u_near, u_far), own_rows)
-        q_far = along_both(forwarded(q_near, 1))
+        q_send = forwarded(after(q_near, up_columns), 1)
+        q_far = along_both(q_send)
         marked = after(marked, u)
     else:
         q, u = exchange(to_columns(qkv_weight, 3)), exchange(to_columns(up_weight, 1))
@@ -718,13 +781,15 @@
     grad_rows = lax.all_gather(
         after(cotangent, marked), "ctx", axis=1, tiled=True
     ).reshape(count, width)
+    if shared:
+        all_tokens = after(all_tokens, q_send)
     hidden, stats = normalize(all_tokens, norm_gain, norm_bias)
-    if shared:
-        q_far = after(q_far, up_columns, hidden)
-        qkv_columns = full_rows(four_parts(q, q_near, q_far), own_rows)
     digits = all_tokens[:, width : width + 2].astype(F32)
     places = (digits[:, 0] * 32.0 + digits[:, 1]).reshape(seqs, length)
     tables = [rotary_lanes(places[s]) for s in range(seqs)]
+    if shared:
+        q_far = after(q_far, hidden, tables)
+        qkv_columns = full_rows(four_parts(q, q_near, q_far), own_rows)
 
     qkv_own_bias = take(qkv_bias.reshape(3, parts, own), part, 1, 1).reshape(1, 3 * own)
     up_own_bias = take(up_bias, part * own_ff, own_ff, 0)
@@ -738,8 +803,8 @@
         for s in range(seqs)
     ]
     attended = jnp.concatenate([a[4] for a in ahead])
-    own_maxima = jnp.max(jnp.stack([a[6][0, :own_heads] for a in ahead]), axis=0)
-    upward = dot(hidden, up_columns, (1, 0)) + up_own_bias
+    own_maxima = jnp.max(jnp.stack([a[6] for a in ahead]), axis=0)
+    upward = dot(after(hidden, attended), up_columns, (1, 0)) + up_own_bias
     activated, gelu_back = jax.vjp(partial(jax.nn.gelu, approximate=True), upward)
     activated = activated.astype(BF16)
 
@@ -769,17 +834,9 @@
             tiled=True,
         ).reshape(rows, width)
 
-    def own_sums(joined_sum, up_low):
-        return jnp.concatenate(
-            [
-                joined_sum[0],
-                jnp.sum(up_low.astype(F32), axis=0),
-                jnp.sum(take(grad_rows, part * own, own, 1).astype(F32), axis=0),
-            ]
-        )
-
-    def small_sums(shifts, mine):
-        return jnp.concatenate([shifts.reshape(2 * width), mine])[None], own_maxima[None]
+    def small_sums(shifts, joined_sum, up_sum):
+        everyone = [shifts.reshape(1, 2 * width), cotangent_sum]
+        return jnp.concatenate(everyone + [joined_sum, up_sum], axis=1), own_maxima
 
     def finish_rows(branch_sum, hidden_grad):
         return finish(
@@ -800,10 +857,6 @@
     def spread(small):
         value = jnp.concatenate(small, axis=1)
         return exchange(jnp.broadcast_to(value[None], (parts,) + value.shape))
-
-    def clip(small):
-        head_maxima = small[:, 0, small.shape[2] - own_heads :].reshape(heads)
-        return head_maxima, clip_columns(qkv_weight, qkv_bias, head_maxima, clip_limit, head_dim)
 
     grad_rows, attended, activated = lax.optimization_barrier((grad_rows, attended, activated))
     mixed_out = jnp.concatenate([attended, activated], axis=1)
@@ -827,19 +880,17 @@
         u_send, o_got = together((u_send, o_got))
         u_got = along_both(u_send)
         o_part = second_sums(o_keep, o_got, 1)
-        hidden_part, shifts = input_part(
+        hidden_part, shifts, up_sum = input_part(
             after(joined_low, o_part), qkv_columns, up_low, up_columns, all_tokens, stats
         )
-        mine = own_sums(joined_sum, after(up_low, qkv_raw))
-        q_got, o_part, shifts, mine = together((q_got, o_part, shifts, mine))
+        small = small_sums(shifts, joined_sum, up_sum)
+        u_part = second_sums(u_keep, after(u_got, shifts), 1)
+        q_got, o_part, small = after((q_got, o_part, small), u_part)
+        u_part = exchange(u_part)
         q_send, q_keep = first_sums(qkv_raw, q_got, 1)
-        small = small_sums(shifts, mine)
-        q_send, u_got, small = together((q_send, u_got, small))
-        u_part = second_sums(u_keep, u_got, 1)
-        u_part, o_part, q_send, small = together((u_part, o_part, q_send, small))
+        q_send, o_part, small = together((q_send, o_part, small))
         q_got = along_both(q_send)
         o_near = along_both((o_part, o_part))
-        u_part = exchange(u_part)
         small = dp_step(small, 1)
         q_got, u_part, o_near, small = together((q_got, u_part, o_near, small))
         hidden_grad = sum_branch(after(hidden_part, u_part))
@@ -856,22 +907,25 @@
         dense_grad = full_columns(o_parts, 0, own, own)
         down_grad = full_columns(o_parts, own, own_ff, own)
         small = spread(after(small, down_grad))
-        q_near, u_far, small, dense_grad, down_grad = together(
-            (q_near, u_far, small, dense_grad, down_grad)
-        )
+        q_near, u_far, small, down_grad = together((q_near, u_far, small, down_grad))
         q_send = forwarded(q_near, 1)
         q_far = along_both(q_send)
-        u_far, branch_sum, hidden_grad = after((u_far, branch_sum, hidden_grad), q_send)
+        u_far, branch_sum, hidden_grad, small = after(
+            (u_far, branch_sum, hidden_grad, small), q_send
+        )
         up_grad = full_grad(four_parts(u_part, u_near, u_far), own_rows, 1)
         ends = finish_rows(branch_sum, hidden_grad)
-        head_maxima, (clipped_weight, clipped_bias) = clip(after(small, q_send))
-        q_far, up_grad, ends, clipped_weight = together((q_far, up_grad, ends, clipped_weight))
+        clipped = clip_columns(qkv_weight, qkv_bias, small, clip_limit, own_heads, head_dim)
+        vectors = unpack(small, 3 * width, own, own_ff, own_heads)
+        q_far, up_grad, ends, clipped, vectors = together(
+            (q_far, up_grad, ends, clipped, vectors)
+        )
         qkv_grad = full_grad(four_parts(q_part, q_near, q_far), own_rows, 3)
     else:
         up_low, up_raw = feed_forward_back(grad_rows)
         joined_low, joined_sum, qkv_raw = attention_back(grad_rows)
         branch_sum = sum_branch(output_part(attended, dense_weight, activated, down_weight))
-        hidden_part, shifts = input_part(
+        hidden_part, shifts, up_sum = input_part(
             joined_low, qkv_columns, up_low, up_columns, all_tokens, stats
         )
         hidden_grad = sum_branch(hidden_part)
@@ -879,36 +933,30 @@
         dense_grad, down_grad = out_grad[:own], out_grad[own:]
         up_grad = reduce_input_grad(up_raw, own_rows, 1)
         qkv_grad = reduce_input_grad(qkv_raw, own_rows, 3)
-        small = small_sums(shifts, own_sums(joined_sum, up_low))
+        small = small_sums(shifts, joined_sum, up_sum)
         small = spread((lax.psum(small[0], "dp"), lax.pmax(small[1], "dp")))
-        head_maxima, (clipped_weight, clipped_bias) = clip(small)
+        clipped = clip_columns(qkv_weight, qkv_bias, small, clip_limit, own_heads, head_dim)
+        vectors = unpack(small, 3 * width, own, own_ff, own_heads)
         ends = finish_rows(branch_sum, hidden_grad)
     layer_out, tokens_grad = ends
-    shifts = jnp.sum(small[:, 0, : 2 * width], axis=0)
-    both = small[:, 0, 2 * width :]
-    cut = 3 * own + own_ff
-    qkv_bias_grad = (
-        both[:, : 3 * own].reshape(parts, 3, own).transpose(1, 0, 2).reshape(3 * width)
-    )
-    up_bias_grad = both[:, 3 * own : cut].reshape(parts * own_ff)
-    out_bias_grad = both[:, cut : cut + own].reshape(width)
-
+    clipped_weight, clipped_bias = clipped
+    shifts, qkv_bias_grad, up_bias_grad, head_maxima = vectors
     return (
         layer_out.reshape(seqs, stretch, width),
         tokens_grad.reshape(seqs, stretch, width),
-        shifts[:width],
-        shifts[width:],
+        shifts[0].reshape(width),
+        shifts[1].reshape(width),
         qkv_grad,
-        qkv_bias_grad,
+        qkv_bias_grad.reshape(3 * width),
         dense_grad,
-        out_bias_grad,
+        shifts[2].reshape(width),
         up_grad,
-        up_bias_grad,
+        up_bias_grad.reshape(parts * own_ff),
         down_grad,
-        out_bias_grad,
-        head_maxima,
+        shifts[2].reshape(width),
+        head_maxima.reshape(heads),
         clipped_weight,
-        clipped_bias,
+        clipped_bias.reshape(2 * width),
     )
 
 

time: 439 us -> 424 us (0.966)
  blocking collectives: 0 us -> 13.4 us
  local copies, waits for them, and re-layouts: 62.2 us -> 52.7 us
  starting transfers between devices: 61.4 us -> 53.5 us
  other arithmetic: 25 us -> 17.5 us
    all_to_all x5 -> x4, waiting for transfers between devices: 65.8 us -> 45.7 us  [exchange(): lax.all_to_all(blocks, 'ctx', split_axis=0, concat_axis=0, tiled=True)]
    ppermute x34, waiting for transfers between devices: 84.4 us -> 101 us  [swap(): lax.ppermute(value, axis, [(i, i ^ bit) for i in range(lax.axis_size(axis...]
    all_to_all x0 -> x1, blocking collectives: none -> 13.4 us  [exchange(): lax.all_to_all(blocks, 'ctx', split_axis=0, concat_axis=0, tiled=True)]
    all_to_all x5 -> x4, starting transfers between devices: 25.7 us -> 17.7 us  [exchange(): lax.all_to_all(blocks, 'ctx', split_axis=0, concat_axis=0, tiled=True)]
    convert_element_type x6, other arithmetic: 16.3 us -> 11.6 us  [plus(): return (left.astype(F32) + right.astype(F32)).astype(BF16)]
    unnamed x150 -> x176, local copies, waits for them, and re-layouts: 29.6 us -> 29.3 us
  transfers between devices with their start and end apart: 43 -> 42, of which waited for: 13 -> 19; matrix products, arithmetic and copies ran while one was open for 19% -> 15% of each run, Pallas kernels for 18% -> 19%
where the time goes in v4:
time: 424 us; the launch traced here: 419 us
  waiting for transfers between devices  147 us (35%)
  Pallas kernels  83.4 us (20%)
  starting transfers between devices  53.5 us (13%)
  local copies, waits for them, and re-layouts  52.7 us (12%)
  matrix products  36.2 us (9%)
  other arithmetic  17.5 us (4%)
  between operations  15.2 us (4%)
  blocking collectives  13.4 us (3%)
    ppermute x34, waiting for transfers between devices, swap(): lax.ppermute(value, axis, [(i, i ^ bit) for i in range(lax.axis_size(axis...  101 us
    all_to_all x4, waiting for transfers between devices, exchange(): lax.all_to_all(blocks, 'ctx', split_axis=0, concat_axis=0, tiled=True)  45.7 us
    dot_general x7, matrix products, dot(): lax.dot_general(left, right, ((contract[:1], contract[1:]), ((), ())), pr...  36.2 us
    ppermute x34, starting transfers between devices, swap(): lax.ppermute(value, axis, [(i, i ^ bit) for i in range(lax.axis_size(axis...  35.2 us
    unnamed x176, local copies, waits for them, and re-layouts  29.3 us
    pallas_call x6, Pallas kernels, place(): pl.pallas_call(body, out_shape=out_shape, grid_spec=pltpu.PrefetchScalarG...  29.2 us
    all_to_all x4, starting transfers between devices, exchange(): lax.all_to_all(blocks, 'ctx', split_axis=0, concat_axis=0, tiled=True)  17.7 us
    pallas_call x1, Pallas kernels, attend_back(): pl.pallas_call(partial(attend_back_kernel, heads, scale), name='attend_ba...  14.7 us
  transfers between devices with their start and end apart: 42, of which 19 were waited for; matrix products, arithmetic and copies ran while one was open for 15% of the time, Pallas kernels for 19%

profile of v4, /device:TPU:0, one launch (start us, length us, event | category | flops | bytes accessed | tf_op | source)
XLA Modules:
  0.0 419.2 jit_solution(5530877075506395462)
XLA Ops:
  10.7 6.3 %all-to-all-start = ((bf16[8,64,1024]{2,1,0:T(8,128)(2,1)}), bf16[8,64,1024]{2,1,0:T(8,128)(2,1)S(1)}, u32[]{:S(2)}, u32[]{:S(2)}) async-start(bf16[8,64,1024]{2,1,0:T(8,128)(2,1)} %bitcast.60), calls=%async_computation | async-start | bytes 2097152 | tf_op jit(solution)/shard_map/all_to_all | solution.py:707
  21.6 22.0 %all-to-all-done.refs_0_ = bf16[8,64,1024]{2,1,0:T(8,128)(2,1)S(1)} async-done(((bf16[8,64,1024]{2,1,0:T(8,128)(2,1)}), bf16[8,64,1024]{2,1,0:T(8,128)(2,1)S(1)}, u32[]{:S(2)}, u32[]{:S(2)}) %all-to-all-start) | async-done | bytes 1048608 | tf_op jit(solution)/shard_map/all_to_all | solution.py:707
  47.5 3.6 all-to-all-start.1
  51.6 17.5 %collective-permute-done.refs_2_ = bf16[8,64,1024]{2,1,0:T(8,128)(2,1)S(1)} collective-permute-done((bf16[8,64,1024]{2,1,0:T(8,128)(2,1)S(1)}, bf16[8,64,1024]{2,1,0:T(8,128)(2,1)S(1)}, u32[]{:S(2)}, u32[]{:S(2)}) %collective-permute-start) | collective-permute-done | bytes 1048608 | tf_op jit(solution)/shard_map/ppermute | solution.py:29
  71.5 1.9 slice.69
  74.9 18.7 %all-to-all-done.1.refs_0_ = bf16[8,64,768]{2,1,0:T(8,128)(2,1)S(1)} async-done(((bf16[8,64,768]{2,1,0:T(8,128)(2,1)}), bf16[8,64,768]{2,1,0:T(8,128)(2,1)S(1)}, u32[]{:S(2)}, u32[]{:S(2)}) %all-to-all-start.1) | async-done | bytes 786464 | tf_op jit(solution)/shard_map/all_to_all | solution.py:707
  98.0 4.2 %shard_map.253.up = bf16[2048,1024]{1,0:T(8,128)(2,1)S(1)} custom-call(s32[1]{0:T(128)} %bitcast.6.index_ref, bf16[8,64,1024]{2,1,0:T(8,128)(2,1)S(1)} %all-to-all-done.refs_0_, bf16[8,64,1024]{2,1,0:T(8,128)(2,1)} %collective-permute-done.2.refs_1_, bf16[8,64,1024]{2,1,0:T(8,128)(2,1)S(1)} %collective-permute-done.refs_2_, ...), custom_call_target="tpu_custom_call" | custom-call | flops 1 | bytes 1 | tf_op jit(solution)/shard_map/pallas_call | solution.py:362
  102.3 2.0 copy-done.2
  104.3 9.0 %collective-permute-done.4.refs_1_ = bf16[8,64,768]{2,1,0:T(8,128)(2,1)} collective-permute-done((bf16[8,64,768]{2,1,0:T(8,128)(2,1)S(1)}, bf16[8,64,768]{2,1,0:T(8,128)(2,1)}, u32[]{:S(2)}, u32[]{:S(2)}) %collective-permute-start.4) | collective-permute-done | bytes 786464 | tf_op jit(solution)/shard_map/ppermute | solution.py:29
  115.5 1.7 collective-permute-start.6
  117.5 2.3 copy-done
  119.8 3.4 normalize.1
  123.6 2.0 fusion.11
  128.6 4.1 shard_map.254.qkv
  132.7 3.4 fusion.25.joined
  136.2 10.7 %attend.1 = (bf16[1024,256]{1,0:T(8,128)(2,1)S(1)}, bf16[1024,256]{1,0:T(8,128)(2,1)S(1)}, bf16[1024,256]{1,0:T(8,128)(2,1)S(1)}, f32[1024,256]{1,0:T(8,128)S(1)...) custom-call(f32[1024,768]{1,0:T(8,128)S(1)} %fusion.25.joined, ...), custom_call_target="tpu_custom_call" | custom-call | flops 2147483648 | bytes 6815744 | tf_op jit(solution)/shard_map/attend/pallas_call | solution.py:553
  151.9 7.2 %multiply_convert_fusion = (bf16[1024,1024]{1,0:T(8,128)(2,1)}, f32[1024,1024]{1,0:T(8,128)}) fusion(f32[1024]{0:T(1024)S(1)} %copy-done.76, bf16[1024,2048]{1,0:T(8,128)(2,1)S(1)} %get-tuple-element.141, bf16[2048,1024]{1,0:T(8,128)(2,1)S(1)} %copy-done.3), kind=kOutput, calls=%fused_computation.10 | convolution fusion | flops 4305453056 | bytes 14684160 | tf_op jit(solution)/shard_map/dot_general | solution.py:23
  159.2 8.5 %convolution_convert_fusion = bf16[1280,2048]{1,0:T(8,128)(2,1)S(1)} fusion(bf16[1024,2048]{1,0:T(8,128)(2,1)} %bitcast.90, bf16[1024,1024]{1,0:T(8,128)(2,1)} %get-tuple-element.144.activated, bf16[1024,256]{1,0:T(8,128)(2,1)} %copy-done.36), kind=kOutput, calls=%fused_computation | convolution fusion | flops 5376573440 | bytes 12058624 | tf_op jit(solution)/shard_map/dot_general | solution.py:23
  167.7 1.8 constant_dynamic-slice_fusion.16
  172.7 7.1 %fusion.6.upward = bf16[1024,1024]{1,0:T(8,128)(2,1)S(1)} fusion(f32[1024,1024]{1,0:T(8,128)S(1)} %copy-done.85, f32[1024]{0:T(1024)S(1)} %copy-done.76, bf16[1024,2048]{1,0:T(8,128)(2,1)S(1)} %bitcast.91, bf16[1024,2048]{1,0:T(8,128)(2,1)S(1)} %copy-done.7), kind=kOutput, calls=%fused_computation.9 | convolution fusion | flops 4316987392 | bytes 14684160 | tf_op jit(solution)/shard_map/dot_general | solution.py:23
  179.8 4.9 %convolution_convert_fusion.1 = bf16[2048,1024]{1,0:T(8,128)(2,1)S(1)} fusion(bf16[1024,2048]{1,0:T(8,128)(2,1)S(1)} %copy-done.54, bf16[1024,1024]{1,0:T(8,128)(2,1)S(1)} %fusion.6.upward), kind=kOutput, calls=%fused_computation.11 | convolution fusion | flops 4297064448 | bytes 10485760 | tf_op jit(solution)/shard_map/dot_general | solution.py:23
  188.9 8.2 %output_part.1 = bf16[1024,2048]{1,0:T(8,128)(2,1)S(1)} custom-call(bf16[1024,256]{1,0:T(8,128)(2,1)S(1)} %copy-done.37, bf16[256,2048]{1,0:T(8,128)(2,1)S(1)} %copy-done.28, bf16[1024,1024]{1,0:T(8,128)(2,1)S(1)} %copy-done.23, bf16[1024,2048]{1,0:T(8,128)(2,1)S(1)} %copy-done.7), custom_call_target="tpu_custom_call" | custom-call | flops 1 | bytes 1 | tf_op jit(solution)/shard_map/output_part/pallas_call | solution.py:136
  197.1 2.0 copy-done.1
  199.1 2.4 collective-permute-done.8
  202.3 3.6 add_convert_fusion.1
  209.9 14.7 %attend_back.1 = (bf16[1024,768]{1,0:T(8,128)(2,1)S(1)}, f32[1,768]{1,0:T(1,128)S(1)}) custom-call(bf16[1024,256]{1,0:T(8,128)(2,1)S(1)} %copy-done.59, bf16[1024,256]{1,0:T(8,128)(2,1)S(1)} %copy-done.61, bf16[1024,256]{1,0:T(8,128)(2,1)S(1)} %copy-done.63, bf16[1024,256]{1,0:T(8,128)(2,1)S(1)} %copy-done.61, ...), custom_call_target="tpu_custom_call" | custom-call | flops 5368709120 | bytes 5242880 | tf_op jit(solution)/shard_map/attend_back/pallas_call | solution.py:665
  224.6 3.8 convolution_convert_fusion.2
  230.7 2.6 add_convert_fusion.4
  234.3 4.3 %collective-permute-done.15 = bf16[1280,256]{1,0:T(8,128)(2,1)S(1)} collective-permute-done((bf16[1280,256]{1,0:T(8,128)(2,1)S(1)}, bf16[1280,256]{1,0:T(8,128)(2,1)S(1)}, u32[]{:S(2)}, u32[]{:S(2)}) %collective-permute-start.15) | collective-permute-done | bytes 655392 | tf_op jit(solution)/shard_map/ppermute | solution.py:29
  242.1 11.9 %input_part.1 = (bf16[1024,2048]{1,0:T(8,128)(2,1)S(1)}, f32[2,2048]{1,0:T(2,128)S(1)}, f32[1,1024]{1,0:T(1,128)S(1)}) custom-call(bf16[1024,768]{1,0:T(8,128)(2,1)S(1)} %get-tuple-element.159.joined, bf16[2048,768]{1,0:T(8,128)(2,1)S(1)} %shard_map.254.qkv, bf16[1024,1024]{1,0:T(8,128)(2,1)S(1)} %copy-done.20, bf16[2048,1024]{1,0:T(8,128)(2,1)} %copy-done.2, ...), custom_call_target="tpu_custom_call" | custom-call | flops 1 | bytes 1 | tf_op jit(solution)/shard_map/input_part/pallas_call | solution.py:171
  254.1 8.9 %collective-permute-done.16 = bf16[8,32,1024]{2,1,0:T(8,128)(2,1)S(1)} collective-permute-done((bf16[8,32,1024]{2,1,0:T(8,128)(2,1)}, bf16[8,32,1024]{2,1,0:T(8,128)(2,1)S(1)}, u32[]{:S(2)}, u32[]{:S(2)}) %collective-permute-start.16) | collective-permute-done | bytes 524320 | tf_op jit(solution)/shard_map/ppermute | solution.py:29
  270.7 4.2 %all-to-all-start.2 = ((bf16[8,64,1024]{2,1,0:T(8,128)(2,1)}), bf16[8,64,1024]{2,1,0:T(8,128)(2,1)}, u32[]{:S(2)}, u32[]{:S(2)}) async-start(bf16[8,64,1024]{2,1,0:T(8,128)(2,1)} %add_convert_fusion.3), calls=%async_computation.2 | async-start | bytes 2097152 | tf_op jit(solution)/shard_map/all_to_all | solution.py:707
  276.9 27.6 %collective-permute-done.18 = bf16[8,32,768]{2,1,0:T(8,128)(2,1)S(1)} collective-permute-done((bf16[8,32,768]{2,1,0:T(8,128)(2,1)}, bf16[8,32,768]{2,1,0:T(8,128)(2,1)S(1)}, u32[]{:S(2)}, u32[]{:S(2)}) %collective-permute-start.18) | collective-permute-done | bytes 393248 | tf_op jit(solution)/shard_map/ppermute | solution.py:29
  307.3 1.7 collective-permute-start.24
  309.4 2.2 add_convert_fusion.6
  311.6 3.5 all-to-all-start.3
  316.2 1.7 collective-permute-start.26
  317.9 16.4 %collective-permute-done.27 = f32[1,8064]{1,0:T(1,128)S(1)} collective-permute-done((f32[1,8064]{1,0:T(1,128)S(1)}, f32[1,8064]{1,0:T(1,128)S(1)}, u32[]{:S(2)}, u32[]{:S(2)}) %collective-permute-start.27) | collective-permute-done | bytes 32288 | tf_op jit(solution)/shard_map/ppermute | solution.py:29
  334.4 6.8 %collective-permute-done.25.refs_3_ = bf16[1280,256]{1,0:T(8,128)(2,1)S(1)} collective-permute-done((bf16[1280,256]{1,0:T(8,128)(2,1)S(1)}, bf16[1280,256]{1,0:T(8,128)(2,1)S(1)}, u32[]{:S(2)}, u32[]{:S(2)}) %collective-permute-start.25) | collective-permute-done | bytes 655392 | tf_op jit(solution)/shard_map/ppermute | solution.py:29
  343.9 5.0 %all-to-all-done.3.refs_0_ = bf16[8,64,768]{2,1,0:T(8,128)(2,1)S(1)} async-done(((bf16[8,64,768]{2,1,0:T(8,128)(2,1)}), bf16[8,64,768]{2,1,0:T(8,128)(2,1)S(1)}, u32[]{:S(2)}, u32[]{:S(2)}) %all-to-all-start.3) | async-done | bytes 786464 | tf_op jit(solution)/shard_map/all_to_all | solution.py:707
  357.5 5.1 %shard_map.255 = f32[1024,2048]{1,0:T(8,128)} custom-call(s32[1]{0:T(128)} %bitcast.6.index_ref, bf16[1280,512]{1,0:T(8,128)(2,1)} %add_convert_fusion.refs_0_, bf16[1280,512]{1,0:T(8,128)(2,1)S(1)} %collective-permute-done.20.refs_1_, bf16[1280,512]{1,0:T(8,128)(2,1)S(1)} %collective-permute-done.21.refs_2_, bf16[1280,256]{1,0:T(8,128)(2,1)S(1)} %copy-done.12, ...), custom_call_target="tpu_custom_call" | custom-call | flops 1 | bytes 1 | tf_op jit(solution)/shard_map/pallas_call | solution.py:362
  362.7 13.4 %all_to_all.25.tops.small = f32[8,1,8064]{2,1,0:T(1,128)} all-to-all(f32[8,1,8064]{2,1,0:T(1,128)S(1)} %broadcast_in_dim.53), channel_id=1, replica_groups=mesh['dp'=4,'ctx'=8] {'ctx'}, dimensions={0} | all-to-all | bytes 516096 | tf_op jit(solution)/shard_map/all_to_all | solution.py:707
  376.1 3.2 collective-permute-done.30.refs_3_
  387.6 2.4 shard_map.258
  393.8 8.0 %shard_map.256 = f32[256,8192]{1,0:T(8,128)} custom-call(s32[1]{0:T(128)} %bitcast.6.index_ref, bf16[8,64,1024]{2,1,0:T(8,128)(2,1)} %all-to-all-done.2.refs_0_, bf16[8,64,1024]{2,1,0:T(8,128)(2,1)} %collective-permute-done.23.refs_1_, bf16[8,64,1024]{2,1,0:T(8,128)(2,1)} %collective-permute-done.24.refs_2_, bf16[8,32,1024]{2,1,0:T(8,128)(2,1)S(1)} %copy-done.33, ...), custom_call_target="tpu_custom_call" | custom-call | flops 1 | bytes 1 | tf_op jit(solution)/shard_map/pallas_call | solution.py:362
  401.9 2.9 clip_columns.1
  404.8 1.7 finish.1
  406.6 5.3 %shard_map.257 = f32[256,6144]{1,0:T(8,128)} custom-call(s32[1]{0:T(128)} %bitcast.6.index_ref, bf16[8,64,768]{2,1,0:T(8,128)(2,1)S(1)} %all-to-all-done.3.refs_0_, bf16[8,64,768]{2,1,0:T(8,128)(2,1)S(1)} %copy-done.25, bf16[8,64,768]{2,1,0:T(8,128)(2,1)S(1)} %copy-done.27, bf16[8,32,768]{2,1,0:T(8,128)(2,1)} %collective-permute-done.32.refs_3_, ...), custom_call_target="tpu_custom_call" | custom-call | flops 1 | bytes 1 | tf_op jit(solution)/shard_map/pallas_call | solution.py:362
  (297 shorter events, 88.1 us)
Async XLA Ops:
  10.7 32.9 %all-to-all-start = ((bf16[8,64,1024]{2,1,0:T(8,128)(2,1)}), bf16[8,64,1024]{2,1,0:T(8,128)(2,1)S(1)}, u32[]{:S(2)}, u32[]{:S(2)}) async-start(bf16[8,64,1024]{2,1,0:T(8,128)(2,1)} %bitcast.60), calls=%async_computation | async-start | bytes 2097152 | tf_op jit(solution)/shard_map/all_to_all | solution.py:707
  17.0 100.4 %all-gather.3.cloned.1.call-start = ((), (), s32[]{:S(2)}) async-start(), calls=%async_computation.7 | async-start | bytes 5013504 | tf_op jit(solution)/shard_map/all_gather | solution.py:780
  20.6 73.2 %copy-start.48 = (f32[6144]{0:T(1024)S(1)}, f32[6144]{0:T(1024)}, u32[]{:S(2)}) copy-start(f32[6144]{0:T(1024)} %param.19) | copy-start | bytes 73732
  20.6 76.7 %copy-start.5 = (bf16[1,128,2048]{2,1,0:T(8,128)(2,1)S(1)}, bf16[1,128,2048]{2,1,0:T(8,128)(2,1)}, u32[]{:S(2)}) copy-start(bf16[1,128,2048]{2,1,0:T(8,128)(2,1)} %param.27) | copy-start | bytes 1572868
  43.6 115.5 %all-gather.5.cloned.1.call-start = ((), (), s32[]{:S(2)}) async-start(), calls=%async_computation.8 | async-start | bytes 4718592 | tf_op jit(solution)/shard_map/all_gather | solution.py:781
  44.4 24.8 %collective-permute-start = (bf16[8,64,1024]{2,1,0:T(8,128)(2,1)S(1)}, bf16[8,64,1024]{2,1,0:T(8,128)(2,1)S(1)}, u32[]{:S(2)}, u32[]{:S(2)}) collective-permute-start(bf16[8,64,1024]{2,1,0:T(8,128)(2,1)S(1)} %all-to-all-done.refs_0_), channel_id=1, source_target_pairs={{0,16},{8,24},{16,0},{24,8},{1,17},{9,25},{17,1},{25,9},{2,18},{10... | collective-permute-start | bytes 3145736 | tf_op jit(solution)/shard_map/ppermute | solution.py:29
  46.0 25.5 %collective-permute-start.2 = (bf16[8,64,1024]{2,1,0:T(8,128)(2,1)S(1)}, bf16[8,64,1024]{2,1,0:T(8,128)(2,1)}, u32[]{:S(2)}, u32[]{:S(2)}) collective-permute-start(bf16[8,64,1024]{2,1,0:T(8,128)(2,1)S(1)} %all-to-all-done.refs_0_), channel_id=1, source_target_pairs={{0,8},{8,0},{16,24},{24,16},{1,9},{9,1},{17,25},{25,17},{2,10},{10... | collective-permute-start | bytes 3145736 | tf_op jit(solution)/shard_map/ppermute | solution.py:29
  47.5 46.1 %all-to-all-start.1 = ((bf16[8,64,768]{2,1,0:T(8,128)(2,1)}), bf16[8,64,768]{2,1,0:T(8,128)(2,1)S(1)}, u32[]{:S(2)}, u32[]{:S(2)}) async-start(bf16[8,64,768]{2,1,0:T(8,128)(2,1)} %reshape.191), calls=%async_computation.1 | async-start | bytes 1572864 | tf_op jit(solution)/shard_map/all_to_all | solution.py:707
  51.0 339.0 %reduce-scatter.3.cloned.1.call-start = ((), (), s32[]{:S(2)}) async-start(), calls=%async_computation.9 | async-start | bytes 4718592 | tf_op jit(solution)/shard_map/reduce_scatter | solution.py:830
  70.0 23.6 %collective-permute-start.1 = (bf16[8,32,1024]{2,1,0:T(8,128)(2,1)}, bf16[8,32,1024]{2,1,0:T(8,128)(2,1)}, u32[]{:S(2)}, u32[]{:S(2)}) collective-permute-start(bf16[8,32,1024]{2,1,0:T(8,128)(2,1)} %slice.68), channel_id=1, source_target_pairs={{0,8},{8,0},{16,24},{24,16},{1,9},{9,1},{17,25},{25,17},{2,10},{10... | collective-permute-start | bytes 1572872 | tf_op jit(solution)/shard_map/ppermute | solution.py:29
  73.4 20.2 %collective-permute-start.3 = (bf16[8,32,1024]{2,1,0:T(8,128)(2,1)}, bf16[8,32,1024]{2,1,0:T(8,128)(2,1)}, u32[]{:S(2)}, u32[]{:S(2)}) collective-permute-start(bf16[8,32,1024]{2,1,0:T(8,128)(2,1)} %slice.69), channel_id=1, source_target_pairs={{0,16},{8,24},{16,0},{24,8},{1,17},{9,25},{17,1},{25,9},{2,18},{10... | collective-permute-start | bytes 1572872 | tf_op jit(solution)/shard_map/ppermute | solution.py:29
  93.6 19.7 %collective-permute-start.4 = (bf16[8,64,768]{2,1,0:T(8,128)(2,1)S(1)}, bf16[8,64,768]{2,1,0:T(8,128)(2,1)}, u32[]{:S(2)}, u32[]{:S(2)}) collective-permute-start(bf16[8,64,768]{2,1,0:T(8,128)(2,1)S(1)} %all-to-all-done.1.refs_0_), channel_id=1, source_target_pairs={{0,8},{8,0},{16,24},{24,16},{1,9},{9,1},{17,25},{25,17},{2,10},{10... | collective-permute-start | bytes 2359304 | tf_op jit(solution)/shard_map/ppermute | solution.py:29
  93.7 19.7 %collective-permute-start.5 = (bf16[8,64,768]{2,1,0:T(8,128)(2,1)S(1)}, bf16[8,64,768]{2,1,0:T(8,128)(2,1)}, u32[]{:S(2)}, u32[]{:S(2)}) collective-permute-start(bf16[8,64,768]{2,1,0:T(8,128)(2,1)S(1)} %all-to-all-done.1.refs_0_), channel_id=1, source_target_pairs={{0,16},{8,24},{16,0},{24,8},{1,17},{9,25},{17,1},{25,9},{2,18},{10... | collective-permute-start | bytes 2359304 | tf_op jit(solution)/shard_map/ppermute | solution.py:29
  115.5 10.3 %collective-permute-start.6 = (bf16[8,32,768]{2,1,0:T(8,128)(2,1)S(1)}, bf16[8,32,768]{2,1,0:T(8,128)(2,1)S(1)}, u32[]{:S(2)}, u32[]{:S(2)}) collective-permute-start(bf16[8,32,768]{2,1,0:T(8,128)(2,1)S(1)} %slice.53), channel_id=1, source_target_pairs={{0,8},{8,0},{16,24},{24,16},{1,9},{9,1},{17,25},{25,17},{2,10},{10... | collective-permute-start | bytes 1179656 | tf_op jit(solution)/shard_map/ppermute | solution.py:29
  117.2 9.6 %collective-permute-start.7 = (bf16[8,32,768]{2,1,0:T(8,128)(2,1)S(1)}, bf16[8,32,768]{2,1,0:T(8,128)(2,1)S(1)}, u32[]{:S(2)}, u32[]{:S(2)}) collective-permute-start(bf16[8,32,768]{2,1,0:T(8,128)(2,1)S(1)} %slice.54), channel_id=1, source_target_pairs={{0,16},{8,24},{16,0},{24,8},{1,17},{9,25},{17,1},{25,9},{2,18},{10... | collective-permute-start | bytes 1179656 | tf_op jit(solution)/shard_map/ppermute | solution.py:29
  123.2 28.7 %copy-start.53 = (bf16[1024,2048]{1,0:T(8,128)(2,1)}, bf16[1024,2048]{1,0:T(8,128)(2,1)S(1)}, u32[]{:S(2)}) copy-start(bf16[1024,2048]{1,0:T(8,128)(2,1)S(1)} %get-tuple-element.141) | copy-start | bytes 12582916
  169.5 32.0 %collective-permute-start.8 = (bf16[1280,512]{1,0:T(8,128)(2,1)}, bf16[1280,512]{1,0:T(8,128)(2,1)}, u32[]{:S(2)}, u32[]{:S(2)}) collective-permute-start(bf16[1280,512]{1,0:T(8,128)(2,1)} %get-tuple-element.236), channel_id=1, source_target_pairs={{0,8},{8,0},{16,24},{24,16},{1,9},{9,1},{17,25},{25,17},{2,10},{10... | collective-permute-start | bytes 3932168 | tf_op jit(solution)/shard_map/ppermute | solution.py:29
  170.2 32.0 %collective-permute-start.9 = (bf16[1280,512]{1,0:T(8,128)(2,1)}, bf16[1280,512]{1,0:T(8,128)(2,1)}, u32[]{:S(2)}, u32[]{:S(2)}) collective-permute-start(bf16[1280,512]{1,0:T(8,128)(2,1)} %get-tuple-element.235), channel_id=1, source_target_pairs={{0,16},{8,24},{16,0},{24,8},{1,17},{9,25},{17,1},{25,9},{2,18},{10... | collective-permute-start | bytes 3932168 | tf_op jit(solution)/shard_map/ppermute | solution.py:29
  186.2 42.4 %collective-permute-start.10 = (bf16[8,64,1024]{2,1,0:T(8,128)(2,1)}, bf16[8,64,1024]{2,1,0:T(8,128)(2,1)}, u32[]{:S(2)}, u32[]{:S(2)}) collective-permute-start(bf16[8,64,1024]{2,1,0:T(8,128)(2,1)} %get-tuple-element.240), channel_id=1, source_target_pairs={{0,8},{8,0},{16,24},{24,16},{1,9},{9,1},{17,25},{25,17},{2,10},{10... | collective-permute-start | bytes 3145736 | tf_op jit(solution)/shard_map/ppermute | solution.py:29
  187.8 40.8 %collective-permute-start.11 = (bf16[8,64,1024]{2,1,0:T(8,128)(2,1)}, bf16[8,64,1024]{2,1,0:T(8,128)(2,1)}, u32[]{:S(2)}, u32[]{:S(2)}) collective-permute-start(bf16[8,64,1024]{2,1,0:T(8,128)(2,1)} %get-tuple-element.239), channel_id=1, source_target_pairs={{0,16},{8,24},{16,0},{24,8},{1,17},{9,25},{17,1},{25,9},{2,18},{10... | collective-permute-start | bytes 3145736 | tf_op jit(solution)/shard_map/ppermute | solution.py:29
  206.0 32.7 %collective-permute-start.15 = (bf16[1280,256]{1,0:T(8,128)(2,1)S(1)}, bf16[1280,256]{1,0:T(8,128)(2,1)S(1)}, u32[]{:S(2)}, u32[]{:S(2)}) collective-permute-start(bf16[1280,256]{1,0:T(8,128)(2,1)S(1)} %get-tuple-element.250), channel_id=1, source_target_pairs={{0,16},{8,24},{16,0},{24,8},{1,17},{9,25},{17,1},{25,9},{2,18},{10... | collective-permute-start | bytes 1966088 | tf_op jit(solution)/shard_map/ppermute | solution.py:29
  207.1 31.6 %collective-permute-start.14 = (bf16[1280,256]{1,0:T(8,128)(2,1)S(1)}, bf16[1280,256]{1,0:T(8,128)(2,1)S(1)}, u32[]{:S(2)}, u32[]{:S(2)}) collective-permute-start(bf16[1280,256]{1,0:T(8,128)(2,1)S(1)} %get-tuple-element.252), channel_id=1, source_target_pairs={{0,8},{8,0},{16,24},{24,16},{1,9},{9,1},{17,25},{25,17},{2,10},{10... | collective-permute-start | bytes 1966088 | tf_op jit(solution)/shard_map/ppermute | solution.py:29
  228.6 36.5 %collective-permute-start.12 = (bf16[8,64,768]{2,1,0:T(8,128)(2,1)S(1)}, bf16[8,64,768]{2,1,0:T(8,128)(2,1)S(1)}, u32[]{:S(2)}, u32[]{:S(2)}) collective-permute-start(bf16[8,64,768]{2,1,0:T(8,128)(2,1)S(1)} %get-tuple-element.153), channel_id=1, source_target_pairs={{0,8},{8,0},{16,24},{24,16},{1,9},{9,1},{17,25},{25,17},{2,10},{10... | collective-permute-start | bytes 2359304 | tf_op jit(solution)/shard_map/ppermute | solution.py:29
  230.0 35.1 %collective-permute-start.13 = (bf16[8,64,768]{2,1,0:T(8,128)(2,1)S(1)}, bf16[8,64,768]{2,1,0:T(8,128)(2,1)S(1)}, u32[]{:S(2)}, u32[]{:S(2)}) collective-permute-start(bf16[8,64,768]{2,1,0:T(8,128)(2,1)S(1)} %get-tuple-element.154), channel_id=1, source_target_pairs={{0,16},{8,24},{16,0},{24,8},{1,17},{9,25},{17,1},{25,9},{2,18},{10... | collective-permute-start | bytes 2359304 | tf_op jit(solution)/shard_map/ppermute | solution.py:29
  240.1 22.9 %collective-permute-start.16 = (bf16[8,32,1024]{2,1,0:T(8,128)(2,1)}, bf16[8,32,1024]{2,1,0:T(8,128)(2,1)S(1)}, u32[]{:S(2)}, u32[]{:S(2)}) collective-permute-start(bf16[8,32,1024]{2,1,0:T(8,128)(2,1)} %get-tuple-element.165), channel_id=1, source_target_pairs={{0,8},{8,0},{16,24},{24,16},{1,9},{9,1},{17,25},{25,17},{2,10},{10... | collective-permute-start | bytes 1572872 | tf_op jit(solution)/shard_map/ppermute | solution.py:29
  241.4 22.3 %collective-permute-start.17 = (bf16[8,32,1024]{2,1,0:T(8,128)(2,1)S(1)}, bf16[8,32,1024]{2,1,0:T(8,128)(2,1)S(1)}, u32[]{:S(2)}, u32[]{:S(2)}) collective-permute-start(bf16[8,32,1024]{2,1,0:T(8,128)(2,1)S(1)} %get-tuple-element.166), channel_id=1, source_target_pairs={{0,16},{8,24},{16,0},{24,8},{1,17},{9,25},{17,1},{25,9},{2,18},{10... | collective-permute-start | bytes 1572872 | tf_op jit(solution)/shard_map/ppermute | solution.py:29
  267.4 9.5 %collective-permute-start.22 = (f32[1,8064]{1,0:T(1,128)S(1)}, f32[1,8064]{1,0:T(1,128)S(1)}, u32[]{:S(2)}, u32[]{:S(2)}) collective-permute-start(f32[1,8064]{1,0:T(1,128)S(1)} %pad_maximum_fusion.2), channel_id=1, source_target_pairs={{0,8},{8,0},{16,24},{24,16},{1,9},{9,1},{17,25},{25,17},{2,10},{10... | collective-permute-start | bytes 96776 | tf_op jit(solution)/shard_map/ppermute | solution.py:29
  268.4 36.8 %collective-permute-start.20 = (bf16[1280,512]{1,0:T(8,128)(2,1)}, bf16[1280,512]{1,0:T(8,128)(2,1)S(1)}, u32[]{:S(2)}, u32[]{:S(2)}) collective-permute-start(bf16[1280,512]{1,0:T(8,128)(2,1)} %add_convert_fusion.refs_0_), channel_id=1, source_target_pairs={{0,8},{8,0},{16,24},{24,16},{1,9},{9,1},{17,25},{25,17},{2,10},{10... | collective-permute-start | bytes 3932168 | tf_op jit(solution)/shard_map/ppermute | solution.py:29
  269.5 36.6 %collective-permute-start.21 = (bf16[1280,512]{1,0:T(8,128)(2,1)}, bf16[1280,512]{1,0:T(8,128)(2,1)S(1)}, u32[]{:S(2)}, u32[]{:S(2)}) collective-permute-start(bf16[1280,512]{1,0:T(8,128)(2,1)} %add_convert_fusion.refs_0_), channel_id=1, source_target_pairs={{0,16},{8,24},{16,0},{24,8},{1,17},{9,25},{17,1},{25,9},{2,18},{10... | collective-permute-start | bytes 3932168 | tf_op jit(solution)/shard_map/ppermute | solution.py:29
  270.7 35.4 %all-to-all-start.2 = ((bf16[8,64,1024]{2,1,0:T(8,128)(2,1)}), bf16[8,64,1024]{2,1,0:T(8,128)(2,1)}, u32[]{:S(2)}, u32[]{:S(2)}) async-start(bf16[8,64,1024]{2,1,0:T(8,128)(2,1)} %add_convert_fusion.3), calls=%async_computation.2 | async-start | bytes 2097152 | tf_op jit(solution)/shard_map/all_to_all | solution.py:707
  274.9 115.1 %reduce-scatter.5.cloned.1.call-start = ((), (), s32[]{:S(2)}) async-start(), calls=%async_computation.10 | async-start | bytes 4718592 | tf_op jit(solution)/shard_map/reduce_scatter | solution.py:830
  275.0 29.5 %collective-permute-start.18 = (bf16[8,32,768]{2,1,0:T(8,128)(2,1)}, bf16[8,32,768]{2,1,0:T(8,128)(2,1)S(1)}, u32[]{:S(2)}, u32[]{:S(2)}) collective-permute-start(bf16[8,32,768]{2,1,0:T(8,128)(2,1)} %get-tuple-element.174), channel_id=1, source_target_pairs={{0,8},{8,0},{16,24},{24,16},{1,9},{9,1},{17,25},{25,17},{2,10},{10... | collective-permute-start | bytes 1179656 | tf_op jit(solution)/shard_map/ppermute | solution.py:29
  276.3 29.0 %collective-permute-start.19 = (bf16[8,32,768]{2,1,0:T(8,128)(2,1)}, bf16[8,32,768]{2,1,0:T(8,128)(2,1)S(1)}, u32[]{:S(2)}, u32[]{:S(2)}) collective-permute-start(bf16[8,32,768]{2,1,0:T(8,128)(2,1)} %get-tuple-element.175), channel_id=1, source_target_pairs={{0,16},{8,24},{16,0},{24,8},{1,17},{9,25},{17,1},{25,9},{2,18},{10... | collective-permute-start | bytes 1179656 | tf_op jit(solution)/shard_map/ppermute | solution.py:29
  306.1 37.8 %collective-permute-start.23 = (bf16[8,64,1024]{2,1,0:T(8,128)(2,1)}, bf16[8,64,1024]{2,1,0:T(8,128)(2,1)}, u32[]{:S(2)}, u32[]{:S(2)}) collective-permute-start(bf16[8,64,1024]{2,1,0:T(8,128)(2,1)} %all-to-all-done.2.refs_0_), channel_id=1, source_target_pairs={{0,8},{8,0},{16,24},{24,16},{1,9},{9,1},{17,25},{25,17},{2,10},{10... | collective-permute-start | bytes 3145736 | tf_op jit(solution)/shard_map/ppermute | solution.py:29
  307.3 36.6 %collective-permute-start.24 = (bf16[8,64,1024]{2,1,0:T(8,128)(2,1)}, bf16[8,64,1024]{2,1,0:T(8,128)(2,1)}, u32[]{:S(2)}, u32[]{:S(2)}) collective-permute-start(bf16[8,64,1024]{2,1,0:T(8,128)(2,1)} %all-to-all-done.2.refs_0_), channel_id=1, source_target_pairs={{0,16},{8,24},{16,0},{24,8},{1,17},{9,25},{17,1},{25,9},{2,18},{10... | collective-permute-start | bytes 3145736 | tf_op jit(solution)/shard_map/ppermute | solution.py:29
  309.1 25.3 %collective-permute-start.27 = (f32[1,8064]{1,0:T(1,128)S(1)}, f32[1,8064]{1,0:T(1,128)S(1)}, u32[]{:S(2)}, u32[]{:S(2)}) collective-permute-start(f32[1,8064]{1,0:T(1,128)S(1)} %pad_maximum_fusion.3), channel_id=1, source_target_pairs={{0,16},{8,24},{16,0},{24,8},{1,17},{9,25},{17,1},{25,9},{2,18},{10... | collective-permute-start | bytes 96776 | tf_op jit(solution)/shard_map/ppermute | solution.py:29
  311.6 37.3 %all-to-all-start.3 = ((bf16[8,64,768]{2,1,0:T(8,128)(2,1)}), bf16[8,64,768]{2,1,0:T(8,128)(2,1)S(1)}, u32[]{:S(2)}, u32[]{:S(2)}) async-start(bf16[8,64,768]{2,1,0:T(8,128)(2,1)} %add_convert_fusion.6), calls=%async_computation.3 | async-start | bytes 1572864 | tf_op jit(solution)/shard_map/all_to_all | solution.py:707
  315.2 25.9 %collective-permute-start.25 = (bf16[1280,256]{1,0:T(8,128)(2,1)S(1)}, bf16[1280,256]{1,0:T(8,128)(2,1)S(1)}, u32[]{:S(2)}, u32[]{:S(2)}) collective-permute-start(bf16[1280,256]{1,0:T(8,128)(2,1)S(1)} %slice.60), channel_id=1, source_target_pairs={{0,8},{8,0},{16,24},{24,16},{1,9},{9,1},{17,25},{25,17},{2,10},{10... | collective-permute-start | bytes 1966088 | tf_op jit(solution)/shard_map/ppermute | solution.py:29
  316.2 26.9 %collective-permute-start.26 = (bf16[1280,256]{1,0:T(8,128)(2,1)S(1)}, bf16[1280,256]{1,0:T(8,128)(2,1)S(1)}, u32[]{:S(2)}, u32[]{:S(2)}) collective-permute-start(bf16[1280,256]{1,0:T(8,128)(2,1)S(1)} %slice.61), channel_id=1, source_target_pairs={{0,16},{8,24},{16,0},{24,8},{1,17},{9,25},{17,1},{25,9},{2,18},{10... | collective-permute-start | bytes 1966088 | tf_op jit(solution)/shard_map/ppermute | solution.py:29
  348.9 32.0 %collective-permute-start.28 = (bf16[8,64,768]{2,1,0:T(8,128)(2,1)S(1)}, bf16[8,64,768]{2,1,0:T(8,128)(2,1)S(1)}, u32[]{:S(2)}, u32[]{:S(2)}) collective-permute-start(bf16[8,64,768]{2,1,0:T(8,128)(2,1)S(1)} %all-to-all-done.3.refs_0_), channel_id=1, source_target_pairs={{0,8},{8,0},{16,24},{24,16},{1,9},{9,1},{17,25},{25,17},{2,10},{10... | collective-permute-start | bytes 2359304 | tf_op jit(solution)/shard_map/ppermute | solution.py:29
  349.8 31.1 %collective-permute-start.29 = (bf16[8,64,768]{2,1,0:T(8,128)(2,1)S(1)}, bf16[8,64,768]{2,1,0:T(8,128)(2,1)S(1)}, u32[]{:S(2)}, u32[]{:S(2)}) collective-permute-start(bf16[8,64,768]{2,1,0:T(8,128)(2,1)S(1)} %all-to-all-done.3.refs_0_), channel_id=1, source_target_pairs={{0,16},{8,24},{16,0},{24,8},{1,17},{9,25},{17,1},{25,9},{2,18},{10... | collective-permute-start | bytes 2359304 | tf_op jit(solution)/shard_map/ppermute | solution.py:29
  352.5 32.9 %copy-start.84 = (s32[32]{0:T(128)S(1)}, s32[32]{0:T(128)}, u32[]{:S(2)}) copy-start(s32[32]{0:T(128)} %param.26) | copy-start | bytes 388
  352.5 32.9 %copy-start.73 = (f32[2048]{0:T(1024)S(1)}, f32[2048]{0:T(1024)}, u32[]{:S(2)}) copy-start(f32[2048]{0:T(1024)} %param.21) | copy-start | bytes 24580
  352.5 32.9 %copy-start.74 = (f32[2048]{0:T(1024)S(1)}, f32[2048]{0:T(1024)}, u32[]{:S(2)}) copy-start(f32[2048]{0:T(1024)} %param.25) | copy-start | bytes 24580
  353.6 25.7 %collective-permute-start.30 = (bf16[8,32,1024]{2,1,0:T(8,128)(2,1)S(1)}, bf16[8,32,1024]{2,1,0:T(8,128)(2,1)S(1)}, u32[]{:S(2)}, u32[]{:S(2)}) collective-permute-start(bf16[8,32,1024]{2,1,0:T(8,128)(2,1)S(1)} %slice.64), channel_id=1, source_target_pairs={{0,8},{8,0},{16,24},{24,16},{1,9},{9,1},{17,25},{25,17},{2,10},{10... | collective-permute-start | bytes 1572872 | tf_op jit(solution)/shard_map/ppermute | solution.py:29
  355.0 25.1 %collective-permute-start.31 = (bf16[8,32,1024]{2,1,0:T(8,128)(2,1)S(1)}, bf16[8,32,1024]{2,1,0:T(8,128)(2,1)S(1)}, u32[]{:S(2)}, u32[]{:S(2)}) collective-permute-start(bf16[8,32,1024]{2,1,0:T(8,128)(2,1)S(1)} %slice.65), channel_id=1, source_target_pairs={{0,16},{8,24},{16,0},{24,8},{1,17},{9,25},{17,1},{25,9},{2,18},{10... | collective-permute-start | bytes 1572872 | tf_op jit(solution)/shard_map/ppermute | solution.py:29
  382.7 23.8 %collective-permute-start.32 = (bf16[8,32,768]{2,1,0:T(8,128)(2,1)}, bf16[8,32,768]{2,1,0:T(8,128)(2,1)}, u32[]{:S(2)}, u32[]{:S(2)}) collective-permute-start(bf16[8,32,768]{2,1,0:T(8,128)(2,1)} %slice.66), channel_id=1, source_target_pairs={{0,8},{8,0},{16,24},{24,16},{1,9},{9,1},{17,25},{25,17},{2,10},{10... | collective-permute-start | bytes 1179656 | tf_op jit(solution)/shard_map/ppermute | solution.py:29
  383.7 22.9 %collective-permute-start.33 = (bf16[8,32,768]{2,1,0:T(8,128)(2,1)}, bf16[8,32,768]{2,1,0:T(8,128)(2,1)}, u32[]{:S(2)}, u32[]{:S(2)}) collective-permute-start(bf16[8,32,768]{2,1,0:T(8,128)(2,1)} %slice.67), channel_id=1, source_target_pairs={{0,16},{8,24},{16,0},{24,8},{1,17},{9,25},{17,1},{25,9},{2,18},{10... | collective-permute-start | bytes 1179656 | tf_op jit(solution)/shard_map/ppermute | solution.py:29
  (80 other events, 391.1 us)
Sparse Core Ops, SparseCore 0:
  43.8 64.9 all-gather.2
  110.4 44.7 all-gather.4
  199.2 47.8 reduce-scatter.2
  306.2 61.4 reduce-scatter.4

commit v5 on v4

--- a/solution.py
+++ b/solution.py
@@ -16,6 +16,7 @@
 LANES = 128
 HEAD = 64
 VMEM = 40 << 20
+MOST_VMEM = 58 << 20
 LIGHT = pl.CostEstimate(flops=1, transcendentals=0, bytes_accessed=1)
 
 
@@ -356,7 +357,9 @@
         out[:, columns] = ref[cut].astype(out.dtype)
 
 
-def place(body, parts, axis, grid, in_block, in_map, out_shape, out_block, out_map):
+def place(
+    body, vmem, parts, axis, grid, in_block, in_map, out_shape, out_block, out_map, cost=LIGHT
+):
     half = list(in_block)
     half[axis] //= 2
     return pl.pallas_call(
@@ -369,8 +372,8 @@
             + [pl.BlockSpec(tuple(half), in_map)] * (len(parts) - 3),
             out_specs=pl.BlockSpec(out_block, out_map),
         ),
-        compiler_params=pltpu.CompilerParams(vmem_limit_bytes=VMEM),
-        cost_estimate=LIGHT,
+        compiler_params=pltpu.CompilerParams(vmem_limit_bytes=vmem),
+        cost_estimate=cost,
     )(dp_index(), *parts)
 
 
@@ -378,6 +381,7 @@
     blocks, size, columns = parts[0].shape
     return place(
         place_rows,
+        VMEM,
         parts,
         1,
         (blocks,),
@@ -389,13 +393,14 @@
     )
 
 
-def full_grad(parts, own_rows, groups):
+def full_grad(parts, own_rows, groups, cost=LIGHT):
     blocks, size, columns = parts[0].shape
     width = columns // groups
     several = max(1, min(blocks, 1024 // width))
     steps = blocks // several
     return place(
         place_rows,
+        MOST_VMEM,
         parts,
         1,
         (groups, steps),
@@ -404,6 +409,7 @@
         jax.ShapeDtypeStruct((own_rows, groups * blocks * width), F32),
         (own_rows, several * width),
         lambda g, i, index: (0, g * steps + i),
+        cost,
     )
 
 
@@ -411,6 +417,7 @@
     size = parts[0].shape[1]
     return place(
         place_columns,
+        MOST_VMEM,
         parts,
         1,
         (count // block,),
@@ -553,8 +560,7 @@
     return pl.pallas_call(
         partial(attend_kernel, heads, scale),
         name="attend",
-        out_shape=[jax.ShapeDtypeStruct(s, d) for s, d in shapes]
-        + [jax.ShapeDtypeStruct((1, LANES), F32)],
+        out_shape=[pltpu.HBM(s, d) for s, d in shapes] + [jax.ShapeDtypeStruct((1, LANES), F32)],
         grid_spec=pltpu.PrefetchScalarGridSpec(
             num_scalar_prefetch=0,
             grid=(length // block,),
@@ -886,41 +892,38 @@
         small = small_sums(shifts, joined_sum, up_sum)
         u_part = second_sums(u_keep, after(u_got, shifts), 1)
         q_got, o_part, small = after((q_got, o_part, small), u_part)
-        u_part = exchange(u_part)
         q_send, q_keep = first_sums(qkv_raw, q_got, 1)
-        q_send, o_part, small = together((q_send, o_part, small))
+        u_part = exchange(after(u_part, q_send))
         q_got = along_both(q_send)
+        o_part, small = after((o_part, small), q_send)
         o_near = along_both((o_part, o_part))
         small = dp_step(small, 1)
         q_got, u_part, o_near, small = together((q_got, u_part, o_near, small))
-        hidden_grad = sum_branch(after(hidden_part, u_part))
         u_near = along_both((u_part, u_part))
         o_send = forwarded(o_near, 1)
         q_part = exchange(second_sums(q_keep, q_got, 1))
         o_far = along_both(o_send)
         small = dp_step(small, 2)
         u_near, q_part, o_far, small = together((u_near, q_part, o_far, small))
+        hidden_grad = sum_branch(after(hidden_part, q_part))
         q_near = along_both((q_part, q_part))
         u_send = forwarded(u_near, 1)
         u_far = along_both(u_send)
         o_parts = four_parts(o_part, o_near, after(o_far, u_send))
-        dense_grad = full_columns(o_parts, 0, own, own)
         down_grad = full_columns(o_parts, own, own_ff, own)
         small = spread(after(small, down_grad))
-        q_near, u_far, small, down_grad = together((q_near, u_far, small, down_grad))
+        dense_grad = full_columns(after(o_parts, down_grad), 0, own, own)
+        q_near, u_far, small, dense_grad = together((q_near, u_far, small, dense_grad))
         q_send = forwarded(q_near, 1)
         q_far = along_both(q_send)
-        u_far, branch_sum, hidden_grad, small = after(
-            (u_far, branch_sum, hidden_grad, small), q_send
-        )
+        u_far, small = after((u_far, small), q_send)
         up_grad = full_grad(four_parts(u_part, u_near, u_far), own_rows, 1)
-        ends = finish_rows(branch_sum, hidden_grad)
+        small = after(small, up_grad)
         clipped = clip_columns(qkv_weight, qkv_bias, small, clip_limit, own_heads, head_dim)
         vectors = unpack(small, 3 * width, own, own_ff, own_heads)
-        q_far, up_grad, ends, clipped, vectors = together(
-            (q_far, up_grad, ends, clipped, vectors)
-        )
+        q_far, clipped, vectors = together((q_far, clipped, vectors))
         qkv_grad = full_grad(four_parts(q_part, q_near, q_far), own_rows, 3)
+        ends = finish_rows(*after((branch_sum, hidden_grad), qkv_grad))
     else:
         up_low, up_raw = feed_forward_back(grad_rows)
         joined_low, joined_sum, qkv_raw = attention_back(grad_rows)

time: 424 us -> 413 us (0.974)
  local copies, waits for them, and re-layouts: 52.7 us -> 38.4 us
  blocking collectives: 13.4 us -> 0 us
  waiting for transfers between devices: 147 us -> 156 us
  starting transfers between devices: 53.5 us -> 58.9 us
    unnamed x176 -> x142, local copies, waits for them, and re-layouts: 29.3 us -> 12.6 us
    all_to_all x1 -> x0, blocking collectives: 13.4 us -> none  [exchange(): lax.all_to_all(blocks, 'ctx', split_axis=0, concat_axis=0, tiled=True)]
    all_to_all x4 -> x5, waiting for transfers between devices: 45.7 us -> 52.1 us  [exchange(): lax.all_to_all(blocks, 'ctx', split_axis=0, concat_axis=0, tiled=True)]
    all_to_all x4 -> x5, starting transfers between devices: 17.7 us -> 21.8 us  [exchange(): lax.all_to_all(blocks, 'ctx', split_axis=0, concat_axis=0, tiled=True)]
  transfers between devices with their start and end apart: 42 -> 43, of which waited for: 19 -> 21; matrix products, arithmetic and copies ran while one was open for 15% -> 16% of each run, Pallas kernels for 19% -> 21%
where the time goes in v5:
time: 413 us; the launch traced here: 408 us
  waiting for transfers between devices  156 us (38%)
  Pallas kernels  86 us (21%)
  starting transfers between devices  58.9 us (14%)
  local copies, waits for them, and re-layouts  38.4 us (9%)
  matrix products  36.2 us (9%)
  other arithmetic  17.8 us (4%)
  between operations  15.2 us (4%)
    ppermute x34, waiting for transfers between devices, swap(): lax.ppermute(value, axis, [(i, i ^ bit) for i in range(lax.axis_size(axis...  103 us
    all_to_all x5, waiting for transfers between devices, exchange(): lax.all_to_all(blocks, 'ctx', split_axis=0, concat_axis=0, tiled=True)  52.1 us
    ppermute x34, starting transfers between devices, swap(): lax.ppermute(value, axis, [(i, i ^ bit) for i in range(lax.axis_size(axis...  36.5 us
    dot_general x7, matrix products, dot(): lax.dot_general(left, right, ((contract[:1], contract[1:]), ((), ())), pr...  36.2 us
    pallas_call x6, Pallas kernels, place(): pl.pallas_call(body, out_shape=out_shape, grid_spec=pltpu.PrefetchScalarG...  30.7 us
    all_to_all x5, starting transfers between devices, exchange(): lax.all_to_all(blocks, 'ctx', split_axis=0, concat_axis=0, tiled=True)  21.8 us
    pallas_call x1, Pallas kernels, attend_back(): pl.pallas_call(partial(attend_back_kernel, heads, scale), name='attend_ba...  14.7 us
    unnamed x142, local copies, waits for them, and re-layouts  12.6 us
  transfers between devices with their start and end apart: 43, of which 21 were waited for; matrix products, arithmetic and copies ran while one was open for 16% of the time, Pallas kernels for 21%

profile of v5, /device:TPU:0, one launch (start us, length us, event | category | flops | bytes accessed | tf_op | source)
XLA Modules:
  0.0 408.3 jit_solution(10190861911396139820)
XLA Ops:
  10.7 6.3 %all-to-all-start = ((bf16[8,64,1024]{2,1,0:T(8,128)(2,1)}), bf16[8,64,1024]{2,1,0:T(8,128)(2,1)S(1)}, u32[]{:S(2)}, u32[]{:S(2)}) async-start(bf16[8,64,1024]{2,1,0:T(8,128)(2,1)} %bitcast.60), calls=%async_computation | async-start | bytes 2097152 | tf_op jit(solution)/shard_map/all_to_all | solution.py:713
  21.6 22.0 %all-to-all-done.refs_0_ = bf16[8,64,1024]{2,1,0:T(8,128)(2,1)S(1)} async-done(((bf16[8,64,1024]{2,1,0:T(8,128)(2,1)}), bf16[8,64,1024]{2,1,0:T(8,128)(2,1)S(1)}, u32[]{:S(2)}, u32[]{:S(2)}) %all-to-all-start) | async-done | bytes 1048608 | tf_op jit(solution)/shard_map/all_to_all | solution.py:713
  47.5 3.6 all-to-all-start.1
  51.6 17.5 %collective-permute-done.refs_2_ = bf16[8,64,1024]{2,1,0:T(8,128)(2,1)S(1)} collective-permute-done((bf16[8,64,1024]{2,1,0:T(8,128)(2,1)S(1)}, bf16[8,64,1024]{2,1,0:T(8,128)(2,1)S(1)}, u32[]{:S(2)}, u32[]{:S(2)}) %collective-permute-start) | collective-permute-done | bytes 1048608 | tf_op jit(solution)/shard_map/ppermute | solution.py:30
  71.5 1.9 slice.69
  74.9 18.7 %all-to-all-done.1.refs_0_ = bf16[8,64,768]{2,1,0:T(8,128)(2,1)S(1)} async-done(((bf16[8,64,768]{2,1,0:T(8,128)(2,1)}), bf16[8,64,768]{2,1,0:T(8,128)(2,1)S(1)}, u32[]{:S(2)}, u32[]{:S(2)}) %all-to-all-start.1) | async-done | bytes 786464 | tf_op jit(solution)/shard_map/all_to_all | solution.py:713
  98.0 4.2 %shard_map.253.up = bf16[2048,1024]{1,0:T(8,128)(2,1)S(1)} custom-call(s32[1]{0:T(128)} %bitcast.9.index_ref, bf16[8,64,1024]{2,1,0:T(8,128)(2,1)S(1)} %all-to-all-done.refs_0_, bf16[8,64,1024]{2,1,0:T(8,128)(2,1)} %collective-permute-done.2.refs_1_, bf16[8,64,1024]{2,1,0:T(8,128)(2,1)S(1)} %collective-permute-done.refs_2_, ...), custom_call_target="tpu_custom_call" | custom-call | flops 1 | bytes 1 | tf_op jit(solution)/shard_map/pallas_call | solution.py:365
  102.3 2.0 copy-done.2
  104.3 9.0 %collective-permute-done.4.refs_1_ = bf16[8,64,768]{2,1,0:T(8,128)(2,1)} collective-permute-done((bf16[8,64,768]{2,1,0:T(8,128)(2,1)S(1)}, bf16[8,64,768]{2,1,0:T(8,128)(2,1)}, u32[]{:S(2)}, u32[]{:S(2)}) %collective-permute-start.4) | collective-permute-done | bytes 786464 | tf_op jit(solution)/shard_map/ppermute | solution.py:30
  117.5 2.3 copy-done
  119.8 3.4 normalize.1
  123.7 2.0 fusion.11
  128.6 4.1 %shard_map.254.qkv = bf16[2048,768]{1,0:T(8,128)(2,1)S(1)} custom-call(s32[1]{0:T(128)} %bitcast.9.index_ref, bf16[8,64,768]{2,1,0:T(8,128)(2,1)S(1)} %copy-done.10, bf16[8,64,768]{2,1,0:T(8,128)(2,1)} %collective-permute-done.4.refs_1_, bf16[8,64,768]{2,1,0:T(8,128)(2,1)} %collective-permute-done.5.refs_2_, ...), custom_call_target="tpu_custom_call" | custom-call | flops 1 | bytes 1 | tf_op jit(solution)/shard_map/pallas_call | solution.py:365
  132.8 3.4 fusion.25.joined
  136.2 11.7 %attend.1 = (bf16[1024,256]{1,0:T(8,128)(2,1)}, bf16[1024,256]{1,0:T(8,128)(2,1)}, bf16[1024,256]{1,0:T(8,128)(2,1)}, f32[1024,256]{1,0:T(8,128)}, bf16[1024,256...) custom-call(f32[1024,768]{1,0:T(8,128)S(1)} %fusion.25.joined, f32[1,768]{1,0:T(1,128)S(1)} %bitcast.76, ...), custom_call_target="tpu_custom_call" | custom-call | flops 2147483648 | bytes 6815744 | tf_op jit(solution)/shard_map/attend/pallas_call | solution.py:560
  148.0 7.2 %multiply_convert_fusion = (bf16[1024,1024]{1,0:T(8,128)(2,1)}, f32[1024,1024]{1,0:T(8,128)}) fusion(f32[1024]{0:T(1024)S(1)} %copy-done.59, bf16[1024,2048]{1,0:T(8,128)(2,1)S(1)} %get-tuple-element.140, bf16[2048,1024]{1,0:T(8,128)(2,1)S(1)} %copy-done.3), kind=kOutput, calls=%fused_computation.10 | convolution fusion | flops 4305453056 | bytes 14684160 | tf_op jit(solution)/shard_map/dot_general | solution.py:24
  155.3 8.5 %convolution_convert_fusion = bf16[1280,2048]{1,0:T(8,128)(2,1)S(1)} fusion(bf16[1024,2048]{1,0:T(8,128)(2,1)} %bitcast.90, bf16[1024,1024]{1,0:T(8,128)(2,1)} %get-tuple-element.143.activated, bf16[1024,256]{1,0:T(8,128)(2,1)} %get-tuple-element.145.attended), kind=kOutput, calls=%fused_computation | convolution fusion | flops 5376573440 | bytes 12058624 | tf_op jit(solution)/shard_map/dot_general | solution.py:24
  163.8 1.8 constant_dynamic-slice_fusion.16
  168.8 7.1 %fusion.6.upward = bf16[1024,1024]{1,0:T(8,128)(2,1)S(1)} fusion(f32[1024,1024]{1,0:T(8,128)S(1)} %copy-done.68, f32[1024]{0:T(1024)S(1)} %copy-done.59, bf16[1024,2048]{1,0:T(8,128)(2,1)S(1)} %bitcast.91, bf16[1024,2048]{1,0:T(8,128)(2,1)S(1)} %copy-done.7), kind=kOutput, calls=%fused_computation.9 | convolution fusion | flops 4316987392 | bytes 14684160 | tf_op jit(solution)/shard_map/dot_general | solution.py:24
  175.8 4.9 %convolution_convert_fusion.1 = bf16[2048,1024]{1,0:T(8,128)(2,1)S(1)} fusion(bf16[1024,2048]{1,0:T(8,128)(2,1)S(1)} %copy-done.37, bf16[1024,1024]{1,0:T(8,128)(2,1)S(1)} %fusion.6.upward), kind=kOutput, calls=%fused_computation.11 | convolution fusion | flops 4297064448 | bytes 10485760 | tf_op jit(solution)/shard_map/dot_general | solution.py:24
  185.3 8.2 %output_part.1 = bf16[1024,2048]{1,0:T(8,128)(2,1)S(1)} custom-call(bf16[1024,256]{1,0:T(8,128)(2,1)S(1)} %copy-done.20, bf16[256,2048]{1,0:T(8,128)(2,1)S(1)} %copy-done.16, bf16[1024,1024]{1,0:T(8,128)(2,1)S(1)} %copy-done.15, bf16[1024,2048]{1,0:T(8,128)(2,1)S(1)} %copy-done.7), custom_call_target="tpu_custom_call" | custom-call | flops 1 | bytes 1 | tf_op jit(solution)/shard_map/output_part/pallas_call | solution.py:137
  193.6 2.1 copy-done.1
  195.6 1.9 collective-permute-done.8
  199.0 3.7 add_convert_fusion.1
  206.7 14.7 %attend_back.1 = (bf16[1024,768]{1,0:T(8,128)(2,1)S(1)}, f32[1,768]{1,0:T(1,128)S(1)}) custom-call(bf16[1024,256]{1,0:T(8,128)(2,1)S(1)} %copy-done.40, bf16[1024,256]{1,0:T(8,128)(2,1)S(1)} %copy-done.41, bf16[1024,256]{1,0:T(8,128)(2,1)S(1)} %copy-done.42, bf16[1024,256]{1,0:T(8,128)(2,1)S(1)} %copy-done.41, ...), custom_call_target="tpu_custom_call" | custom-call | flops 5368709120 | bytes 5242880 | tf_op jit(solution)/shard_map/attend_back/pallas_call | solution.py:671
  221.4 3.8 convolution_convert_fusion.2
  227.5 2.6 add_convert_fusion.4
  231.1 2.8 collective-permute-done.12
  236.8 12.0 %input_part.1 = (bf16[1024,2048]{1,0:T(8,128)(2,1)S(1)}, f32[2,2048]{1,0:T(2,128)S(1)}, f32[1,1024]{1,0:T(1,128)S(1)}) custom-call(bf16[1024,768]{1,0:T(8,128)(2,1)S(1)} %get-tuple-element.159.joined, bf16[2048,768]{1,0:T(8,128)(2,1)S(1)} %shard_map.254.qkv, bf16[1024,1024]{1,0:T(8,128)(2,1)S(1)} %copy-done.12, bf16[2048,1024]{1,0:T(8,128)(2,1)} %copy-done.2, ...), custom_call_target="tpu_custom_call" | custom-call | flops 1 | bytes 1 | tf_op jit(solution)/shard_map/input_part/pallas_call | solution.py:172
  250.9 10.4 %collective-permute-done.16 = bf16[8,32,1024]{2,1,0:T(8,128)(2,1)S(1)} collective-permute-done((bf16[8,32,1024]{2,1,0:T(8,128)(2,1)S(1)}, bf16[8,32,1024]{2,1,0:T(8,128)(2,1)S(1)}, u32[]{:S(2)}, u32[]{:S(2)}) %collective-permute-start.16) | collective-permute-done | bytes 524320 | tf_op jit(solution)/shard_map/ppermute | solution.py:30
  271.0 4.3 %all-to-all-start.2 = ((bf16[8,64,1024]{2,1,0:T(8,128)(2,1)}), bf16[8,64,1024]{2,1,0:T(8,128)(2,1)}, u32[]{:S(2)}, u32[]{:S(2)}) async-start(bf16[8,64,1024]{2,1,0:T(8,128)(2,1)} %add_convert_fusion.3), calls=%async_computation.3 | async-start | bytes 2097152 | tf_op jit(solution)/shard_map/all_to_all | solution.py:713
  275.3 4.0 collective-permute-done.18
  280.8 23.8 %collective-permute-done.20.refs_1_ = bf16[1280,512]{1,0:T(8,128)(2,1)S(1)} collective-permute-done((bf16[1280,512]{1,0:T(8,128)(2,1)}, bf16[1280,512]{1,0:T(8,128)(2,1)S(1)}, u32[]{:S(2)}, u32[]{:S(2)}) %collective-permute-start.20) | collective-permute-done | bytes 1310752 | tf_op jit(solution)/shard_map/ppermute | solution.py:30
  308.3 2.4 add_convert_fusion.6
  310.7 4.2 %all-to-all-start.3 = ((bf16[8,64,768]{2,1,0:T(8,128)(2,1)}), bf16[8,64,768]{2,1,0:T(8,128)(2,1)}, u32[]{:S(2)}, u32[]{:S(2)}) async-start(bf16[8,64,768]{2,1,0:T(8,128)(2,1)} %add_convert_fusion.6), calls=%async_computation.4 | async-start | bytes 1572864 | tf_op jit(solution)/shard_map/all_to_all | solution.py:713
  318.1 15.1 %collective-permute-done.27 = f32[1,8064]{1,0:T(1,128)S(1)} collective-permute-done((f32[1,8064]{1,0:T(1,128)S(1)}, f32[1,8064]{1,0:T(1,128)S(1)}, u32[]{:S(2)}, u32[]{:S(2)}) %collective-permute-start.27) | collective-permute-done | bytes 32288 | tf_op jit(solution)/shard_map/ppermute | solution.py:30
  333.2 8.4 %collective-permute-done.25.refs_3_ = bf16[1280,256]{1,0:T(8,128)(2,1)S(1)} collective-permute-done((bf16[1280,256]{1,0:T(8,128)(2,1)S(1)}, bf16[1280,256]{1,0:T(8,128)(2,1)S(1)}, u32[]{:S(2)}, u32[]{:S(2)}) %collective-permute-start.25) | collective-permute-done | bytes 655392 | tf_op jit(solution)/shard_map/ppermute | solution.py:30
  341.5 2.5 collective-permute-done.26.refs_4_
  345.8 1.9 slice.64
  347.6 1.9 collective-permute-start.30
  349.6 1.9 slice.65
  351.9 5.9 %shard_map.255 = f32[1024,2048]{1,0:T(8,128)} custom-call(s32[1]{0:T(128)} %bitcast.9.index_ref, bf16[1280,512]{1,0:T(8,128)(2,1)} %add_convert_fusion.refs_0_, bf16[1280,512]{1,0:T(8,128)(2,1)} %copy-done.44, bf16[1280,512]{1,0:T(8,128)(2,1)} %copy-done.45, bf16[1280,256]{1,0:T(8,128)(2,1)} %copy-done.49, bf16[1280,256]{1,0:T(8,128)(2,1)} %collective-permute-done.26.refs_4_), custom_call_target="tpu_custom_call" | custom-call | flops 1 | bytes 1 | tf_op jit(solution)/shard_map/pallas_call | solution.py:365
  358.7 3.4 all-to-all-start.4
  362.2 2.7 shard_map.256
  364.9 11.3 %all-to-all-done.4.tops.small = f32[8,1,8064]{2,1,0:T(1,128)S(1)} async-done(((f32[8,1,8064]{2,1,0:T(1,128)}), f32[8,1,8064]{2,1,0:T(1,128)S(1)}, u32[]{:S(2)}, u32[]{:S(2)}) %all-to-all-start.4) | async-done | bytes 258080 | tf_op jit(solution)/shard_map/all_to_all | solution.py:713
  379.8 7.7 %shard_map.257 = f32[256,8192]{1,0:T(8,128)} custom-call(s32[1]{0:T(128)} %bitcast.9.index_ref, bf16[8,64,1024]{2,1,0:T(8,128)(2,1)} %all-to-all-done.2.refs_0_, bf16[8,64,1024]{2,1,0:T(8,128)(2,1)} %collective-permute-done.23.refs_1_, bf16[8,64,1024]{2,1,0:T(8,128)(2,1)} %collective-permute-done.24.refs_2_, bf16[8,32,1024]{2,1,0:T(8,128)(2,1)} %copy-done.52, ...), custom_call_target="tpu_custom_call" | custom-call | flops 1 | bytes 1 | tf_op jit(solution)/shard_map/pallas_call | solution.py:365
  388.2 2.9 clip_columns.1
  391.1 6.0 %shard_map.258 = f32[256,6144]{1,0:T(8,128)} custom-call(s32[1]{0:T(128)} %bitcast.9.index_ref, bf16[8,64,768]{2,1,0:T(8,128)(2,1)} %all-to-all-done.3.refs_0_, bf16[8,64,768]{2,1,0:T(8,128)(2,1)} %copy-done.50, bf16[8,64,768]{2,1,0:T(8,128)(2,1)} %copy-done.51, bf16[8,32,768]{2,1,0:T(8,128)(2,1)} %collective-permute-done.32.refs_3_, ...), custom_call_target="tpu_custom_call" | custom-call | flops 1 | bytes 1 | tf_op jit(solution)/shard_map/pallas_call | solution.py:365
  (264 shorter events, 79.3 us)
Async XLA Ops:
  10.7 32.9 %all-to-all-start = ((bf16[8,64,1024]{2,1,0:T(8,128)(2,1)}), bf16[8,64,1024]{2,1,0:T(8,128)(2,1)S(1)}, u32[]{:S(2)}, u32[]{:S(2)}) async-start(bf16[8,64,1024]{2,1,0:T(8,128)(2,1)} %bitcast.60), calls=%async_computation | async-start | bytes 2097152 | tf_op jit(solution)/shard_map/all_to_all | solution.py:713
  17.0 100.4 %all-gather.5.cloned.1.call-start = ((), (), s32[]{:S(2)}) async-start(), calls=%async_computation.8 | async-start | bytes 5013504 | tf_op jit(solution)/shard_map/all_gather | solution.py:786
  20.8 73.0 %copy-start.31 = (f32[6144]{0:T(1024)S(1)}, f32[6144]{0:T(1024)}, u32[]{:S(2)}) copy-start(f32[6144]{0:T(1024)} %param.19) | copy-start | bytes 73732
  20.8 76.5 %copy-start.5 = (bf16[1,128,2048]{2,1,0:T(8,128)(2,1)S(1)}, bf16[1,128,2048]{2,1,0:T(8,128)(2,1)}, u32[]{:S(2)}) copy-start(bf16[1,128,2048]{2,1,0:T(8,128)(2,1)} %param.27) | copy-start | bytes 1572868
  43.7 111.6 %all-gather.3.cloned.1.call-start = ((), (), s32[]{:S(2)}) async-start(), calls=%async_computation.7 | async-start | bytes 4718592 | tf_op jit(solution)/shard_map/all_gather | solution.py:787
  44.4 24.8 %collective-permute-start = (bf16[8,64,1024]{2,1,0:T(8,128)(2,1)S(1)}, bf16[8,64,1024]{2,1,0:T(8,128)(2,1)S(1)}, u32[]{:S(2)}, u32[]{:S(2)}) collective-permute-start(bf16[8,64,1024]{2,1,0:T(8,128)(2,1)S(1)} %all-to-all-done.refs_0_), channel_id=1, source_target_pairs={{0,16},{8,24},{16,0},{24,8},{1,17},{9,25},{17,1},{25,9},{2,18},{10... | collective-permute-start | bytes 3145736 | tf_op jit(solution)/shard_map/ppermute | solution.py:30
  46.0 25.5 %collective-permute-start.2 = (bf16[8,64,1024]{2,1,0:T(8,128)(2,1)S(1)}, bf16[8,64,1024]{2,1,0:T(8,128)(2,1)}, u32[]{:S(2)}, u32[]{:S(2)}) collective-permute-start(bf16[8,64,1024]{2,1,0:T(8,128)(2,1)S(1)} %all-to-all-done.refs_0_), channel_id=1, source_target_pairs={{0,8},{8,0},{16,24},{24,16},{1,9},{9,1},{17,25},{25,17},{2,10},{10... | collective-permute-start | bytes 3145736 | tf_op jit(solution)/shard_map/ppermute | solution.py:30
  47.5 46.1 %all-to-all-start.1 = ((bf16[8,64,768]{2,1,0:T(8,128)(2,1)}), bf16[8,64,768]{2,1,0:T(8,128)(2,1)S(1)}, u32[]{:S(2)}, u32[]{:S(2)}) async-start(bf16[8,64,768]{2,1,0:T(8,128)(2,1)} %reshape.193), calls=%async_computation.1 | async-start | bytes 1572864 | tf_op jit(solution)/shard_map/all_to_all | solution.py:713
  51.1 346.1 %reduce-scatter.3.cloned.1.call-start = ((), (), s32[]{:S(2)}) async-start(), calls=%async_computation.9 | async-start | bytes 4718592 | tf_op jit(solution)/shard_map/reduce_scatter | solution.py:836
  70.0 23.6 %collective-permute-start.1 = (bf16[8,32,1024]{2,1,0:T(8,128)(2,1)}, bf16[8,32,1024]{2,1,0:T(8,128)(2,1)}, u32[]{:S(2)}, u32[]{:S(2)}) collective-permute-start(bf16[8,32,1024]{2,1,0:T(8,128)(2,1)} %slice.68), channel_id=1, source_target_pairs={{0,8},{8,0},{16,24},{24,16},{1,9},{9,1},{17,25},{25,17},{2,10},{10... | collective-permute-start | bytes 1572872 | tf_op jit(solution)/shard_map/ppermute | solution.py:30
  73.4 20.2 %collective-permute-start.3 = (bf16[8,32,1024]{2,1,0:T(8,128)(2,1)}, bf16[8,32,1024]{2,1,0:T(8,128)(2,1)}, u32[]{:S(2)}, u32[]{:S(2)}) collective-permute-start(bf16[8,32,1024]{2,1,0:T(8,128)(2,1)} %slice.69), channel_id=1, source_target_pairs={{0,16},{8,24},{16,0},{24,8},{1,17},{9,25},{17,1},{25,9},{2,18},{10... | collective-permute-start | bytes 1572872 | tf_op jit(solution)/shard_map/ppermute | solution.py:30
  93.6 19.7 %collective-permute-start.4 = (bf16[8,64,768]{2,1,0:T(8,128)(2,1)S(1)}, bf16[8,64,768]{2,1,0:T(8,128)(2,1)}, u32[]{:S(2)}, u32[]{:S(2)}) collective-permute-start(bf16[8,64,768]{2,1,0:T(8,128)(2,1)S(1)} %all-to-all-done.1.refs_0_), channel_id=1, source_target_pairs={{0,8},{8,0},{16,24},{24,16},{1,9},{9,1},{17,25},{25,17},{2,10},{10... | collective-permute-start | bytes 2359304 | tf_op jit(solution)/shard_map/ppermute | solution.py:30
  93.7 19.7 %collective-permute-start.5 = (bf16[8,64,768]{2,1,0:T(8,128)(2,1)S(1)}, bf16[8,64,768]{2,1,0:T(8,128)(2,1)}, u32[]{:S(2)}, u32[]{:S(2)}) collective-permute-start(bf16[8,64,768]{2,1,0:T(8,128)(2,1)S(1)} %all-to-all-done.1.refs_0_), channel_id=1, source_target_pairs={{0,16},{8,24},{16,0},{24,8},{1,17},{9,25},{17,1},{25,9},{2,18},{10... | collective-permute-start | bytes 2359304 | tf_op jit(solution)/shard_map/ppermute | solution.py:30
  98.0 19.5 %copy-start.33 = (f32[2048]{0:T(1024)S(1)}, f32[2048]{0:T(1024)}, u32[]{:S(2)}) copy-start(f32[2048]{0:T(1024)} %param.16) | copy-start | bytes 24580
  98.0 19.5 %copy-start.34 = (f32[2048]{0:T(1024)S(1)}, f32[2048]{0:T(1024)}, u32[]{:S(2)}) copy-start(f32[2048]{0:T(1024)} %param.17) | copy-start | bytes 24580
  115.5 10.3 %collective-permute-start.6 = (bf16[8,32,768]{2,1,0:T(8,128)(2,1)S(1)}, bf16[8,32,768]{2,1,0:T(8,128)(2,1)S(1)}, u32[]{:S(2)}, u32[]{:S(2)}) collective-permute-start(bf16[8,32,768]{2,1,0:T(8,128)(2,1)S(1)} %slice.53), channel_id=1, source_target_pairs={{0,8},{8,0},{16,24},{24,16},{1,9},{9,1},{17,25},{25,17},{2,10},{10... | collective-permute-start | bytes 1179656 | tf_op jit(solution)/shard_map/ppermute | solution.py:30
  117.2 9.6 %collective-permute-start.7 = (bf16[8,32,768]{2,1,0:T(8,128)(2,1)S(1)}, bf16[8,32,768]{2,1,0:T(8,128)(2,1)S(1)}, u32[]{:S(2)}, u32[]{:S(2)}) collective-permute-start(bf16[8,32,768]{2,1,0:T(8,128)(2,1)S(1)} %slice.54), channel_id=1, source_target_pairs={{0,16},{8,24},{16,0},{24,8},{1,17},{9,25},{17,1},{25,9},{2,18},{10... | collective-permute-start | bytes 1179656 | tf_op jit(solution)/shard_map/ppermute | solution.py:30
  123.2 24.8 %copy-start.36 = (bf16[1024,2048]{1,0:T(8,128)(2,1)}, bf16[1024,2048]{1,0:T(8,128)(2,1)S(1)}, u32[]{:S(2)}) copy-start(bf16[1024,2048]{1,0:T(8,128)(2,1)S(1)} %get-tuple-element.140) | copy-start | bytes 12582916
  165.6 31.9 %collective-permute-start.8 = (bf16[1280,512]{1,0:T(8,128)(2,1)}, bf16[1280,512]{1,0:T(8,128)(2,1)}, u32[]{:S(2)}, u32[]{:S(2)}) collective-permute-start(bf16[1280,512]{1,0:T(8,128)(2,1)} %get-tuple-element.240), channel_id=1, source_target_pairs={{0,8},{8,0},{16,24},{24,16},{1,9},{9,1},{17,25},{25,17},{2,10},{10... | collective-permute-start | bytes 3932168 | tf_op jit(solution)/shard_map/ppermute | solution.py:30
  167.0 32.0 %collective-permute-start.9 = (bf16[1280,512]{1,0:T(8,128)(2,1)}, bf16[1280,512]{1,0:T(8,128)(2,1)}, u32[]{:S(2)}, u32[]{:S(2)}) collective-permute-start(bf16[1280,512]{1,0:T(8,128)(2,1)} %get-tuple-element.239), channel_id=1, source_target_pairs={{0,16},{8,24},{16,0},{24,8},{1,17},{9,25},{17,1},{25,9},{2,18},{10... | collective-permute-start | bytes 3932168 | tf_op jit(solution)/shard_map/ppermute | solution.py:30
  182.3 43.1 %collective-permute-start.10 = (bf16[8,64,1024]{2,1,0:T(8,128)(2,1)}, bf16[8,64,1024]{2,1,0:T(8,128)(2,1)}, u32[]{:S(2)}, u32[]{:S(2)}) collective-permute-start(bf16[8,64,1024]{2,1,0:T(8,128)(2,1)} %get-tuple-element.244), channel_id=1, source_target_pairs={{0,8},{8,0},{16,24},{24,16},{1,9},{9,1},{17,25},{25,17},{2,10},{10... | collective-permute-start | bytes 3145736 | tf_op jit(solution)/shard_map/ppermute | solution.py:30
  183.9 41.5 %collective-permute-start.11 = (bf16[8,64,1024]{2,1,0:T(8,128)(2,1)}, bf16[8,64,1024]{2,1,0:T(8,128)(2,1)}, u32[]{:S(2)}, u32[]{:S(2)}) collective-permute-start(bf16[8,64,1024]{2,1,0:T(8,128)(2,1)} %get-tuple-element.243), channel_id=1, source_target_pairs={{0,16},{8,24},{16,0},{24,8},{1,17},{9,25},{17,1},{25,9},{2,18},{10... | collective-permute-start | bytes 3145736 | tf_op jit(solution)/shard_map/ppermute | solution.py:30
  202.8 31.2 %collective-permute-start.12 = (bf16[1280,256]{1,0:T(8,128)(2,1)S(1)}, bf16[1280,256]{1,0:T(8,128)(2,1)S(1)}, u32[]{:S(2)}, u32[]{:S(2)}) collective-permute-start(bf16[1280,256]{1,0:T(8,128)(2,1)S(1)} %get-tuple-element.256), channel_id=1, source_target_pairs={{0,8},{8,0},{16,24},{24,16},{1,9},{9,1},{17,25},{25,17},{2,10},{10... | collective-permute-start | bytes 1966088 | tf_op jit(solution)/shard_map/ppermute | solution.py:30
  203.5 31.9 %collective-permute-start.13 = (bf16[1280,256]{1,0:T(8,128)(2,1)S(1)}, bf16[1280,256]{1,0:T(8,128)(2,1)S(1)}, u32[]{:S(2)}, u32[]{:S(2)}) collective-permute-start(bf16[1280,256]{1,0:T(8,128)(2,1)S(1)} %get-tuple-element.254), channel_id=1, source_target_pairs={{0,16},{8,24},{16,0},{24,8},{1,17},{9,25},{17,1},{25,9},{2,18},{10... | collective-permute-start | bytes 1966088 | tf_op jit(solution)/shard_map/ppermute | solution.py:30
  225.4 38.5 %collective-permute-start.14 = (bf16[8,64,768]{2,1,0:T(8,128)(2,1)S(1)}, bf16[8,64,768]{2,1,0:T(8,128)(2,1)S(1)}, u32[]{:S(2)}, u32[]{:S(2)}) collective-permute-start(bf16[8,64,768]{2,1,0:T(8,128)(2,1)S(1)} %get-tuple-element.162), channel_id=1, source_target_pairs={{0,8},{8,0},{16,24},{24,16},{1,9},{9,1},{17,25},{25,17},{2,10},{10... | collective-permute-start | bytes 2359304 | tf_op jit(solution)/shard_map/ppermute | solution.py:30
  226.7 37.2 %collective-permute-start.15 = (bf16[8,64,768]{2,1,0:T(8,128)(2,1)S(1)}, bf16[8,64,768]{2,1,0:T(8,128)(2,1)S(1)}, u32[]{:S(2)}, u32[]{:S(2)}) collective-permute-start(bf16[8,64,768]{2,1,0:T(8,128)(2,1)S(1)} %get-tuple-element.163), channel_id=1, source_target_pairs={{0,16},{8,24},{16,0},{24,8},{1,17},{9,25},{17,1},{25,9},{2,18},{10... | collective-permute-start | bytes 2359304 | tf_op jit(solution)/shard_map/ppermute | solution.py:30
  248.8 12.5 %collective-permute-start.16 = (bf16[8,32,1024]{2,1,0:T(8,128)(2,1)S(1)}, bf16[8,32,1024]{2,1,0:T(8,128)(2,1)S(1)}, u32[]{:S(2)}, u32[]{:S(2)}) collective-permute-start(bf16[8,32,1024]{2,1,0:T(8,128)(2,1)S(1)} %get-tuple-element.168), channel_id=1, source_target_pairs={{0,8},{8,0},{16,24},{24,16},{1,9},{9,1},{17,25},{25,17},{2,10},{10... | collective-permute-start | bytes 1572872 | tf_op jit(solution)/shard_map/ppermute | solution.py:30
  249.5 13.0 %collective-permute-start.17 = (bf16[8,32,1024]{2,1,0:T(8,128)(2,1)S(1)}, bf16[8,32,1024]{2,1,0:T(8,128)(2,1)S(1)}, u32[]{:S(2)}, u32[]{:S(2)}) collective-permute-start(bf16[8,32,1024]{2,1,0:T(8,128)(2,1)S(1)} %copy-done.54), channel_id=1, source_target_pairs={{0,16},{8,24},{16,0},{24,8},{1,17},{9,25},{17,1},{25,9},{2,18},{10... | collective-permute-start | bytes 1572872 | tf_op jit(solution)/shard_map/ppermute | solution.py:30
  266.3 9.0 %collective-permute-start.22 = (f32[1,8064]{1,0:T(1,128)S(1)}, f32[1,8064]{1,0:T(1,128)S(1)}, u32[]{:S(2)}, u32[]{:S(2)}) collective-permute-start(f32[1,8064]{1,0:T(1,128)S(1)} %pad_maximum_fusion.2), channel_id=1, source_target_pairs={{0,8},{8,0},{16,24},{24,16},{1,9},{9,1},{17,25},{25,17},{2,10},{10... | collective-permute-start | bytes 96776 | tf_op jit(solution)/shard_map/ppermute | solution.py:30
  267.0 12.4 %collective-permute-start.18 = (bf16[8,32,768]{2,1,0:T(8,128)(2,1)}, bf16[8,32,768]{2,1,0:T(8,128)(2,1)}, u32[]{:S(2)}, u32[]{:S(2)}) collective-permute-start(bf16[8,32,768]{2,1,0:T(8,128)(2,1)} %get-tuple-element.264), channel_id=1, source_target_pairs={{0,8},{8,0},{16,24},{24,16},{1,9},{9,1},{17,25},{25,17},{2,10},{10... | collective-permute-start | bytes 1179656 | tf_op jit(solution)/shard_map/ppermute | solution.py:30
  268.4 12.4 %collective-permute-start.19 = (bf16[8,32,768]{2,1,0:T(8,128)(2,1)}, bf16[8,32,768]{2,1,0:T(8,128)(2,1)}, u32[]{:S(2)}, u32[]{:S(2)}) collective-permute-start(bf16[8,32,768]{2,1,0:T(8,128)(2,1)} %get-tuple-element.262), channel_id=1, source_target_pairs={{0,16},{8,24},{16,0},{24,8},{1,17},{9,25},{17,1},{25,9},{2,18},{10... | collective-permute-start | bytes 1179656 | tf_op jit(solution)/shard_map/ppermute | solution.py:30
  269.9 34.7 %collective-permute-start.20 = (bf16[1280,512]{1,0:T(8,128)(2,1)}, bf16[1280,512]{1,0:T(8,128)(2,1)S(1)}, u32[]{:S(2)}, u32[]{:S(2)}) collective-permute-start(bf16[1280,512]{1,0:T(8,128)(2,1)} %add_convert_fusion.refs_0_), channel_id=1, source_target_pairs={{0,8},{8,0},{16,24},{24,16},{1,9},{9,1},{17,25},{25,17},{2,10},{10... | collective-permute-start | bytes 3932168 | tf_op jit(solution)/shard_map/ppermute | solution.py:30
  270.4 35.0 %collective-permute-start.21 = (bf16[1280,512]{1,0:T(8,128)(2,1)}, bf16[1280,512]{1,0:T(8,128)(2,1)S(1)}, u32[]{:S(2)}, u32[]{:S(2)}) collective-permute-start(bf16[1280,512]{1,0:T(8,128)(2,1)} %add_convert_fusion.refs_0_), channel_id=1, source_target_pairs={{0,16},{8,24},{16,0},{24,8},{1,17},{9,25},{17,1},{25,9},{2,18},{10... | collective-permute-start | bytes 3932168 | tf_op jit(solution)/shard_map/ppermute | solution.py:30
  271.0 34.4 %all-to-all-start.2 = ((bf16[8,64,1024]{2,1,0:T(8,128)(2,1)}), bf16[8,64,1024]{2,1,0:T(8,128)(2,1)}, u32[]{:S(2)}, u32[]{:S(2)}) async-start(bf16[8,64,1024]{2,1,0:T(8,128)(2,1)} %add_convert_fusion.3), calls=%async_computation.3 | async-start | bytes 2097152 | tf_op jit(solution)/shard_map/all_to_all | solution.py:713
  305.4 38.6 %collective-permute-start.23 = (bf16[8,64,1024]{2,1,0:T(8,128)(2,1)}, bf16[8,64,1024]{2,1,0:T(8,128)(2,1)}, u32[]{:S(2)}, u32[]{:S(2)}) collective-permute-start(bf16[8,64,1024]{2,1,0:T(8,128)(2,1)} %all-to-all-done.2.refs_0_), channel_id=1, source_target_pairs={{0,8},{8,0},{16,24},{24,16},{1,9},{9,1},{17,25},{25,17},{2,10},{10... | collective-permute-start | bytes 3145736 | tf_op jit(solution)/shard_map/ppermute | solution.py:30
  306.1 37.9 %collective-permute-start.24 = (bf16[8,64,1024]{2,1,0:T(8,128)(2,1)}, bf16[8,64,1024]{2,1,0:T(8,128)(2,1)}, u32[]{:S(2)}, u32[]{:S(2)}) collective-permute-start(bf16[8,64,1024]{2,1,0:T(8,128)(2,1)} %all-to-all-done.2.refs_0_), channel_id=1, source_target_pairs={{0,16},{8,24},{16,0},{24,8},{1,17},{9,25},{17,1},{25,9},{2,18},{10... | collective-permute-start | bytes 3145736 | tf_op jit(solution)/shard_map/ppermute | solution.py:30
  307.7 25.4 %collective-permute-start.27 = (f32[1,8064]{1,0:T(1,128)S(1)}, f32[1,8064]{1,0:T(1,128)S(1)}, u32[]{:S(2)}, u32[]{:S(2)}) collective-permute-start(f32[1,8064]{1,0:T(1,128)S(1)} %pad_maximum_fusion.3), channel_id=1, source_target_pairs={{0,16},{8,24},{16,0},{24,8},{1,17},{9,25},{17,1},{25,9},{2,18},{10... | collective-permute-start | bytes 96776 | tf_op jit(solution)/shard_map/ppermute | solution.py:30
  310.7 33.3 %all-to-all-start.3 = ((bf16[8,64,768]{2,1,0:T(8,128)(2,1)}), bf16[8,64,768]{2,1,0:T(8,128)(2,1)}, u32[]{:S(2)}, u32[]{:S(2)}) async-start(bf16[8,64,768]{2,1,0:T(8,128)(2,1)} %add_convert_fusion.6), calls=%async_computation.4 | async-start | bytes 1572864 | tf_op jit(solution)/shard_map/all_to_all | solution.py:713
  314.9 82.2 %reduce-scatter.5.cloned.1.call-start = ((), (), s32[]{:S(2)}) async-start(), calls=%async_computation.10 | async-start | bytes 4718592 | tf_op jit(solution)/shard_map/reduce_scatter | solution.py:836
  315.0 26.5 %collective-permute-start.25 = (bf16[1280,256]{1,0:T(8,128)(2,1)S(1)}, bf16[1280,256]{1,0:T(8,128)(2,1)S(1)}, u32[]{:S(2)}, u32[]{:S(2)}) collective-permute-start(bf16[1280,256]{1,0:T(8,128)(2,1)S(1)} %slice.60), channel_id=1, source_target_pairs={{0,8},{8,0},{16,24},{24,16},{1,9},{9,1},{17,25},{25,17},{2,10},{10... | collective-permute-start | bytes 1966088 | tf_op jit(solution)/shard_map/ppermute | solution.py:30
  316.4 27.6 %collective-permute-start.26 = (bf16[1280,256]{1,0:T(8,128)(2,1)S(1)}, bf16[1280,256]{1,0:T(8,128)(2,1)}, u32[]{:S(2)}, u32[]{:S(2)}) collective-permute-start(bf16[1280,256]{1,0:T(8,128)(2,1)S(1)} %slice.61), channel_id=1, source_target_pairs={{0,16},{8,24},{16,0},{24,8},{1,17},{9,25},{17,1},{25,9},{2,18},{10... | collective-permute-start | bytes 1966088 | tf_op jit(solution)/shard_map/ppermute | solution.py:30
  344.1 32.2 %collective-permute-start.28 = (bf16[8,64,768]{2,1,0:T(8,128)(2,1)}, bf16[8,64,768]{2,1,0:T(8,128)(2,1)S(1)}, u32[]{:S(2)}, u32[]{:S(2)}) collective-permute-start(bf16[8,64,768]{2,1,0:T(8,128)(2,1)} %all-to-all-done.3.refs_0_), channel_id=1, source_target_pairs={{0,8},{8,0},{16,24},{24,16},{1,9},{9,1},{17,25},{25,17},{2,10},{10... | collective-permute-start | bytes 2359304 | tf_op jit(solution)/shard_map/ppermute | solution.py:30
  344.2 32.1 %collective-permute-start.29 = (bf16[8,64,768]{2,1,0:T(8,128)(2,1)}, bf16[8,64,768]{2,1,0:T(8,128)(2,1)S(1)}, u32[]{:S(2)}, u32[]{:S(2)}) collective-permute-start(bf16[8,64,768]{2,1,0:T(8,128)(2,1)} %all-to-all-done.3.refs_0_), channel_id=1, source_target_pairs={{0,16},{8,24},{16,0},{24,8},{1,17},{9,25},{17,1},{25,9},{2,18},{10... | collective-permute-start | bytes 2359304 | tf_op jit(solution)/shard_map/ppermute | solution.py:30
  347.6 28.6 %collective-permute-start.30 = (bf16[8,32,1024]{2,1,0:T(8,128)(2,1)}, bf16[8,32,1024]{2,1,0:T(8,128)(2,1)S(1)}, u32[]{:S(2)}, u32[]{:S(2)}) collective-permute-start(bf16[8,32,1024]{2,1,0:T(8,128)(2,1)} %slice.64), channel_id=1, source_target_pairs={{0,8},{8,0},{16,24},{24,16},{1,9},{9,1},{17,25},{25,17},{2,10},{10... | collective-permute-start | bytes 1572872 | tf_op jit(solution)/shard_map/ppermute | solution.py:30
  351.4 24.8 %collective-permute-start.31 = (bf16[8,32,1024]{2,1,0:T(8,128)(2,1)}, bf16[8,32,1024]{2,1,0:T(8,128)(2,1)S(1)}, u32[]{:S(2)}, u32[]{:S(2)}) collective-permute-start(bf16[8,32,1024]{2,1,0:T(8,128)(2,1)} %slice.65), channel_id=1, source_target_pairs={{0,16},{8,24},{16,0},{24,8},{1,17},{9,25},{17,1},{25,9},{2,18},{10... | collective-permute-start | bytes 1572872 | tf_op jit(solution)/shard_map/ppermute | solution.py:30
  358.7 17.5 %all-to-all-start.4 = ((f32[8,1,8064]{2,1,0:T(1,128)}), f32[8,1,8064]{2,1,0:T(1,128)S(1)}, u32[]{:S(2)}, u32[]{:S(2)}) async-start(f32[8,1,8064]{2,1,0:T(1,128)} %broadcast_in_dim.53), calls=%async_computation.6 | async-start | bytes 516096 | tf_op jit(solution)/shard_map/all_to_all | solution.py:713
  377.2 13.9 %collective-permute-start.32 = (bf16[8,32,768]{2,1,0:T(8,128)(2,1)}, bf16[8,32,768]{2,1,0:T(8,128)(2,1)}, u32[]{:S(2)}, u32[]{:S(2)}) collective-permute-start(bf16[8,32,768]{2,1,0:T(8,128)(2,1)} %slice.66), channel_id=1, source_target_pairs={{0,8},{8,0},{16,24},{24,16},{1,9},{9,1},{17,25},{25,17},{2,10},{10... | collective-permute-start | bytes 1179656 | tf_op jit(solution)/shard_map/ppermute | solution.py:30
  378.0 13.1 %collective-permute-start.33 = (bf16[8,32,768]{2,1,0:T(8,128)(2,1)}, bf16[8,32,768]{2,1,0:T(8,128)(2,1)}, u32[]{:S(2)}, u32[]{:S(2)}) collective-permute-start(bf16[8,32,768]{2,1,0:T(8,128)(2,1)} %slice.67), channel_id=1, source_target_pairs={{0,16},{8,24},{16,0},{24,8},{1,17},{9,25},{17,1},{25,9},{2,18},{10... | collective-permute-start | bytes 1179656 | tf_op jit(solution)/shard_map/ppermute | solution.py:30
  (64 other events, 430.1 us)
Sparse Core Ops, SparseCore 0:
  43.8 64.9 all-gather.4
  110.4 44.7 all-gather.2
  195.8 48.2 reduce-scatter.2
  344.2 52.0 reduce-scatter.4

commit v6 on v5

--- a/solution.py
+++ b/solution.py
@@ -911,15 +911,17 @@
         u_far = along_both(u_send)
         o_parts = four_parts(o_part, o_near, after(o_far, u_send))
         down_grad = full_columns(o_parts, own, own_ff, own)
-        small = spread(after(small, down_grad))
+        small = spread(after(small, u_send))
         dense_grad = full_columns(after(o_parts, down_grad), 0, own, own)
+        small = after(small, dense_grad)
+        clipped = clip_columns(qkv_weight, qkv_bias, small, clip_limit, own_heads, head_dim)
+        small, clipped = together((small, clipped))
         q_near, u_far, small, dense_grad = together((q_near, u_far, small, dense_grad))
         q_send = forwarded(q_near, 1)
         q_far = along_both(q_send)
         u_far, small = after((u_far, small), q_send)
         up_grad = full_grad(four_parts(u_part, u_near, u_far), own_rows, 1)
         small = after(small, up_grad)
-        clipped = clip_columns(qkv_weight, qkv_bias, small, clip_limit, own_heads, head_dim)
         vectors = unpack(small, 3 * width, own, own_ff, own_heads)
         q_far, clipped, vectors = together((q_far, clipped, vectors))
         qkv_grad = full_grad(four_parts(q_part, q_near, q_far), own_rows, 3)

time: 413 us -> 413 us (level)
    all_to_all x5, waiting for transfers between devices: 52.1 us -> 45.9 us  [exchange(): lax.all_to_all(blocks, 'ctx', split_axis=0, concat_axis=0, tiled=True)]
    unnamed x142 -> x138, local copies, waits for them, and re-layouts: 12.6 us -> 13.4 us
  transfers between devices with their start and end apart: 43 -> 43, of which waited for: 21 -> 23; matrix products, arithmetic and copies ran while one was open for 16% -> 16% of each run, Pallas kernels for 21% -> 21%
where the time goes in v6:
time: 413 us; the launch traced here: 407 us
  waiting for transfers between devices  154 us (37%)
  Pallas kernels  85.8 us (21%)
  starting transfers between devices  59.1 us (14%)
  local copies, waits for them, and re-layouts  39.6 us (10%)
  matrix products  36.2 us (9%)
  other arithmetic  17.8 us (4%)
  between operations  15.1 us (4%)
    ppermute x34, waiting for transfers between devices, swap(): lax.ppermute(value, axis, [(i, i ^ bit) for i in range(lax.axis_size(axis...  104 us
    all_to_all x5, waiting for transfers between devices, exchange(): lax.all_to_all(blocks, 'ctx', split_axis=0, concat_axis=0, tiled=True)  45.9 us
    ppermute x34, starting transfers between devices, swap(): lax.ppermute(value, axis, [(i, i ^ bit) for i in range(lax.axis_size(axis...  36.7 us
    dot_general x7, matrix products, dot(): lax.dot_general(left, right, ((contract[:1], contract[1:]), ((), ())), pr...  36.2 us
    pallas_call x6, Pallas kernels, place(): pl.pallas_call(body, out_shape=out_shape, grid_spec=pltpu.PrefetchScalarG...  30.5 us
    all_to_all x5, starting transfers between devices, exchange(): lax.all_to_all(blocks, 'ctx', split_axis=0, concat_axis=0, tiled=True)  21.7 us
    pallas_call x1, Pallas kernels, attend_back(): pl.pallas_call(partial(attend_back_kernel, heads, scale), name='attend_ba...  14.7 us
    unnamed x138, local copies, waits for them, and re-layouts  13.4 us
  transfers between devices with their start and end apart: 43, of which 23 were waited for; matrix products, arithmetic and copies ran while one was open for 16% of the time, Pallas kernels for 21%

profile of v6, /device:TPU:0, one launch (start us, length us, event | category | flops | bytes accessed | tf_op | source)
XLA Modules:
  0.0 407.4 jit_solution(13876940418650431479)
XLA Ops:
  10.7 6.3 %all-to-all-start = ((bf16[8,64,1024]{2,1,0:T(8,128)(2,1)}), bf16[8,64,1024]{2,1,0:T(8,128)(2,1)S(1)}, u32[]{:S(2)}, u32[]{:S(2)}) async-start(bf16[8,64,1024]{2,1,0:T(8,128)(2,1)} %bitcast.60), calls=%async_computation | async-start | bytes 2097152 | tf_op jit(solution)/shard_map/all_to_all | solution.py:713
  21.6 22.0 %all-to-all-done.refs_0_ = bf16[8,64,1024]{2,1,0:T(8,128)(2,1)S(1)} async-done(((bf16[8,64,1024]{2,1,0:T(8,128)(2,1)}), bf16[8,64,1024]{2,1,0:T(8,128)(2,1)S(1)}, u32[]{:S(2)}, u32[]{:S(2)}) %all-to-all-start) | async-done | bytes 1048608 | tf_op jit(solution)/shard_map/all_to_all | solution.py:713
  47.5 3.6 all-to-all-start.1
  51.6 17.5 %collective-permute-done.refs_2_ = bf16[8,64,1024]{2,1,0:T(8,128)(2,1)S(1)} collective-permute-done((bf16[8,64,1024]{2,1,0:T(8,128)(2,1)S(1)}, bf16[8,64,1024]{2,1,0:T(8,128)(2,1)S(1)}, u32[]{:S(2)}, u32[]{:S(2)}) %collective-permute-start) | collective-permute-done | bytes 1048608 | tf_op jit(solution)/shard_map/ppermute | solution.py:30
  71.5 1.9 slice.69
  74.9 18.7 %all-to-all-done.1.refs_0_ = bf16[8,64,768]{2,1,0:T(8,128)(2,1)S(1)} async-done(((bf16[8,64,768]{2,1,0:T(8,128)(2,1)}), bf16[8,64,768]{2,1,0:T(8,128)(2,1)S(1)}, u32[]{:S(2)}, u32[]{:S(2)}) %all-to-all-start.1) | async-done | bytes 786464 | tf_op jit(solution)/shard_map/all_to_all | solution.py:713
  98.0 4.2 %shard_map.253.up = bf16[2048,1024]{1,0:T(8,128)(2,1)S(1)} custom-call(s32[1]{0:T(128)} %bitcast.9.index_ref, bf16[8,64,1024]{2,1,0:T(8,128)(2,1)S(1)} %all-to-all-done.refs_0_, bf16[8,64,1024]{2,1,0:T(8,128)(2,1)} %collective-permute-done.2.refs_1_, bf16[8,64,1024]{2,1,0:T(8,128)(2,1)S(1)} %collective-permute-done.refs_2_, ...), custom_call_target="tpu_custom_call" | custom-call | flops 1 | bytes 1 | tf_op jit(solution)/shard_map/pallas_call | solution.py:365
  102.3 2.0 copy-done.2
  104.3 9.0 %collective-permute-done.4.refs_1_ = bf16[8,64,768]{2,1,0:T(8,128)(2,1)} collective-permute-done((bf16[8,64,768]{2,1,0:T(8,128)(2,1)S(1)}, bf16[8,64,768]{2,1,0:T(8,128)(2,1)}, u32[]{:S(2)}, u32[]{:S(2)}) %collective-permute-start.4) | collective-permute-done | bytes 786464 | tf_op jit(solution)/shard_map/ppermute | solution.py:30
  117.5 2.3 copy-done
  119.8 3.4 normalize.1
  123.7 2.0 fusion.11
  128.6 4.1 %shard_map.254.qkv = bf16[2048,768]{1,0:T(8,128)(2,1)S(1)} custom-call(s32[1]{0:T(128)} %bitcast.9.index_ref, bf16[8,64,768]{2,1,0:T(8,128)(2,1)S(1)} %copy-done.10, bf16[8,64,768]{2,1,0:T(8,128)(2,1)} %collective-permute-done.4.refs_1_, bf16[8,64,768]{2,1,0:T(8,128)(2,1)} %collective-permute-done.5.refs_2_, ...), custom_call_target="tpu_custom_call" | custom-call | flops 1 | bytes 1 | tf_op jit(solution)/shard_map/pallas_call | solution.py:365
  132.8 3.4 fusion.25.joined
  136.2 11.7 %attend.1 = (bf16[1024,256]{1,0:T(8,128)(2,1)}, bf16[1024,256]{1,0:T(8,128)(2,1)}, bf16[1024,256]{1,0:T(8,128)(2,1)}, f32[1024,256]{1,0:T(8,128)}, bf16[1024,256...) custom-call(f32[1024,768]{1,0:T(8,128)S(1)} %fusion.25.joined, f32[1,768]{1,0:T(1,128)S(1)} %bitcast.76, ...), custom_call_target="tpu_custom_call" | custom-call | flops 2147483648 | bytes 6815744 | tf_op jit(solution)/shard_map/attend/pallas_call | solution.py:560
  148.0 7.3 %multiply_convert_fusion = (bf16[1024,1024]{1,0:T(8,128)(2,1)}, f32[1024,1024]{1,0:T(8,128)}) fusion(f32[1024]{0:T(1024)S(1)} %copy-done.57, bf16[1024,2048]{1,0:T(8,128)(2,1)S(1)} %get-tuple-element.144, bf16[2048,1024]{1,0:T(8,128)(2,1)S(1)} %copy-done.3), kind=kOutput, calls=%fused_computation.10 | convolution fusion | flops 4305453056 | bytes 14684160 | tf_op jit(solution)/shard_map/dot_general | solution.py:24
  155.3 8.5 %convolution_convert_fusion = bf16[1280,2048]{1,0:T(8,128)(2,1)S(1)} fusion(bf16[1024,2048]{1,0:T(8,128)(2,1)} %bitcast.90, bf16[1024,1024]{1,0:T(8,128)(2,1)} %get-tuple-element.147.activated, bf16[1024,256]{1,0:T(8,128)(2,1)} %get-tuple-element.149.attended), kind=kOutput, calls=%fused_computation | convolution fusion | flops 5376573440 | bytes 12058624 | tf_op jit(solution)/shard_map/dot_general | solution.py:24
  168.8 7.1 %fusion.6.upward = bf16[1024,1024]{1,0:T(8,128)(2,1)S(1)} fusion(f32[1024,1024]{1,0:T(8,128)S(1)} %copy-done.66, f32[1024]{0:T(1024)S(1)} %copy-done.57, bf16[1024,2048]{1,0:T(8,128)(2,1)S(1)} %bitcast.91, bf16[1024,2048]{1,0:T(8,128)(2,1)S(1)} %copy-done.7), kind=kOutput, calls=%fused_computation.9 | convolution fusion | flops 4316987392 | bytes 14684160 | tf_op jit(solution)/shard_map/dot_general | solution.py:24
  175.9 4.9 %convolution_convert_fusion.1 = bf16[2048,1024]{1,0:T(8,128)(2,1)S(1)} fusion(bf16[1024,2048]{1,0:T(8,128)(2,1)S(1)} %copy-done.37, bf16[1024,1024]{1,0:T(8,128)(2,1)S(1)} %fusion.6.upward), kind=kOutput, calls=%fused_computation.11 | convolution fusion | flops 4297064448 | bytes 10485760 | tf_op jit(solution)/shard_map/dot_general | solution.py:24
  185.3 8.2 %output_part.1 = bf16[1024,2048]{1,0:T(8,128)(2,1)S(1)} custom-call(bf16[1024,256]{1,0:T(8,128)(2,1)S(1)} %copy-done.20, bf16[256,2048]{1,0:T(8,128)(2,1)S(1)} %copy-done.16, bf16[1024,1024]{1,0:T(8,128)(2,1)S(1)} %copy-done.15, bf16[1024,2048]{1,0:T(8,128)(2,1)S(1)} %copy-done.7), custom_call_target="tpu_custom_call" | custom-call | flops 1 | bytes 1 | tf_op jit(solution)/shard_map/output_part/pallas_call | solution.py:137
  193.6 2.0 copy-done.1
  195.6 1.9 collective-permute-done.8
  199.0 3.7 add_convert_fusion.1
  206.8 14.7 %attend_back.1 = (bf16[1024,768]{1,0:T(8,128)(2,1)S(1)}, f32[1,768]{1,0:T(1,128)S(1)}) custom-call(bf16[1024,256]{1,0:T(8,128)(2,1)S(1)} %copy-done.40, bf16[1024,256]{1,0:T(8,128)(2,1)S(1)} %copy-done.41, bf16[1024,256]{1,0:T(8,128)(2,1)S(1)} %copy-done.42, bf16[1024,256]{1,0:T(8,128)(2,1)S(1)} %copy-done.41, ...), custom_call_target="tpu_custom_call" | custom-call | flops 5368709120 | bytes 5242880 | tf_op jit(solution)/shard_map/attend_back/pallas_call | solution.py:671
  221.5 3.8 convolution_convert_fusion.2
  227.6 2.6 add_convert_fusion.4
  231.2 2.8 collective-permute-done.12
  236.8 12.0 %input_part.1 = (bf16[1024,2048]{1,0:T(8,128)(2,1)S(1)}, f32[2,2048]{1,0:T(2,128)S(1)}, f32[1,1024]{1,0:T(1,128)S(1)}) custom-call(bf16[1024,768]{1,0:T(8,128)(2,1)S(1)} %get-tuple-element.163.joined, bf16[2048,768]{1,0:T(8,128)(2,1)S(1)} %shard_map.254.qkv, bf16[1024,1024]{1,0:T(8,128)(2,1)S(1)} %copy-done.12, bf16[2048,1024]{1,0:T(8,128)(2,1)} %copy-done.2, ...), custom_call_target="tpu_custom_call" | custom-call | flops 1 | bytes 1 | tf_op jit(solution)/shard_map/input_part/pallas_call | solution.py:172
  251.0 10.3 %collective-permute-done.16 = bf16[8,32,1024]{2,1,0:T(8,128)(2,1)S(1)} collective-permute-done((bf16[8,32,1024]{2,1,0:T(8,128)(2,1)S(1)}, bf16[8,32,1024]{2,1,0:T(8,128)(2,1)S(1)}, u32[]{:S(2)}, u32[]{:S(2)}) %collective-permute-start.16) | collective-permute-done | bytes 524320 | tf_op jit(solution)/shard_map/ppermute | solution.py:30
  271.0 4.2 %all-to-all-start.2 = ((bf16[8,64,1024]{2,1,0:T(8,128)(2,1)}), bf16[8,64,1024]{2,1,0:T(8,128)(2,1)}, u32[]{:S(2)}, u32[]{:S(2)}) async-start(bf16[8,64,1024]{2,1,0:T(8,128)(2,1)} %add_convert_fusion.3), calls=%async_computation.3 | async-start | bytes 2097152 | tf_op jit(solution)/shard_map/all_to_all | solution.py:713
  275.4 4.0 collective-permute-done.18
  280.8 23.8 %collective-permute-done.20.refs_1_ = bf16[1280,512]{1,0:T(8,128)(2,1)S(1)} collective-permute-done((bf16[1280,512]{1,0:T(8,128)(2,1)}, bf16[1280,512]{1,0:T(8,128)(2,1)S(1)}, u32[]{:S(2)}, u32[]{:S(2)}) %collective-permute-start.20) | collective-permute-done | bytes 1310752 | tf_op jit(solution)/shard_map/ppermute | solution.py:30
  308.2 2.4 add_convert_fusion.6
  310.6 4.2 %all-to-all-start.3 = ((bf16[8,64,768]{2,1,0:T(8,128)(2,1)}), bf16[8,64,768]{2,1,0:T(8,128)(2,1)}, u32[]{:S(2)}, u32[]{:S(2)}) async-start(bf16[8,64,768]{2,1,0:T(8,128)(2,1)} %add_convert_fusion.6), calls=%async_computation.4 | async-start | bytes 1572864 | tf_op jit(solution)/shard_map/all_to_all | solution.py:713
  318.0 15.1 %collective-permute-done.27 = f32[1,8064]{1,0:T(1,128)S(1)} collective-permute-done((f32[1,8064]{1,0:T(1,128)S(1)}, f32[1,8064]{1,0:T(1,128)S(1)}, u32[]{:S(2)}, u32[]{:S(2)}) %collective-permute-start.27) | collective-permute-done | bytes 32288 | tf_op jit(solution)/shard_map/ppermute | solution.py:30
  333.1 8.3 %collective-permute-done.25.refs_3_ = bf16[1280,256]{1,0:T(8,128)(2,1)S(1)} collective-permute-done((bf16[1280,256]{1,0:T(8,128)(2,1)S(1)}, bf16[1280,256]{1,0:T(8,128)(2,1)S(1)}, u32[]{:S(2)}, u32[]{:S(2)}) %collective-permute-start.25) | collective-permute-done | bytes 655392 | tf_op jit(solution)/shard_map/ppermute | solution.py:30
  341.4 2.5 collective-permute-done.26.refs_4_
  345.7 1.9 slice.64
  347.6 1.9 collective-permute-start.30
  349.5 1.9 slice.65
  352.8 3.4 all-to-all-start.4
  356.3 5.9 %shard_map.255 = f32[1024,2048]{1,0:T(8,128)} custom-call(s32[1]{0:T(128)} %bitcast.9.index_ref, bf16[1280,512]{1,0:T(8,128)(2,1)} %add_convert_fusion.refs_0_, bf16[1280,512]{1,0:T(8,128)(2,1)} %copy-done.44, bf16[1280,512]{1,0:T(8,128)(2,1)} %copy-done.45, bf16[1280,256]{1,0:T(8,128)(2,1)} %copy-done.49, bf16[1280,256]{1,0:T(8,128)(2,1)} %collective-permute-done.26.refs_4_), custom_call_target="tpu_custom_call" | custom-call | flops 1 | bytes 1 | tf_op jit(solution)/shard_map/pallas_call | solution.py:365
  362.3 2.8 shard_map.256
  365.1 5.2 %all-to-all-done.4.tops.small = f32[8,1,8064]{2,1,0:T(1,128)S(1)} async-done(((f32[8,1,8064]{2,1,0:T(1,128)}), f32[8,1,8064]{2,1,0:T(1,128)S(1)}, u32[]{:S(2)}, u32[]{:S(2)}) %all-to-all-start.4) | async-done | bytes 258080 | tf_op jit(solution)/shard_map/all_to_all | solution.py:713
  370.3 2.9 clip_columns.1
  377.1 7.3 %shard_map.257 = f32[256,8192]{1,0:T(8,128)} custom-call(s32[1]{0:T(128)} %bitcast.9.index_ref, bf16[8,64,1024]{2,1,0:T(8,128)(2,1)} %all-to-all-done.2.refs_0_, bf16[8,64,1024]{2,1,0:T(8,128)(2,1)} %collective-permute-done.23.refs_1_, bf16[8,64,1024]{2,1,0:T(8,128)(2,1)} %collective-permute-done.24.refs_2_, ...), custom_call_target="tpu_custom_call" | custom-call | flops 1 | bytes 1 | tf_op jit(solution)/shard_map/pallas_call | solution.py:365
  387.0 6.0 %shard_map.258 = f32[256,6144]{1,0:T(8,128)} custom-call(s32[1]{0:T(128)} %bitcast.9.index_ref, bf16[8,64,768]{2,1,0:T(8,128)(2,1)} %all-to-all-done.3.refs_0_, bf16[8,64,768]{2,1,0:T(8,128)(2,1)} %collective-permute-done.28.refs_1_, bf16[8,64,768]{2,1,0:T(8,128)(2,1)} %collective-permute-done.29.refs_2_, bf16[8,32,768]{2,1,0:T(8,128)(2,1)} %copy-done.51, ...), custom_call_target="tpu_custom_call" | custom-call | flops 1 | bytes 1 | tf_op jit(solution)/shard_map/pallas_call | solution.py:365
  393.0 3.2 reduce-scatter.5.cloned.1.call-done
  (260 shorter events, 83.5 us)
Async XLA Ops:
  10.7 32.9 %all-to-all-start = ((bf16[8,64,1024]{2,1,0:T(8,128)(2,1)}), bf16[8,64,1024]{2,1,0:T(8,128)(2,1)S(1)}, u32[]{:S(2)}, u32[]{:S(2)}) async-start(bf16[8,64,1024]{2,1,0:T(8,128)(2,1)} %bitcast.60), calls=%async_computation | async-start | bytes 2097152 | tf_op jit(solution)/shard_map/all_to_all | solution.py:713
  17.0 100.4 %all-gather.5.cloned.1.call-start = ((), (), s32[]{:S(2)}) async-start(), calls=%async_computation.8 | async-start | bytes 5013504 | tf_op jit(solution)/shard_map/all_gather | solution.py:786
  20.8 73.0 %copy-start.31 = (f32[6144]{0:T(1024)S(1)}, f32[6144]{0:T(1024)}, u32[]{:S(2)}) copy-start(f32[6144]{0:T(1024)} %param.19) | copy-start | bytes 73732
  20.8 76.5 %copy-start.5 = (bf16[1,128,2048]{2,1,0:T(8,128)(2,1)S(1)}, bf16[1,128,2048]{2,1,0:T(8,128)(2,1)}, u32[]{:S(2)}) copy-start(bf16[1,128,2048]{2,1,0:T(8,128)(2,1)} %param.27) | copy-start | bytes 1572868
  43.7 111.6 %all-gather.3.cloned.1.call-start = ((), (), s32[]{:S(2)}) async-start(), calls=%async_computation.7 | async-start | bytes 4718592 | tf_op jit(solution)/shard_map/all_gather | solution.py:787
  44.4 24.8 %collective-permute-start = (bf16[8,64,1024]{2,1,0:T(8,128)(2,1)S(1)}, bf16[8,64,1024]{2,1,0:T(8,128)(2,1)S(1)}, u32[]{:S(2)}, u32[]{:S(2)}) collective-permute-start(bf16[8,64,1024]{2,1,0:T(8,128)(2,1)S(1)} %all-to-all-done.refs_0_), channel_id=1, source_target_pairs={{0,16},{8,24},{16,0},{24,8},{1,17},{9,25},{17,1},{25,9},{2,18},{10... | collective-permute-start | bytes 3145736 | tf_op jit(solution)/shard_map/ppermute | solution.py:30
  46.0 25.5 %collective-permute-start.2 = (bf16[8,64,1024]{2,1,0:T(8,128)(2,1)S(1)}, bf16[8,64,1024]{2,1,0:T(8,128)(2,1)}, u32[]{:S(2)}, u32[]{:S(2)}) collective-permute-start(bf16[8,64,1024]{2,1,0:T(8,128)(2,1)S(1)} %all-to-all-done.refs_0_), channel_id=1, source_target_pairs={{0,8},{8,0},{16,24},{24,16},{1,9},{9,1},{17,25},{25,17},{2,10},{10... | collective-permute-start | bytes 3145736 | tf_op jit(solution)/shard_map/ppermute | solution.py:30
  47.5 46.1 %all-to-all-start.1 = ((bf16[8,64,768]{2,1,0:T(8,128)(2,1)}), bf16[8,64,768]{2,1,0:T(8,128)(2,1)S(1)}, u32[]{:S(2)}, u32[]{:S(2)}) async-start(bf16[8,64,768]{2,1,0:T(8,128)(2,1)} %reshape.193), calls=%async_computation.1 | async-start | bytes 1572864 | tf_op jit(solution)/shard_map/all_to_all | solution.py:713
  51.1 342.0 %reduce-scatter.3.cloned.1.call-start = ((), (), s32[]{:S(2)}) async-start(), calls=%async_computation.9 | async-start | bytes 4718592 | tf_op jit(solution)/shard_map/reduce_scatter | solution.py:836
  70.0 23.6 %collective-permute-start.1 = (bf16[8,32,1024]{2,1,0:T(8,128)(2,1)}, bf16[8,32,1024]{2,1,0:T(8,128)(2,1)}, u32[]{:S(2)}, u32[]{:S(2)}) collective-permute-start(bf16[8,32,1024]{2,1,0:T(8,128)(2,1)} %slice.68), channel_id=1, source_target_pairs={{0,8},{8,0},{16,24},{24,16},{1,9},{9,1},{17,25},{25,17},{2,10},{10... | collective-permute-start | bytes 1572872 | tf_op jit(solution)/shard_map/ppermute | solution.py:30
  73.4 20.2 %collective-permute-start.3 = (bf16[8,32,1024]{2,1,0:T(8,128)(2,1)}, bf16[8,32,1024]{2,1,0:T(8,128)(2,1)}, u32[]{:S(2)}, u32[]{:S(2)}) collective-permute-start(bf16[8,32,1024]{2,1,0:T(8,128)(2,1)} %slice.69), channel_id=1, source_target_pairs={{0,16},{8,24},{16,0},{24,8},{1,17},{9,25},{17,1},{25,9},{2,18},{10... | collective-permute-start | bytes 1572872 | tf_op jit(solution)/shard_map/ppermute | solution.py:30
  93.6 19.7 %collective-permute-start.4 = (bf16[8,64,768]{2,1,0:T(8,128)(2,1)S(1)}, bf16[8,64,768]{2,1,0:T(8,128)(2,1)}, u32[]{:S(2)}, u32[]{:S(2)}) collective-permute-start(bf16[8,64,768]{2,1,0:T(8,128)(2,1)S(1)} %all-to-all-done.1.refs_0_), channel_id=1, source_target_pairs={{0,8},{8,0},{16,24},{24,16},{1,9},{9,1},{17,25},{25,17},{2,10},{10... | collective-permute-start | bytes 2359304 | tf_op jit(solution)/shard_map/ppermute | solution.py:30
  93.7 19.7 %collective-permute-start.5 = (bf16[8,64,768]{2,1,0:T(8,128)(2,1)S(1)}, bf16[8,64,768]{2,1,0:T(8,128)(2,1)}, u32[]{:S(2)}, u32[]{:S(2)}) collective-permute-start(bf16[8,64,768]{2,1,0:T(8,128)(2,1)S(1)} %all-to-all-done.1.refs_0_), channel_id=1, source_target_pairs={{0,16},{8,24},{16,0},{24,8},{1,17},{9,25},{17,1},{25,9},{2,18},{10... | collective-permute-start | bytes 2359304 | tf_op jit(solution)/shard_map/ppermute | solution.py:30
  98.0 19.5 %copy-start.33 = (f32[2048]{0:T(1024)S(1)}, f32[2048]{0:T(1024)}, u32[]{:S(2)}) copy-start(f32[2048]{0:T(1024)} %param.16) | copy-start | bytes 24580
  98.0 19.5 %copy-start.34 = (f32[2048]{0:T(1024)S(1)}, f32[2048]{0:T(1024)}, u32[]{:S(2)}) copy-start(f32[2048]{0:T(1024)} %param.17) | copy-start | bytes 24580
  115.5 10.3 %collective-permute-start.6 = (bf16[8,32,768]{2,1,0:T(8,128)(2,1)S(1)}, bf16[8,32,768]{2,1,0:T(8,128)(2,1)S(1)}, u32[]{:S(2)}, u32[]{:S(2)}) collective-permute-start(bf16[8,32,768]{2,1,0:T(8,128)(2,1)S(1)} %slice.53), channel_id=1, source_target_pairs={{0,8},{8,0},{16,24},{24,16},{1,9},{9,1},{17,25},{25,17},{2,10},{10... | collective-permute-start | bytes 1179656 | tf_op jit(solution)/shard_map/ppermute | solution.py:30
  117.2 9.6 %collective-permute-start.7 = (bf16[8,32,768]{2,1,0:T(8,128)(2,1)S(1)}, bf16[8,32,768]{2,1,0:T(8,128)(2,1)S(1)}, u32[]{:S(2)}, u32[]{:S(2)}) collective-permute-start(bf16[8,32,768]{2,1,0:T(8,128)(2,1)S(1)} %slice.54), channel_id=1, source_target_pairs={{0,16},{8,24},{16,0},{24,8},{1,17},{9,25},{17,1},{25,9},{2,18},{10... | collective-permute-start | bytes 1179656 | tf_op jit(solution)/shard_map/ppermute | solution.py:30
  123.2 24.8 %copy-start.36 = (bf16[1024,2048]{1,0:T(8,128)(2,1)}, bf16[1024,2048]{1,0:T(8,128)(2,1)S(1)}, u32[]{:S(2)}) copy-start(bf16[1024,2048]{1,0:T(8,128)(2,1)S(1)} %get-tuple-element.144) | copy-start | bytes 12582916
  165.6 31.9 %collective-permute-start.8 = (bf16[1280,512]{1,0:T(8,128)(2,1)}, bf16[1280,512]{1,0:T(8,128)(2,1)}, u32[]{:S(2)}, u32[]{:S(2)}) collective-permute-start(bf16[1280,512]{1,0:T(8,128)(2,1)} %get-tuple-element.248), channel_id=1, source_target_pairs={{0,8},{8,0},{16,24},{24,16},{1,9},{9,1},{17,25},{25,17},{2,10},{10... | collective-permute-start | bytes 3932168 | tf_op jit(solution)/shard_map/ppermute | solution.py:30
  167.0 32.0 %collective-permute-start.9 = (bf16[1280,512]{1,0:T(8,128)(2,1)}, bf16[1280,512]{1,0:T(8,128)(2,1)}, u32[]{:S(2)}, u32[]{:S(2)}) collective-permute-start(bf16[1280,512]{1,0:T(8,128)(2,1)} %get-tuple-element.247), channel_id=1, source_target_pairs={{0,16},{8,24},{16,0},{24,8},{1,17},{9,25},{17,1},{25,9},{2,18},{10... | collective-permute-start | bytes 3932168 | tf_op jit(solution)/shard_map/ppermute | solution.py:30
  182.3 43.1 %collective-permute-start.10 = (bf16[8,64,1024]{2,1,0:T(8,128)(2,1)}, bf16[8,64,1024]{2,1,0:T(8,128)(2,1)}, u32[]{:S(2)}, u32[]{:S(2)}) collective-permute-start(bf16[8,64,1024]{2,1,0:T(8,128)(2,1)} %get-tuple-element.252), channel_id=1, source_target_pairs={{0,8},{8,0},{16,24},{24,16},{1,9},{9,1},{17,25},{25,17},{2,10},{10... | collective-permute-start | bytes 3145736 | tf_op jit(solution)/shard_map/ppermute | solution.py:30
  183.9 41.6 %collective-permute-start.11 = (bf16[8,64,1024]{2,1,0:T(8,128)(2,1)}, bf16[8,64,1024]{2,1,0:T(8,128)(2,1)}, u32[]{:S(2)}, u32[]{:S(2)}) collective-permute-start(bf16[8,64,1024]{2,1,0:T(8,128)(2,1)} %get-tuple-element.251), channel_id=1, source_target_pairs={{0,16},{8,24},{16,0},{24,8},{1,17},{9,25},{17,1},{25,9},{2,18},{10... | collective-permute-start | bytes 3145736 | tf_op jit(solution)/shard_map/ppermute | solution.py:30
  202.8 31.2 %collective-permute-start.12 = (bf16[1280,256]{1,0:T(8,128)(2,1)S(1)}, bf16[1280,256]{1,0:T(8,128)(2,1)S(1)}, u32[]{:S(2)}, u32[]{:S(2)}) collective-permute-start(bf16[1280,256]{1,0:T(8,128)(2,1)S(1)} %get-tuple-element.264), channel_id=1, source_target_pairs={{0,8},{8,0},{16,24},{24,16},{1,9},{9,1},{17,25},{25,17},{2,10},{10... | collective-permute-start | bytes 1966088 | tf_op jit(solution)/shard_map/ppermute | solution.py:30
  203.5 31.9 %collective-permute-start.13 = (bf16[1280,256]{1,0:T(8,128)(2,1)S(1)}, bf16[1280,256]{1,0:T(8,128)(2,1)S(1)}, u32[]{:S(2)}, u32[]{:S(2)}) collective-permute-start(bf16[1280,256]{1,0:T(8,128)(2,1)S(1)} %get-tuple-element.262), channel_id=1, source_target_pairs={{0,16},{8,24},{16,0},{24,8},{1,17},{9,25},{17,1},{25,9},{2,18},{10... | collective-permute-start | bytes 1966088 | tf_op jit(solution)/shard_map/ppermute | solution.py:30
  225.4 38.5 %collective-permute-start.14 = (bf16[8,64,768]{2,1,0:T(8,128)(2,1)S(1)}, bf16[8,64,768]{2,1,0:T(8,128)(2,1)S(1)}, u32[]{:S(2)}, u32[]{:S(2)}) collective-permute-start(bf16[8,64,768]{2,1,0:T(8,128)(2,1)S(1)} %get-tuple-element.166), channel_id=1, source_target_pairs={{0,8},{8,0},{16,24},{24,16},{1,9},{9,1},{17,25},{25,17},{2,10},{10... | collective-permute-start | bytes 2359304 | tf_op jit(solution)/shard_map/ppermute | solution.py:30
  226.7 37.2 %collective-permute-start.15 = (bf16[8,64,768]{2,1,0:T(8,128)(2,1)S(1)}, bf16[8,64,768]{2,1,0:T(8,128)(2,1)S(1)}, u32[]{:S(2)}, u32[]{:S(2)}) collective-permute-start(bf16[8,64,768]{2,1,0:T(8,128)(2,1)S(1)} %get-tuple-element.167), channel_id=1, source_target_pairs={{0,16},{8,24},{16,0},{24,8},{1,17},{9,25},{17,1},{25,9},{2,18},{10... | collective-permute-start | bytes 2359304 | tf_op jit(solution)/shard_map/ppermute | solution.py:30
  248.8 12.5 %collective-permute-start.16 = (bf16[8,32,1024]{2,1,0:T(8,128)(2,1)S(1)}, bf16[8,32,1024]{2,1,0:T(8,128)(2,1)S(1)}, u32[]{:S(2)}, u32[]{:S(2)}) collective-permute-start(bf16[8,32,1024]{2,1,0:T(8,128)(2,1)S(1)} %get-tuple-element.172), channel_id=1, source_target_pairs={{0,8},{8,0},{16,24},{24,16},{1,9},{9,1},{17,25},{25,17},{2,10},{10... | collective-permute-start | bytes 1572872 | tf_op jit(solution)/shard_map/ppermute | solution.py:30
  249.5 13.0 %collective-permute-start.17 = (bf16[8,32,1024]{2,1,0:T(8,128)(2,1)S(1)}, bf16[8,32,1024]{2,1,0:T(8,128)(2,1)S(1)}, u32[]{:S(2)}, u32[]{:S(2)}) collective-permute-start(bf16[8,32,1024]{2,1,0:T(8,128)(2,1)S(1)} %copy-done.50), channel_id=1, source_target_pairs={{0,16},{8,24},{16,0},{24,8},{1,17},{9,25},{17,1},{25,9},{2,18},{10... | collective-permute-start | bytes 1572872 | tf_op jit(solution)/shard_map/ppermute | solution.py:30
  266.3 9.0 %collective-permute-start.22 = (f32[1,8064]{1,0:T(1,128)S(1)}, f32[1,8064]{1,0:T(1,128)S(1)}, u32[]{:S(2)}, u32[]{:S(2)}) collective-permute-start(f32[1,8064]{1,0:T(1,128)S(1)} %pad_maximum_fusion.2), channel_id=1, source_target_pairs={{0,8},{8,0},{16,24},{24,16},{1,9},{9,1},{17,25},{25,17},{2,10},{10... | collective-permute-start | bytes 96776 | tf_op jit(solution)/shard_map/ppermute | solution.py:30
  267.0 12.4 %collective-permute-start.18 = (bf16[8,32,768]{2,1,0:T(8,128)(2,1)}, bf16[8,32,768]{2,1,0:T(8,128)(2,1)}, u32[]{:S(2)}, u32[]{:S(2)}) collective-permute-start(bf16[8,32,768]{2,1,0:T(8,128)(2,1)} %get-tuple-element.272), channel_id=1, source_target_pairs={{0,8},{8,0},{16,24},{24,16},{1,9},{9,1},{17,25},{25,17},{2,10},{10... | collective-permute-start | bytes 1179656 | tf_op jit(solution)/shard_map/ppermute | solution.py:30
  268.4 12.4 %collective-permute-start.19 = (bf16[8,32,768]{2,1,0:T(8,128)(2,1)}, bf16[8,32,768]{2,1,0:T(8,128)(2,1)}, u32[]{:S(2)}, u32[]{:S(2)}) collective-permute-start(bf16[8,32,768]{2,1,0:T(8,128)(2,1)} %get-tuple-element.270), channel_id=1, source_target_pairs={{0,16},{8,24},{16,0},{24,8},{1,17},{9,25},{17,1},{25,9},{2,18},{10... | collective-permute-start | bytes 1179656 | tf_op jit(solution)/shard_map/ppermute | solution.py:30
  269.9 34.6 %collective-permute-start.20 = (bf16[1280,512]{1,0:T(8,128)(2,1)}, bf16[1280,512]{1,0:T(8,128)(2,1)S(1)}, u32[]{:S(2)}, u32[]{:S(2)}) collective-permute-start(bf16[1280,512]{1,0:T(8,128)(2,1)} %add_convert_fusion.refs_0_), channel_id=1, source_target_pairs={{0,8},{8,0},{16,24},{24,16},{1,9},{9,1},{17,25},{25,17},{2,10},{10... | collective-permute-start | bytes 3932168 | tf_op jit(solution)/shard_map/ppermute | solution.py:30
  270.5 34.9 %collective-permute-start.21 = (bf16[1280,512]{1,0:T(8,128)(2,1)}, bf16[1280,512]{1,0:T(8,128)(2,1)S(1)}, u32[]{:S(2)}, u32[]{:S(2)}) collective-permute-start(bf16[1280,512]{1,0:T(8,128)(2,1)} %add_convert_fusion.refs_0_), channel_id=1, source_target_pairs={{0,16},{8,24},{16,0},{24,8},{1,17},{9,25},{17,1},{25,9},{2,18},{10... | collective-permute-start | bytes 3932168 | tf_op jit(solution)/shard_map/ppermute | solution.py:30
  271.0 34.3 %all-to-all-start.2 = ((bf16[8,64,1024]{2,1,0:T(8,128)(2,1)}), bf16[8,64,1024]{2,1,0:T(8,128)(2,1)}, u32[]{:S(2)}, u32[]{:S(2)}) async-start(bf16[8,64,1024]{2,1,0:T(8,128)(2,1)} %add_convert_fusion.3), calls=%async_computation.3 | async-start | bytes 2097152 | tf_op jit(solution)/shard_map/all_to_all | solution.py:713
  305.4 38.6 %collective-permute-start.23 = (bf16[8,64,1024]{2,1,0:T(8,128)(2,1)}, bf16[8,64,1024]{2,1,0:T(8,128)(2,1)}, u32[]{:S(2)}, u32[]{:S(2)}) collective-permute-start(bf16[8,64,1024]{2,1,0:T(8,128)(2,1)} %all-to-all-done.2.refs_0_), channel_id=1, source_target_pairs={{0,8},{8,0},{16,24},{24,16},{1,9},{9,1},{17,25},{25,17},{2,10},{10... | collective-permute-start | bytes 3145736 | tf_op jit(solution)/shard_map/ppermute | solution.py:30
  306.1 37.9 %collective-permute-start.24 = (bf16[8,64,1024]{2,1,0:T(8,128)(2,1)}, bf16[8,64,1024]{2,1,0:T(8,128)(2,1)}, u32[]{:S(2)}, u32[]{:S(2)}) collective-permute-start(bf16[8,64,1024]{2,1,0:T(8,128)(2,1)} %all-to-all-done.2.refs_0_), channel_id=1, source_target_pairs={{0,16},{8,24},{16,0},{24,8},{1,17},{9,25},{17,1},{25,9},{2,18},{10... | collective-permute-start | bytes 3145736 | tf_op jit(solution)/shard_map/ppermute | solution.py:30
  307.7 25.4 %collective-permute-start.27 = (f32[1,8064]{1,0:T(1,128)S(1)}, f32[1,8064]{1,0:T(1,128)S(1)}, u32[]{:S(2)}, u32[]{:S(2)}) collective-permute-start(f32[1,8064]{1,0:T(1,128)S(1)} %pad_maximum_fusion.3), channel_id=1, source_target_pairs={{0,16},{8,24},{16,0},{24,8},{1,17},{9,25},{17,1},{25,9},{2,18},{10... | collective-permute-start | bytes 96776 | tf_op jit(solution)/shard_map/ppermute | solution.py:30
  310.6 33.3 %all-to-all-start.3 = ((bf16[8,64,768]{2,1,0:T(8,128)(2,1)}), bf16[8,64,768]{2,1,0:T(8,128)(2,1)}, u32[]{:S(2)}, u32[]{:S(2)}) async-start(bf16[8,64,768]{2,1,0:T(8,128)(2,1)} %add_convert_fusion.6), calls=%async_computation.4 | async-start | bytes 1572864 | tf_op jit(solution)/shard_map/all_to_all | solution.py:713
  314.8 81.4 %reduce-scatter.5.cloned.1.call-start = ((), (), s32[]{:S(2)}) async-start(), calls=%async_computation.10 | async-start | bytes 4718592 | tf_op jit(solution)/shard_map/reduce_scatter | solution.py:836
  314.9 26.5 %collective-permute-start.25 = (bf16[1280,256]{1,0:T(8,128)(2,1)S(1)}, bf16[1280,256]{1,0:T(8,128)(2,1)S(1)}, u32[]{:S(2)}, u32[]{:S(2)}) collective-permute-start(bf16[1280,256]{1,0:T(8,128)(2,1)S(1)} %slice.60), channel_id=1, source_target_pairs={{0,8},{8,0},{16,24},{24,16},{1,9},{9,1},{17,25},{25,17},{2,10},{10... | collective-permute-start | bytes 1966088 | tf_op jit(solution)/shard_map/ppermute | solution.py:30
  316.4 27.6 %collective-permute-start.26 = (bf16[1280,256]{1,0:T(8,128)(2,1)S(1)}, bf16[1280,256]{1,0:T(8,128)(2,1)}, u32[]{:S(2)}, u32[]{:S(2)}) collective-permute-start(bf16[1280,256]{1,0:T(8,128)(2,1)S(1)} %slice.61), channel_id=1, source_target_pairs={{0,16},{8,24},{16,0},{24,8},{1,17},{9,25},{17,1},{25,9},{2,18},{10... | collective-permute-start | bytes 1966088 | tf_op jit(solution)/shard_map/ppermute | solution.py:30
  344.0 29.2 %collective-permute-start.28 = (bf16[8,64,768]{2,1,0:T(8,128)(2,1)}, bf16[8,64,768]{2,1,0:T(8,128)(2,1)}, u32[]{:S(2)}, u32[]{:S(2)}) collective-permute-start(bf16[8,64,768]{2,1,0:T(8,128)(2,1)} %all-to-all-done.3.refs_0_), channel_id=1, source_target_pairs={{0,8},{8,0},{16,24},{24,16},{1,9},{9,1},{17,25},{25,17},{2,10},{10... | collective-permute-start | bytes 2359304 | tf_op jit(solution)/shard_map/ppermute | solution.py:30
  344.1 29.1 %collective-permute-start.29 = (bf16[8,64,768]{2,1,0:T(8,128)(2,1)}, bf16[8,64,768]{2,1,0:T(8,128)(2,1)}, u32[]{:S(2)}, u32[]{:S(2)}) collective-permute-start(bf16[8,64,768]{2,1,0:T(8,128)(2,1)} %all-to-all-done.3.refs_0_), channel_id=1, source_target_pairs={{0,16},{8,24},{16,0},{24,8},{1,17},{9,25},{17,1},{25,9},{2,18},{10... | collective-permute-start | bytes 2359304 | tf_op jit(solution)/shard_map/ppermute | solution.py:30
  347.6 25.6 %collective-permute-start.30 = (bf16[8,32,1024]{2,1,0:T(8,128)(2,1)}, bf16[8,32,1024]{2,1,0:T(8,128)(2,1)}, u32[]{:S(2)}, u32[]{:S(2)}) collective-permute-start(bf16[8,32,1024]{2,1,0:T(8,128)(2,1)} %slice.64), channel_id=1, source_target_pairs={{0,8},{8,0},{16,24},{24,16},{1,9},{9,1},{17,25},{25,17},{2,10},{10... | collective-permute-start | bytes 1572872 | tf_op jit(solution)/shard_map/ppermute | solution.py:30
  351.4 21.8 %collective-permute-start.31 = (bf16[8,32,1024]{2,1,0:T(8,128)(2,1)}, bf16[8,32,1024]{2,1,0:T(8,128)(2,1)}, u32[]{:S(2)}, u32[]{:S(2)}) collective-permute-start(bf16[8,32,1024]{2,1,0:T(8,128)(2,1)} %slice.65), channel_id=1, source_target_pairs={{0,16},{8,24},{16,0},{24,8},{1,17},{9,25},{17,1},{25,9},{2,18},{10... | collective-permute-start | bytes 1572872 | tf_op jit(solution)/shard_map/ppermute | solution.py:30
  352.8 17.5 %all-to-all-start.4 = ((f32[8,1,8064]{2,1,0:T(1,128)}), f32[8,1,8064]{2,1,0:T(1,128)S(1)}, u32[]{:S(2)}, u32[]{:S(2)}) async-start(f32[8,1,8064]{2,1,0:T(1,128)} %broadcast_in_dim.53), calls=%async_computation.6 | async-start | bytes 516096 | tf_op jit(solution)/shard_map/all_to_all | solution.py:713
  374.3 10.9 %collective-permute-start.32 = (bf16[8,32,768]{2,1,0:T(8,128)(2,1)S(1)}, bf16[8,32,768]{2,1,0:T(8,128)(2,1)S(1)}, u32[]{:S(2)}, u32[]{:S(2)}) collective-permute-start(bf16[8,32,768]{2,1,0:T(8,128)(2,1)S(1)} %slice.66), channel_id=1, source_target_pairs={{0,8},{8,0},{16,24},{24,16},{1,9},{9,1},{17,25},{25,17},{2,10},{10... | collective-permute-start | bytes 1179656 | tf_op jit(solution)/shard_map/ppermute | solution.py:30
  375.4 10.9 %collective-permute-start.33 = (bf16[8,32,768]{2,1,0:T(8,128)(2,1)S(1)}, bf16[8,32,768]{2,1,0:T(8,128)(2,1)S(1)}, u32[]{:S(2)}, u32[]{:S(2)}) collective-permute-start(bf16[8,32,768]{2,1,0:T(8,128)(2,1)S(1)} %slice.67), channel_id=1, source_target_pairs={{0,16},{8,24},{16,0},{24,8},{1,17},{9,25},{17,1},{25,9},{2,18},{10... | collective-permute-start | bytes 1179656 | tf_op jit(solution)/shard_map/ppermute | solution.py:30
  (62 other events, 410.5 us)
Sparse Core Ops, SparseCore 0:
  43.8 64.9 all-gather.4
  110.4 44.7 all-gather.2
  195.7 48.2 reduce-scatter.2
  344.1 52.0 reduce-scatter.4
